TPU v7x, 32 devices: a whole 2x2x4 slice. The times are simulated.
32 devices in a mesh: shard: 4 (over y, x), ctx: 2 (over core), tp: 4 (over z).
Axes of the slice: x: 2, y: 2, z: 4, core: 2. Of those that a mesh axis runs over, the one named last changes fastest.
Arguments:
- hidden_in: bfloat16 [4, 2048, 2048], P('shard', 'ctx'), may hold values from -6 to 6
- doc_span: int32 [2, 4, 2048], P(None, 'shard', 'ctx'), may hold values from 0 to 2047, as said below
- cotangent: bfloat16 [4, 2048, 2048], P('shard', 'ctx'), may hold values from -6 to 6
- w_query: float32 [2048, 2048], P(('shard', 'ctx'), 'tp'), may hold values from -0.1875 to 0.1875
- w_key: float32 [2048, 2048], P(('shard', 'ctx'), 'tp'), may hold values from -0.1875 to 0.1875
- w_value: float32 [2048, 2048], P(('shard', 'ctx'), 'tp'), may hold values from -0.125 to 0.125
- w_out: float32 [2048, 2048], P('tp', ('shard', 'ctx')), may hold values from -0.75 to 0.75
- w_inner: float32 [2048, 8192], P(('shard', 'ctx'), 'tp'), may hold values from -0.125 to 0.125
- w_outer: float32 [8192, 2048], P('tp', ('shard', 'ctx')), may hold values from -0.0625 to 0.0625
- norm_gains: float32 [2, 2048], replicated, may hold values from 0.5 to 1.5
- norm_biases: float32 [2, 2048], replicated, may hold values from -1.25 to 1.25
- mom_query: float32 [2048, 2048], P(('shard', 'ctx'), 'tp'), may hold values from -112 to 112
- mom_key: float32 [2048, 2048], P(('shard', 'ctx'), 'tp'), may hold values from -112 to 112
- mom_value: float32 [2048, 2048], P(('shard', 'ctx'), 'tp'), may hold values from -112 to 112
- mom_out: float32 [2048, 2048], P('tp', ('shard', 'ctx')), may hold values from -112 to 112
- mom_inner: float32 [2048, 8192], P(('shard', 'ctx'), 'tp'), may hold values from -112 to 112
- mom_outer: float32 [8192, 2048], P('tp', ('shard', 'ctx')), may hold values from -112 to 112
- gain_moment: float32 [2, 2048], replicated, may hold values from -512 to 512
- bias_moment: float32 [2, 2048], replicated, may hold values from -512 to 512
Outputs:
- layer_out: bfloat16 [4, 2048, 2048], P('shard', 'ctx')
- input_grad: float32 [4, 2048, 2048], P('shard', 'ctx')
- grad_query: float32 [2048, 2048], P(('shard', 'ctx'), 'tp')
- grad_key: float32 [2048, 2048], P(('shard', 'ctx'), 'tp')
- grad_value: float32 [2048, 2048], P(('shard', 'ctx'), 'tp')
- grad_out: float32 [2048, 2048], P('tp', ('shard', 'ctx'))
- grad_inner: float32 [2048, 8192], P(('shard', 'ctx'), 'tp')
- grad_outer: float32 [8192, 2048], P('tp', ('shard', 'ctx'))
- gain_grad: float32 [2, 2048], replicated
- bias_grad: float32 [2, 2048], replicated
- moment_query: float32 [2048, 2048], P(('shard', 'ctx'), 'tp')
- moment_key: float32 [2048, 2048], P(('shard', 'ctx'), 'tp')
- moment_value: float32 [2048, 2048], P(('shard', 'ctx'), 'tp')
- moment_out: float32 [2048, 2048], P('tp', ('shard', 'ctx'))
- moment_inner: float32 [2048, 8192], P(('shard', 'ctx'), 'tp')
- moment_outer: float32 [8192, 2048], P('tp', ('shard', 'ctx'))
- gain_moment_new: float32 [2, 2048], replicated
- bias_moment_new: float32 [2, 2048], replicated
- new_query: float32 [2048, 2048], P(('shard', 'ctx'), 'tp')
- new_key: float32 [2048, 2048], P(('shard', 'ctx'), 'tp')
- new_value: float32 [2048, 2048], P(('shard', 'ctx'), 'tp')
- new_out: float32 [2048, 2048], P('tp', ('shard', 'ctx'))
- new_inner: float32 [2048, 8192], P(('shard', 'ctx'), 'tp')
- new_outer: float32 [8192, 2048], P('tp', ('shard', 'ctx'))
- new_gains: float32 [2, 2048], replicated
- new_biases: float32 [2, 2048], replicated
Inputs may be any that keep to these rules, and one draw needn't show every extreme that they name: doc_span[0, r, i] <= i <= doc_span[1, r, i]; the positions of a packed row that share one pair form a run of consecutive positions (a document), and the documents of a row follow one another without gaps.
All inputs are finite; a program needn't handle non-finite values.
Results may differ from a plain program's by a relative error of at most 0.014.
The roundings to bfloat16 on the way count: a program that leaves them out, or rounds other values in their place, can miss the bound.
Values may be sent and summed in bfloat16 or wider, within the bound.
No kernel may reach another device: no remote copies, remote signals or barrier semaphores. Data moves between devices by JAX's collectives and lax.ppermute only.
A program may use at most 256 MiB of HBM per device.

v0:
```python
import math

import jax
import jax.numpy as jnp
from jax import lax
from jax.sharding import PartitionSpec as P

HEAD_DIM = 128
REACH = 512
BW = 512
NS_STEPS = 5


NS_COEFFS = (3.4445, -4.775, 2.0315)
LN_EPSILON = 1e-12
BETA = 0.5
MATRIX_RATE = 0.5
VECTOR_RATE = 0.3
MASKED = -1e30


def for_sending(value):

    def short(part):
        return part.astype(jnp.bfloat16) if part.dtype == jnp.float32 else part

    return jax.tree.map(short, value)


def padded_2(block, sides, width):
    for axis, dim in sides:
        count = lax.axis_size(axis)
        forward = [(i, i + 1) for i in range(count - 1)]
        backward = [(target, source) for source, target in forward]
        low = lax.ppermute(
            lax.slice_in_dim(block, block.shape[dim] - width, None, axis=dim), axis, forward
        )
        high = lax.ppermute(lax.slice_in_dim(block, 0, width, axis=dim), axis, backward)
        block = jnp.concatenate([low, block, high], axis=dim)
    return block


def from_behind(value, axis, by):
    length = lax.axis_size(axis)
    pairs = [(i, i + by) for i in range(length) if 0 <= i + by < length]
    return lax.ppermute(value, axis, pairs)


def layer_norm(hidden, gain, shift):
    centred = hidden - jnp.mean(hidden, axis=-1, keepdims=True)
    variance = jnp.mean(centred * centred, axis=-1, keepdims=True)
    return centred * lax.rsqrt(variance + LN_EPSILON) * gain + shift


def gelu_tanh(values):
    return jax.nn.gelu(values, approximate=True)


def newton_schulz(owned):
    stack_blocks = owned[:, 0]
    norms = jnp.sqrt(jnp.sum(stack_blocks * stack_blocks, axis=(1, 2), keepdims=True))
    iterate = stack_blocks / (norms + 1e-07)
    for step_index in range(NS_STEPS):
        gram = jnp.einsum("kdi,kdj->kij", iterate, iterate, precision=lax.Precision.HIGHEST)
        polynomial = NS_COEFFS[1] * gram + NS_COEFFS[2] * jnp.einsum(
            "kij,kjl->kil", gram, gram, precision=lax.Precision.HIGHEST
        )
        iterate = NS_COEFFS[0] * iterate + jnp.einsum(
            "kdi,kij->kdj", iterate, polynomial, precision=lax.Precision.HIGHEST
        )
    return iterate[:, None]


def owner_work(owned):
    return lax.all_to_all(
        for_sending(newton_schulz(owned)), ("shard", "ctx"), split_axis=2, concat_axis=1, tiled=True
    )


def body(
    hidden_in,
    doc_span,
    cotangent,
    w_query,
    w_key,
    w_value,
    w_out,
    w_inner,
    w_outer,
    norm_gains,
    norm_biases,
    mom_query,
    mom_key,
    mom_value,
    mom_out,
    mom_inner,
    mom_outer,
    gain_moment,
    bias_moment,
):
    low_query = w_query.astype(jnp.bfloat16)
    low_key = w_key.astype(jnp.bfloat16)
    low_value = w_value.astype(jnp.bfloat16)
    low_out = w_out.astype(jnp.bfloat16)
    low_inner = w_inner.astype(jnp.bfloat16)
    low_outer = w_outer.astype(jnp.bfloat16)
    full_query, full_key, full_value, full_out, full_inner, full_outer = (
        lax.all_gather(low_query, ("shard", "ctx"), axis=0, tiled=True),
        lax.all_gather(low_key, ("shard", "ctx"), axis=0, tiled=True),
        lax.all_gather(low_value, ("shard", "ctx"), axis=0, tiled=True),
        lax.all_gather(low_out, ("shard", "ctx"), axis=1, tiled=True),
        lax.all_gather(low_inner, ("shard", "ctx"), axis=0, tiled=True),
        lax.all_gather(low_outer, ("shard", "ctx"), axis=1, tiled=True),
    )
    hidden = hidden_in[0]
    length = hidden.shape[0]
    local_width = full_query.shape[1]
    head_count = local_width // HEAD_DIM
    queries = jnp.dot(hidden, full_query, preferred_element_type=jnp.float32).astype(jnp.bfloat16)
    keys_low = jnp.dot(hidden, full_key, preferred_element_type=jnp.float32).astype(jnp.bfloat16)
    values_low = jnp.dot(hidden, full_value, preferred_element_type=jnp.float32).astype(
        jnp.bfloat16
    )
    padded = padded_2(jnp.stack([keys_low, values_low]), (("ctx", 1),), REACH)
    padded_shape = (length + 2 * REACH, head_count, HEAD_DIM)
    padded_keys = padded[0].reshape(padded_shape)
    padded_values = padded[1].reshape(padded_shape)
    query_heads = queries.reshape(length, head_count, HEAD_DIM)
    block_rows = min(512, length)
    block_count = length // block_rows
    key_span = block_rows + 2 * REACH
    score_scale = HEAD_DIM ** (-0.5)
    anchor = lax.axis_index("ctx") * length
    lower_all = doc_span[0, 0]
    upper_all = doc_span[1, 0]

    def block_scores(offset):
        query_rows = lax.dynamic_slice_in_dim(query_heads, offset, block_rows, 0)
        key_rows = lax.dynamic_slice_in_dim(padded_keys, offset, key_span, 0)
        value_rows = lax.dynamic_slice_in_dim(padded_values, offset, key_span, 0)
        raw = jnp.einsum("ihd,jhd->hij", query_rows, key_rows, preferred_element_type=jnp.float32)
        query_pos = anchor + offset + jnp.arange(block_rows, dtype=jnp.int32)
        key_pos = anchor + offset - REACH + jnp.arange(key_span, dtype=jnp.int32)
        lower = lax.dynamic_slice_in_dim(lower_all, offset, block_rows, 0)
        upper = lax.dynamic_slice_in_dim(upper_all, offset, block_rows, 0)
        visible = (key_pos[None, :] >= lower[:, None]) & (key_pos[None, :] <= upper[:, None])
        visible = visible & (jnp.abs(key_pos[None, :] - query_pos[:, None]) <= REACH)
        return (
            jnp.where(visible[None], raw * score_scale, MASKED),
            query_rows,
            key_rows,
            value_rows,
        )

    def forward_block(block_index):
        scores, query_rows, key_rows, value_rows = block_scores(block_index * block_rows)
        row_max = jnp.max(scores, axis=-1, keepdims=True)
        expo = jnp.exp(scores - row_max)
        denominator = jnp.sum(expo, axis=-1, keepdims=True)
        weights_low = (expo / denominator).astype(jnp.bfloat16)
        mixed = jnp.einsum(
            "hij,jhd->ihd", weights_low, value_rows, preferred_element_type=jnp.float32
        )
        return (
            mixed.reshape(block_rows, local_width),
            row_max[..., 0] + jnp.log(denominator[..., 0]),
        )

    mixed_blocks, log_totals = lax.map(forward_block, jnp.arange(block_count, dtype=jnp.int32))
    attended = mixed_blocks.reshape(length, local_width).astype(jnp.bfloat16)
    branch = lax.psum(jnp.dot(attended, full_out, preferred_element_type=jnp.float32), "tp")
    normed, norm_pull_one = jax.vjp(
        layer_norm, hidden.astype(jnp.float32) + branch, norm_gains[0], norm_biases[0]
    )
    normed_low = normed.astype(jnp.bfloat16)
    pre_act = jnp.dot(normed_low, full_inner, preferred_element_type=jnp.float32)
    activated, gelu_pull = jax.vjp(gelu_tanh, pre_act)
    act_low = activated.astype(jnp.bfloat16)
    ffn_branch = lax.psum(jnp.dot(act_low, full_outer, preferred_element_type=jnp.float32), "tp")
    layer_f32, norm_pull_two = jax.vjp(
        layer_norm, normed + ffn_branch, norm_gains[1], norm_biases[1]
    )
    layer_out = layer_f32.astype(jnp.bfloat16)[None]
    grad_two, gain_two, shift_two = norm_pull_two(cotangent[0].astype(jnp.float32))
    dffn_low = grad_two.astype(jnp.bfloat16)
    grad_outer_local = jnp.dot(act_low.T, dffn_low, preferred_element_type=jnp.float32)
    dact = jnp.dot(dffn_low, full_outer.T, preferred_element_type=jnp.float32)
    dpre_low = gelu_pull(dact)[0].astype(jnp.bfloat16)
    grad_inner_local = jnp.dot(normed_low.T, dpre_low, preferred_element_type=jnp.float32)
    dnormed = grad_two + lax.psum(
        jnp.dot(dpre_low, full_inner.T, preferred_element_type=jnp.float32), "tp"
    )
    grad_one, gain_one, shift_one = norm_pull_one(dnormed)
    dbranch_low = grad_one.astype(jnp.bfloat16)
    grad_out_local = jnp.dot(attended.T, dbranch_low, preferred_element_type=jnp.float32)
    dattended = (
        jnp.dot(dbranch_low, full_out.T, preferred_element_type=jnp.float32)
        .astype(jnp.bfloat16)
        .reshape(length, head_count, HEAD_DIM)
    )

    def backward_block(carry, inputs):
        key_grad, value_grad = carry
        block_index, log_total = inputs
        offset = block_index * block_rows
        scores, query_rows, key_rows, value_rows = block_scores(offset)
        probabilities = jnp.exp(scores - log_total[..., None])
        dout_rows = lax.dynamic_slice_in_dim(dattended, offset, block_rows, 0)
        dprobs = jnp.einsum(
            "ihd,jhd->hij", dout_rows, value_rows, preferred_element_type=jnp.float32
        )
        dscores = probabilities * (dprobs - jnp.sum(dprobs * probabilities, axis=-1, keepdims=True))
        dscore_low = (dscores * score_scale).astype(jnp.bfloat16)
        query_part = jnp.einsum(
            "hij,jhd->ihd", dscore_low, key_rows, preferred_element_type=jnp.float32
        )
        key_part = jnp.einsum(
            "hij,ihd->jhd", dscore_low, query_rows, preferred_element_type=jnp.float32
        )
        value_part = jnp.einsum(
            "hij,ihd->jhd",
            probabilities.astype(jnp.bfloat16),
            dout_rows,
            preferred_element_type=jnp.float32,
        )
        key_grad = lax.dynamic_update_slice_in_dim(
            key_grad, lax.dynamic_slice_in_dim(key_grad, offset, key_span, 0) + key_part, offset, 0
        )
        value_grad = lax.dynamic_update_slice_in_dim(
            value_grad,
            lax.dynamic_slice_in_dim(value_grad, offset, key_span, 0) + value_part,
            offset,
            0,
        )
        return ((key_grad, value_grad), query_part.reshape(block_rows, local_width))

    empty_grad = jnp.zeros(padded_shape, jnp.float32)
    (key_grad, value_grad), query_blocks = lax.scan(
        backward_block,
        (empty_grad, empty_grad),
        (jnp.arange(block_count, dtype=jnp.int32), log_totals),
    )
    stacked_grad = jnp.stack([key_grad, value_grad]).reshape(2, length + 2 * REACH, local_width)
    from_above = from_behind(stacked_grad[:, :REACH].astype(jnp.bfloat16), "ctx", -1).astype(
        jnp.float32
    )
    from_below = from_behind(
        stacked_grad[:, length + REACH :].astype(jnp.bfloat16), "ctx", 1
    ).astype(jnp.float32)
    centre = stacked_grad[:, REACH : length + REACH]
    centre = centre.at[:, length - REACH :].add(from_above)
    centre = centre.at[:, :REACH].add(from_below)
    kv_low = centre.astype(jnp.bfloat16)
    query_low_grad = query_blocks.reshape(length, local_width).astype(jnp.bfloat16)
    grad_query_local = jnp.dot(hidden.T, query_low_grad, preferred_element_type=jnp.float32)
    grad_key_local = jnp.dot(hidden.T, kv_low[0], preferred_element_type=jnp.float32)
    grad_value_local = jnp.dot(hidden.T, kv_low[1], preferred_element_type=jnp.float32)
    input_terms = jnp.dot(query_low_grad, full_query.T, preferred_element_type=jnp.float32)
    input_terms = input_terms + jnp.dot(kv_low[0], full_key.T, preferred_element_type=jnp.float32)
    input_terms = input_terms + jnp.dot(kv_low[1], full_value.T, preferred_element_type=jnp.float32)
    input_grad = (grad_one + lax.psum(input_terms, "tp"))[None]
    grad_query, grad_key, grad_value, grad_out, grad_inner, grad_outer = (
        lax.psum_scatter(grad_query_local, ("shard", "ctx"), scatter_dimension=0, tiled=True),
        lax.psum_scatter(grad_key_local, ("shard", "ctx"), scatter_dimension=0, tiled=True),
        lax.psum_scatter(grad_value_local, ("shard", "ctx"), scatter_dimension=0, tiled=True),
        lax.psum_scatter(grad_out_local, ("shard", "ctx"), scatter_dimension=1, tiled=True),
        lax.psum_scatter(grad_inner_local, ("shard", "ctx"), scatter_dimension=0, tiled=True),
        lax.psum_scatter(grad_outer_local, ("shard", "ctx"), scatter_dimension=1, tiled=True),
    )
    gain_grad, bias_grad = lax.psum(
        (jnp.stack([gain_one, gain_two]), jnp.stack([shift_one, shift_two])), ("shard", "ctx")
    )
    moment_query = BETA * mom_query + (1.0 - BETA) * grad_query
    moment_key = BETA * mom_key + (1.0 - BETA) * grad_key
    moment_value = BETA * mom_value + (1.0 - BETA) * grad_value
    moment_out = BETA * mom_out + (1.0 - BETA) * grad_out
    moment_inner = BETA * mom_inner + (1.0 - BETA) * grad_inner
    moment_outer = BETA * mom_outer + (1.0 - BETA) * grad_outer
    gain_moment_new = BETA * gain_moment + (1.0 - BETA) * gain_grad
    bias_moment_new = BETA * bias_moment + (1.0 - BETA) * bias_grad
    group = lax.axis_size("shard") * lax.axis_size("ctx")
    local_rows = moment_query.shape[0]
    head_cols = moment_query.shape[1]
    inner_cols = moment_inner.shape[1]
    columns = jnp.concatenate(
        [moment_query, moment_key, moment_value, moment_out.T, moment_inner, moment_outer.T], axis=1
    )
    block_total = columns.shape[1] // BW
    slot_count = -(-block_total // group)
    blocks = jnp.transpose(columns.reshape(local_rows, block_total, BW), (1, 0, 2))
    filler = jnp.zeros((slot_count * group - block_total, local_rows, BW), jnp.float32)
    blocks = jnp.concatenate([blocks, filler], axis=0).reshape(slot_count, group, local_rows, BW)
    returned = owner_work(
        lax.all_to_all(
            blocks.astype(jnp.bfloat16), ("shard", "ctx"), split_axis=1, concat_axis=2, tiled=True
        ).astype(blocks.dtype)
    )
    ordered = returned.reshape(slot_count * group, local_rows, BW)[:block_total]
    directions = jnp.transpose(ordered, (1, 0, 2)).reshape(local_rows, block_total * BW)
    new_query = w_query - MATRIX_RATE * directions[:, :head_cols]
    new_key = w_key - MATRIX_RATE * directions[:, head_cols : 2 * head_cols]
    new_value = w_value - MATRIX_RATE * directions[:, 2 * head_cols : 3 * head_cols]
    new_out = w_out - MATRIX_RATE * directions[:, 3 * head_cols : 4 * head_cols].T
    new_inner = w_inner - MATRIX_RATE * directions[:, 4 * head_cols : 4 * head_cols + inner_cols]
    new_outer = w_outer - MATRIX_RATE * directions[:, 4 * head_cols + inner_cols :].T
    tokens_all = hidden_in.shape[0] * length * lax.axis_size("shard") * lax.axis_size("ctx")
    new_gains = norm_gains - VECTOR_RATE * gain_moment_new / math.sqrt(tokens_all)
    new_biases = norm_biases - VECTOR_RATE * bias_moment_new / math.sqrt(tokens_all)
    return (
        layer_out,
        input_grad,
        grad_query,
        grad_key,
        grad_value,
        grad_out,
        grad_inner,
        grad_outer,
        gain_grad,
        bias_grad,
        moment_query,
        moment_key,
        moment_value,
        moment_out,
        moment_inner,
        moment_outer,
        gain_moment_new,
        bias_moment_new,
        new_query,
        new_key,
        new_value,
        new_out,
        new_inner,
        new_outer,
        new_gains,
        new_biases,
    )


def solution(mesh):
    placed = (
        P("shard", "ctx", None),
        P(None, "shard", "ctx"),
        P("shard", "ctx", None),
        P(("shard", "ctx"), "tp"),
        P(("shard", "ctx"), "tp"),
        P(("shard", "ctx"), "tp"),
        P("tp", ("shard", "ctx")),
        P(("shard", "ctx"), "tp"),
        P("tp", ("shard", "ctx")),
        P(),
        P(),
        P(("shard", "ctx"), "tp"),
        P(("shard", "ctx"), "tp"),
        P(("shard", "ctx"), "tp"),
        P("tp", ("shard", "ctx")),
        P(("shard", "ctx"), "tp"),
        P("tp", ("shard", "ctx")),
        P(),
        P(),
    )
    return jax.shard_map(
        body,
        mesh=mesh,
        in_specs=placed,
        out_specs=(
            P("shard", "ctx", None),
            P("shard", "ctx", None),
            P(("shard", "ctx"), "tp"),
            P(("shard", "ctx"), "tp"),
            P(("shard", "ctx"), "tp"),
            P("tp", ("shard", "ctx")),
            P(("shard", "ctx"), "tp"),
            P("tp", ("shard", "ctx")),
            P(),
            P(),
            P(("shard", "ctx"), "tp"),
            P(("shard", "ctx"), "tp"),
            P(("shard", "ctx"), "tp"),
            P("tp", ("shard", "ctx")),
            P(("shard", "ctx"), "tp"),
            P("tp", ("shard", "ctx")),
            P(),
            P(),
            P(("shard", "ctx"), "tp"),
            P(("shard", "ctx"), "tp"),
            P(("shard", "ctx"), "tp"),
            P("tp", ("shard", "ctx")),
            P(("shard", "ctx"), "tp"),
            P("tp", ("shard", "ctx")),
            P(),
            P(),
        ),
        check_vma=False,
    )
```

profile of v0, /device:TPU:0, one launch (start us, length us, event | category | flops | bytes accessed | tf_op | source)
XLA Modules:
  0.0 2192.5 jit_solution(14958268826398096346)
XLA Ops:
  12.8 28.3 %all-gather.9.cloned.1.call-done = bf16[2048,512]{1,0:T(8,128)(2,1)} async-done(((bf16[256,512]{1,0:T(8,128)(2,1)}), bf16[2048,512]{1,0:T(8,128)(2,1)}) %all-gather.9.cloned.1.call-update) | async-done | bytes 2097168 | tf_op jit(solution)/shard_map/all_gather | solution.py:110
  46.3 25.2 %all-gather.7.cloned.1.call-done = bf16[2048,512]{1,0:T(8,128)(2,1)} async-done(((bf16[256,512]{1,0:T(8,128)(2,1)}), bf16[2048,512]{1,0:T(8,128)(2,1)}) %all-gather.7.cloned.1.call-update) | async-done | bytes 2097168 | tf_op jit(solution)/shard_map/all_gather | solution.py:109
  83.5 18.4 all-gather.11.cloned.1.call-done
  120.4 33.5 %while.32 = (s32[]{:T(128)}, bf16[2,512,512]{2,1,0:T(8,128)(2,1)}, f32[2,4,512]{2,1,0:T(4,128)S(1)}, s32[2]{0:T(128)S(1)}, bf16[2048,4,128]{2,1,0:T(4,128)(2,1)S...) while((s32[]{:T(128)}, bf16[2,512,512]{2,1,0:T(8,128)(2,1)}, ...), condition=%wide.region_3.4_spmd, body=%wide.region_0.3_spmd.sunk | while | flops 1653866496 | bytes 50426156 | solution.py:169
  168.2 285.3 %all-reduce.7.cloned.1.call-done = f32[1024,2048]{1,0:T(8,128)} async-done(((f32[1024,2048]{1,0:T(8,128)}), f32[1024,2048]{1,0:T(8,128)}) %all-reduce.7.cloned.1.call-update) | async-done | bytes 8388624 | tf_op jit(solution)/shard_map/psum | solution.py:171
  462.4 46.9 %all-gather.15.cloned.1.call-done = bf16[2048,2048]{1,0:T(8,128)(2,1)} async-done(((bf16[256,2048]{1,0:T(8,128)(2,1)}), bf16[2048,2048]{1,0:T(8,128)(2,1)}) %all-gather.15.cloned.1.call-update) | async-done | bytes 8388624 | tf_op jit(solution)/shard_map/all_gather | solution.py:112
  525.1 42.6 %all-gather.17.cloned.1.call-done = bf16[2048,2048]{1,0:T(8,128)(2,1)} async-done(((bf16[2048,256]{1,0:T(8,128)(2,1)}), bf16[2048,2048]{1,0:T(8,128)(2,1)}) %all-gather.17.cloned.1.call-update) | async-done | bytes 8388624 | tf_op jit(solution)/shard_map/all_gather | solution.py:113
  584.4 290.5 %all-reduce.9.cloned.1.call-done = f32[1024,2048]{1,0:T(8,128)} async-done(((f32[1024,2048]{1,0:T(8,128)}), f32[1024,2048]{1,0:T(8,128)}) %all-reduce.9.cloned.1.call-update) | async-done | bytes 8388624 | tf_op jit(solution)/shard_map/psum | solution.py:179
  894.5 20.7 fusion.74
  930.1 289.9 %all-reduce.11.cloned.1.call-done = f32[1024,2048]{1,0:T(8,128)} async-done(((f32[1024,2048]{1,0:T(8,128)}), f32[1024,2048]{1,0:T(8,128)}) %all-reduce.11.cloned.1.call-update) | async-done | bytes 8388624 | tf_op jit(solution)/shard_map/psum | solution.py:190
  1258.6 135.8 %while.33 = (s32[]{:T(128)}, f32[2048,4,128]{0,2,1:T(8,128)}, f32[2048,4,128]{0,2,1:T(8,128)}, bf16[2,512,512]{2,1,0:T(8,128)(2,1)}, s32[2]{0:T(128)S(1)}, /*ind...) while((s32[]{:T(128)}, f32[2048,4,128]{0,2,1:T(8,128)}, ...), condition=%wide.region_17.18_spmd, body=%wide.region_15.17_spmd.sunk | while | flops 4077659136 | bytes 173592944 | solution.py:238
  1277.6 19.3 fusion.275
  1296.9 20.3 fusion.273
  1345.2 19.3 fusion.275
  1364.6 20.4 fusion.273
  1427.8 16.5 fusion.163
  1444.9 17.6 fusion.159
  1474.8 32.4 %reduce-scatter.11.cloned.1.call-done = f32[256,512]{0,1:T(8,128)} async-done(((f32[2048,512]{0,1:T(8,128)}), f32[256,512]{0,1:T(8,128)}) %reduce-scatter.11.cloned.1.call-update) | async-done | bytes 524304 | tf_op jit(solution)/shard_map/reduce_scatter | solution.py:265
  1509.2 53.1 %reduce-scatter.9.cloned.1.call-done = f32[256,512]{0,1:T(8,128)} async-done(((f32[2048,512]{0,1:T(8,128)}), f32[256,512]{0,1:T(8,128)}) %reduce-scatter.9.cloned.1.call-update) | async-done | bytes 524304 | tf_op jit(solution)/shard_map/reduce_scatter | solution.py:264
  1567.4 114.8 %reduce-scatter.15.cloned.1.call-done = f32[256,2048]{1,0:T(8,128)} async-done(((f32[2048,2048]{1,0:T(8,128)}), f32[256,2048]{1,0:T(8,128)}) %reduce-scatter.15.cloned.1.call-update) | async-done | bytes 2097168 | tf_op jit(solution)/shard_map/reduce_scatter | solution.py:267
  1686.8 114.9 %reduce-scatter.17.cloned.1.call-done = f32[2048,256]{0,1:T(8,128)} async-done(((f32[2048,2048]{0,1:T(8,128)}), f32[2048,256]{0,1:T(8,128)}) %reduce-scatter.17.cloned.1.call-update) | async-done | bytes 2097168 | tf_op jit(solution)/shard_map/reduce_scatter | solution.py:268
  1834.8 36.4 %all-to-all-done = bf16[2,8,256,512]{3,2,0,1:T(8,128)(2,1)} async-done(((bf16[2,8,256,512]{3,2,0,1:T(8,128)(2,1)}), bf16[2,8,256,512]{3,2,0,1:T(8,128)(2,1)}, u32[]{:S(2)}, u32[]{:S(2)}) %all-to-all-start) | async-done | bytes 4194336 | tf_op jit(solution)/shard_map/all_to_all | solution.py:294
  2046.9 19.0 copy.254
  2079.9 57.6 %all-reduce.1 = (f32[2,2048]{1,0:T(2,128)S(1)}, f32[2,2048]{1,0:T(2,128)S(1)}) all-reduce(f32[2,2048]{1,0:T(2,128)S(1)} %pad_maximum_fusion.3, f32[2,2048]{1,0:T(2,128)S(1)} %pad_maximum_fusion.4), channel_id=1, replica_groups=mesh['shard'=4,'ctx'=2,'tp'=4] {'shard','ctx'}, use_global_device_ids=true, to_apply=%region_27.28 | all-reduce | flops 8192 | bytes 65536 | tf_op jit(solution)/shard_map/psum | solution.py:270
  (353 shorter events, 584.5 us)
Async XLA Ops:
  7.2 33.9 %all-gather.9.cloned.1.call-start = ((), (), s32[]{:S(2)}) async-start(), calls=%async_computation.9 | async-start | bytes 2359296 | tf_op jit(solution)/shard_map/all_gather | solution.py:110
  9.0 62.5 %all-gather.7.cloned.1.call-start = ((), (), s32[]{:S(2)}) async-start(), calls=%async_computation.8 | async-start | bytes 2359296 | tf_op jit(solution)/shard_map/all_gather | solution.py:109
  10.9 91.0 %all-gather.11.cloned.1.call-start = ((), (), s32[]{:S(2)}) async-start(), calls=%async_computation.10 | async-start | bytes 2359296 | tf_op jit(solution)/shard_map/all_gather | solution.py:108
  12.8 141.2 %all-gather.13.cloned.1.call-start = ((), (), s32[]{:S(2)}) async-start(), calls=%async_computation.11 | async-start | bytes 2359296 | tf_op jit(solution)/shard_map/all_gather | solution.py:111
  78.2 30.5 %collective-permute-start = (bf16[2,512,512]{2,1,0:T(8,128)(2,1)}, bf16[2,512,512]{2,1,0:T(8,128)(2,1)}, u32[]{:S(2)}, u32[]{:S(2)}) collective-permute-start(bf16[2,512,512]{2,1,0:T(8,128)(2,1)} %get-tuple-element.673), channel_id=1, source_target_pairs={{0,4},{1,5},{2,6},{3,7},{8,12},{9,13},{10,14},{11,15},{16,20},{17,... | collective-permute-start | bytes 3145736 | tf_op jit(solution)/shard_map/ppermute | solution.py:35
  81.3 27.3 %collective-permute-start.1 = (bf16[2,512,512]{2,1,0:T(8,128)(2,1)}, bf16[2,512,512]{2,1,0:T(8,128)(2,1)}, u32[]{:S(2)}, u32[]{:S(2)}) collective-permute-start(bf16[2,512,512]{2,1,0:T(8,128)(2,1)} %get-tuple-element.674), channel_id=1, source_target_pairs={{4,0},{5,1},{6,2},{7,3},{12,8},{13,9},{14,10},{15,11},{20,16},{21,... | collective-permute-start | bytes 3145736 | tf_op jit(solution)/shard_map/ppermute | solution.py:38
  83.4 370.1 %all-reduce.7.cloned.1.call-start = ((), (), s32[]{:S(2)}) async-start(), calls=%async_computation.12 | async-start | bytes 16777216 | tf_op jit(solution)/shard_map/psum | solution.py:171
  162.5 346.8 %all-gather.15.cloned.1.call-start = ((), (), s32[]{:S(2)}) async-start(), calls=%async_computation.13 | async-start | bytes 9437184 | tf_op jit(solution)/shard_map/all_gather | solution.py:112
  165.1 402.6 %all-gather.17.cloned.1.call-start = ((), (), s32[]{:S(2)}) async-start(), calls=%async_computation.14 | async-start | bytes 9437184 | tf_op jit(solution)/shard_map/all_gather | solution.py:113
  167.9 707.1 %all-reduce.9.cloned.1.call-start = ((), (), s32[]{:S(2)}) async-start(), calls=%async_computation.15 | async-start | bytes 16777216 | tf_op jit(solution)/shard_map/psum | solution.py:179
  168.2 1062.7 %copy-start.34 = (f32[1,2048]{1,0:T(1,128)}, f32[1,2048]{1,0:T(1,128)S(1)}, u32[]{:S(2)}) copy-start(f32[1,2048]{1,0:T(1,128)S(1)} %get-tuple-element.680) | copy-start | bytes 24580
  459.0 772.0 %copy-start.38 = (f32[1024]{0:T(1024)}, f32[1024]{0:T(1024)S(1)}, u32[]{:S(2)}) copy-start(f32[1024]{0:T(1024)S(1)} %broadcast_multiply_fusion.3) | copy-start | bytes 12292
  584.0 636.1 %all-reduce.11.cloned.1.call-start = ((), (), s32[]{:S(2)}) async-start(), calls=%async_computation.16 | async-start | bytes 16777216 | tf_op jit(solution)/shard_map/psum | solution.py:190
  930.1 537.1 %reduce-scatter.13.cloned.1.call-start = ((), (), s32[]{:S(2)}) async-start(), calls=%async_computation.21 | async-start | bytes 4718592 | tf_op jit(solution)/shard_map/reduce_scatter | solution.py:266
  1243.8 226.3 %reduce-scatter.7.cloned.1.call-start = ((), (), s32[]{:S(2)}) async-start(), calls=%async_computation.18 | async-start | bytes 4718592 | tf_op jit(solution)/shard_map/reduce_scatter | solution.py:263
  1401.3 105.9 %reduce-scatter.11.cloned.1.call-start = ((), (), s32[]{:S(2)}) async-start(), calls=%async_computation.20 | async-start | bytes 4718592 | tf_op jit(solution)/shard_map/reduce_scatter | solution.py:265
  1406.2 5.2 collective-permute-start.2
  1407.8 5.4 collective-permute-start.3
  1420.4 141.8 %reduce-scatter.9.cloned.1.call-start = ((), (), s32[]{:S(2)}) async-start(), calls=%async_computation.19 | async-start | bytes 4718592 | tf_op jit(solution)/shard_map/reduce_scatter | solution.py:264
  1427.1 255.2 %reduce-scatter.15.cloned.1.call-start = ((), (), s32[]{:S(2)}) async-start(), calls=%async_computation.22 | async-start | bytes 18874368 | tf_op jit(solution)/shard_map/reduce_scatter | solution.py:267
  1444.3 357.4 %reduce-scatter.17.cloned.1.call-start = ((), (), s32[]{:S(2)}) async-start(), calls=%async_computation.23 | async-start | bytes 18874368 | tf_op jit(solution)/shard_map/reduce_scatter | solution.py:268
  1817.4 53.8 %all-to-all-start = ((bf16[2,8,256,512]{3,2,0,1:T(8,128)(2,1)}), bf16[2,8,256,512]{3,2,0,1:T(8,128)(2,1)}, u32[]{:S(2)}, u32[]{:S(2)}) async-start(bf16[2,8,256,512]{3,2,0,1:T(8,128)(2,1)} %copy.247), calls=%async_computation.6 | async-start | bytes 8388608 | tf_op jit(solution)/shard_map/all_to_all | solution.py:294
  1822.1 322.1 %all-reduce.13.cloned.1.call-start = ((), (), s32[]{:S(2)}) async-start(), calls=%async_computation.17 | async-start | bytes 16777216 | tf_op jit(solution)/shard_map/psum | solution.py:261
  2065.9 93.1 %all-to-all-start.1 = ((bf16[2,1,2048,512]{3,0,1,2:T(2,128)(2,1)}), bf16[2,1,2048,512]{3,0,1,2:T(2,128)(2,1)}, u32[]{:S(2)}, u32[]{:S(2)}) async-start(bf16[2,1,2048,512]{3,0,1,2:T(2,128)(2,1)} %copy.254), calls=%async_computation.7 | async-start | bytes 8388608 | tf_op jit(solution)/shard_map/all_to_all | solution.py:75
  (61 other events, 2746.1 us)
Sparse Core Ops, SparseCore 0:
  10.5 30.5 all-gather.8
  43.6 27.8 all-gather.6
  74.0 27.8 all-gather.10
  104.2 28.2 all-gather.12
  162.6 290.8 all-reduce.6
  455.8 53.3 all-gather.14
  511.7 55.9 all-gather.16
  584.1 290.8 all-reduce.8
  930.2 289.8 all-reduce.10
  1244.0 50.3 reduce-scatter.12
  1401.4 51.2 reduce-scatter.6
  1455.8 51.2 reduce-scatter.10
  1510.9 51.3 reduce-scatter.8
  1566.3 115.9 reduce-scatter.14
  1685.7 115.9 reduce-scatter.16
  1834.9 292.1 all-reduce.12
where the time goes:
time: 2200 us; the launch traced here: 2190 us
  waiting for transfers between devices  1380 us (63%)
  matrix products  477 us (22%)
  local copies, waits for them, and re-layouts  120 us (5%)
  other arithmetic  119 us (5%)
  blocking collectives  57.6 us (3%)
    psum x1, waiting for transfers between devices, body(): lax.psum(jnp.dot(act_low, full_outer, preferred_element_type=jnp.float32)...  291 us
    psum x1, waiting for transfers between devices, body(): lax.psum(jnp.dot(dpre_low, full_inner.T, preferred_element_type=jnp.float...  290 us
    psum x1, waiting for transfers between devices, body(): lax.psum(jnp.dot(attended, full_out, preferred_element_type=jnp.float32),...  285 us
    reduce_scatter x1, waiting for transfers between devices, body(): lax.psum_scatter(grad_outer_local, ('shard', 'ctx'), scatter_dimension=1,...  115 us
    reduce_scatter x1, waiting for transfers between devices, body(): lax.psum_scatter(grad_inner_local, ('shard', 'ctx'), scatter_dimension=0,...  115 us
    dot_general x5, matrix products, newton_schulz(): jnp.einsum('kdi,kij->kdj', iterate, polynomial, precision=lax.Precision.H...  77.2 us
    dot_general x5, matrix products, newton_schulz(): jnp.einsum('kdi,kdj->kij', iterate, iterate, precision=lax.Precision.HIGH...  70.7 us
    psum x1, blocking collectives, body(): lax.psum((jnp.stack([gain_one, gain_two]), jnp.stack([shift_one, shift_tw...  57.6 us
  transfers between devices with their start and end apart: 22, of which 14 were waited for; matrix products, arithmetic and copies ran while one was open for 25% of the time, Pallas kernels for 0%

commit v1 on v0

v1 whole, which is shorter than its diff:
```python
import functools
import math

import jax
import jax.numpy as jnp
from jax import lax
from jax.experimental import pallas as pl
from jax.experimental.pallas import tpu as pltpu
from jax.sharding import PartitionSpec as P

HEAD_DIM = 128
REACH = 512
BW = 512
NS_STEPS = 5
QUERY_ROWS = 256

NS_COEFFS = (3.4445, -4.775, 2.0315)
LN_EPSILON = 1e-12
BETA = 0.5
MATRIX_RATE = 0.5
VECTOR_RATE = 0.3
MASKED = -1e30
WEIGHT_AXES = ("shard", "ctx")
BF16 = jnp.bfloat16
F32 = jnp.float32


def upward(first, last):
    return [(i, i + 1) for i in range(first, last)]


def downward(first, last):
    return [(i, i - 1) for i in range(first, last)]


def ring(count, by):
    return [(i, (i + by) % count) for i in range(count)]


def spread(block, axis):
    count = lax.axis_size(axis)
    return [block] + [lax.ppermute(block, axis, ring(count, r)) for r in range(1, count)]


def send_slot(block, axis, r):
    return lax.ppermute(block, axis, ring(lax.axis_size(axis), -r))


def slot_order(count):
    return sorted(range(1, count), key=lambda r: (-min(r, count - r), r)) + [0]


def total_over(value, axes):
    for axis in axes:
        by = 1
        while by < lax.axis_size(axis):
            pairs = [(i, i ^ by) for i in range(lax.axis_size(axis))]
            value = value + lax.ppermute(value, axis, pairs)
            by *= 2
    return value


def after(value, *others):
    return lax.optimization_barrier((value, *others))[0]


def dot(left, right):
    return jnp.dot(left, right, preferred_element_type=F32)


def dot_nt(left, right):
    return lax.dot_general(left, right, (((1,), (1,)), ((), ())), preferred_element_type=F32)


def dot_tn(left, right):
    return lax.dot_general(left, right, (((0,), (0,)), ((), ())), preferred_element_type=F32)


def normalize(hidden):
    centred = hidden - jnp.mean(hidden, axis=-1, keepdims=True)
    variance = jnp.mean(centred * centred, axis=-1, keepdims=True)
    scale = lax.rsqrt(variance + LN_EPSILON)
    return centred * scale, scale


def norm_backward(grad, unit, scale, gain):
    scaled = grad * gain
    inner = jnp.mean(scaled * unit, axis=-1, keepdims=True)
    dhidden = scale * (scaled - jnp.mean(scaled, axis=-1, keepdims=True) - unit * inner)
    return dhidden, jnp.sum(grad * unit, axis=0), jnp.sum(grad, axis=0)


def gelu_tanh(values):
    return jax.nn.gelu(values, approximate=True)


def window_probs(q, keys, low_ref, high_ref, start):
    scores = dot_nt(keys, q) * (HEAD_DIM**-0.5)
    at = start + lax.broadcasted_iota(jnp.int32, scores.shape, 0)
    scores = jnp.where((at >= low_ref[...]) & (at <= high_ref[...]), scores, MASKED)
    expo = jnp.exp(scores - jnp.max(scores, axis=0, keepdims=True))
    return expo * (1.0 / jnp.sum(expo, axis=0, keepdims=True))


def attend_kernel(low_ref, high_ref, q_ref, k_ref, v_ref, o_ref):
    rows = q_ref.shape[0]
    span = rows + 2 * REACH
    start = pl.multiple_of(pl.program_id(1) * rows, rows)
    probs = window_probs(q_ref[...], k_ref[pl.ds(start, span), :], low_ref, high_ref, start)
    o_ref[...] = dot_tn(probs.astype(BF16), v_ref[pl.ds(start, span), :]).astype(BF16)


def attend_back_kernel(low_ref, high_ref, q_ref, k_ref, v_ref, g_ref, dq_ref, dk_ref, dv_ref):
    rows = q_ref.shape[0]
    span = rows + 2 * REACH
    start = pl.multiple_of(pl.program_id(1) * rows, rows)
    window = pl.ds(start, span)

    @pl.when(pl.program_id(1) == 0)
    def _():
        dk_ref[...] = jnp.zeros_like(dk_ref)
        dv_ref[...] = jnp.zeros_like(dv_ref)

    q, g, keys = q_ref[...], g_ref[...], k_ref[window, :]
    probs = window_probs(q, keys, low_ref, high_ref, start)
    dprobs = dot_nt(v_ref[window, :], g)
    offset = jnp.sum(dprobs * probs, axis=0, keepdims=True)
    dscores = (probs * (dprobs - offset) * (HEAD_DIM**-0.5)).astype(BF16)
    dv_ref[window, :] += dot(probs.astype(BF16), g)
    dk_ref[window, :] += dot(dscores, q)
    dq_ref[...] = dot_tn(dscores, keys).astype(BF16)


def attention_specs(rows, padded, heads):
    bounds = pl.BlockSpec((1, rows), lambda h, b: (0, b))
    queries = pl.BlockSpec((rows, HEAD_DIM), lambda h, b: (b, h))
    keys = pl.BlockSpec((padded, HEAD_DIM), lambda h, b: (0, h))
    values = pl.BlockSpec((padded, HEAD_DIM), lambda h, b: (0, h + heads))
    return bounds, queries, keys, values


def attend(low, high, queries, padded_kv, heads):
    length, padded = queries.shape[0], padded_kv.shape[0]
    rows = min(QUERY_ROWS, length)
    bounds, q_spec, k_spec, v_spec = attention_specs(rows, padded, heads)
    pairs = heads * length * (rows + 2 * REACH)
    return pl.pallas_call(
        attend_kernel,
        grid=(heads, length // rows),
        in_specs=[bounds, bounds, q_spec, k_spec, v_spec],
        out_specs=q_spec,
        out_shape=jax.ShapeDtypeStruct((length, heads * HEAD_DIM), BF16),
        cost_estimate=pl.CostEstimate(
            flops=16 * pairs * HEAD_DIM, transcendentals=pairs, bytes_accessed=8 << 20
        ),
        name="attend",
    )(low, high, queries, padded_kv, padded_kv)


def attend_back(low, high, queries, padded_kv, grads, heads):
    length, padded = queries.shape[0], padded_kv.shape[0]
    rows = min(QUERY_ROWS, length)
    bounds, q_spec, k_spec, v_spec = attention_specs(rows, padded, heads)
    pairs = heads * length * (rows + 2 * REACH)
    total = jax.ShapeDtypeStruct((padded, heads * HEAD_DIM), F32)
    return pl.pallas_call(
        attend_back_kernel,
        grid=(heads, length // rows),
        in_specs=[bounds, bounds, q_spec, k_spec, v_spec, q_spec],
        out_specs=(q_spec, k_spec, k_spec),
        out_shape=(jax.ShapeDtypeStruct((length, heads * HEAD_DIM), BF16), total, total),
        cost_estimate=pl.CostEstimate(
            flops=32 * pairs * HEAD_DIM, transcendentals=pairs, bytes_accessed=20 << 20
        ),
        name="attend_back",
    )(low, high, queries, padded_kv, padded_kv, grads)


def halves(value):
    top = value.astype(BF16)
    return top, (value - top.astype(F32)).astype(BF16)


def newton_schulz_kernel(block_ref, out_ref, iterate, top, rest):
    depth, width = block_ref.shape
    chunk = min(256, depth)
    chunks = depth // chunk

    def columns(c):
        return pl.ds(pl.multiple_of(c * chunk, chunk), chunk)

    def load(c, total):
        part = block_ref[columns(c), :].astype(F32)
        iterate[:, columns(c)] = part.T
        return total + jnp.sum(part * part, axis=(0, 1), keepdims=True)

    norm = jnp.sqrt(lax.fori_loop(0, chunks, load, jnp.zeros((1, 1), F32)))
    inverse = 1.0 / (norm + 1e-07)

    def split(c, scale):
        value = iterate[:, columns(c)] * scale
        iterate[:, columns(c)] = value
        top[:, columns(c)], rest[:, columns(c)] = halves(value)
        return scale

    lax.fori_loop(0, chunks, split, inverse)

    def step(index, carry):
        cross = dot_nt(rest[...], top[...])
        gram = dot_nt(top[...], top[...]) + (cross + cross.T)
        gram_top, gram_rest = halves(gram)
        cross = dot(gram_top, gram_rest)
        square = dot(gram_top, gram_top) + (cross + cross.T)
        poly_top, poly_rest = halves(NS_COEFFS[1] * gram + NS_COEFFS[2] * square)

        def update(c, carry):
            here = columns(c)
            change = dot(poly_top, top[:, here]) + dot(poly_rest, top[:, here])
            value = NS_COEFFS[0] * iterate[:, here] + (change + dot(poly_top, rest[:, here]))
            iterate[:, here] = value
            top[:, here], rest[:, here] = halves(value)
            return carry

        return lax.fori_loop(0, chunks, update, carry)

    lax.fori_loop(0, NS_STEPS, step, 0)

    def store(c, carry):
        out_ref[columns(c), :] = iterate[:, columns(c)].T.astype(BF16)
        return carry

    lax.fori_loop(0, chunks, store, 0)


def newton_schulz(block):
    depth, width = block.shape
    return pl.pallas_call(
        newton_schulz_kernel,
        out_shape=jax.ShapeDtypeStruct((depth, width), BF16),
        in_specs=[pl.BlockSpec(memory_space=pltpu.VMEM)],
        out_specs=pl.BlockSpec(memory_space=pltpu.VMEM),
        scratch_shapes=[
            pltpu.VMEM((width, depth), F32),
            pltpu.VMEM((width, depth), BF16),
            pltpu.VMEM((width, depth), BF16),
        ],
        cost_estimate=pl.CostEstimate(
            flops=2 * NS_STEPS * width * width * (5 * depth + 2 * width),
            transcendentals=0,
            bytes_accessed=4 * depth * width,
        ),
        name="newton_schulz",
    )(block)


def orthogonal_blocks(blocks):
    group = lax.axis_size("shard") * lax.axis_size("ctx")
    copies = group // len(blocks)
    sent = jnp.stack([block.astype(BF16) for block in blocks for _ in range(copies)])
    owned = lax.all_to_all(sent, WEIGHT_AXES, split_axis=0, concat_axis=0, tiled=True)
    done = newton_schulz(owned.reshape(-1, BW)).reshape(owned.shape)
    back = lax.all_to_all(done, WEIGHT_AXES, split_axis=0, concat_axis=0, tiled=True)
    return [back[b * copies].astype(F32) for b in range(len(blocks))]


def column_blocks(value):
    return [value[:, at : at + BW] for at in range(0, value.shape[1], BW)]


def gather_rows(value):
    return lax.all_gather(value, WEIGHT_AXES, axis=0, tiled=True)


def scatter_rows(value):
    low = value.astype(BF16)
    return lax.psum_scatter(low, WEIGHT_AXES, scatter_dimension=0, tiled=True).astype(F32)


def blend(old, grad):
    return BETA * old + (1.0 - BETA) * grad


def body(
    hidden_in,
    doc_span,
    cotangent,
    w_query,
    w_key,
    w_value,
    w_out,
    w_inner,
    w_outer,
    norm_gains,
    norm_biases,
    mom_query,
    mom_key,
    mom_value,
    mom_out,
    mom_inner,
    mom_outer,
    gain_moment,
    bias_moment,
):
    tp = lax.axis_size("tp")
    me = lax.axis_index("tp")
    hidden = hidden_in[0]
    length, width = hidden.shape
    share = length // tp
    local = w_query.shape[1]
    heads = local // HEAD_DIM

    def slice_of(value, r):
        return lax.dynamic_slice_in_dim(value, lax.rem(me - r + tp, tp) * share, share, 0)

    def in_place(slots, dtype):
        whole = jnp.zeros((length, slots[0].shape[1]), dtype)
        for r, slot in enumerate(slots):
            at = lax.rem(me - r + tp, tp) * share
            whole = lax.dynamic_update_slice_in_dim(whole, slot.astype(dtype), at, 0)
        return whole

    full_qkv = gather_rows(jnp.concatenate([w_query, w_key, w_value], axis=1).astype(BF16))
    out_slots = spread(w_out.T.astype(BF16), "tp")
    full_out_t = gather_rows(after(jnp.concatenate(out_slots, axis=1), full_qkv))
    full_inner = gather_rows(after(w_inner.astype(BF16), full_out_t))
    full_outer_t = gather_rows(after(w_outer.T.astype(BF16), full_inner))

    qkv = dot(hidden, full_qkv).astype(BF16)
    queries, own_kv = qkv[:, :local], qkv[:, local:]
    ctx = lax.axis_size("ctx")
    above = lax.ppermute(own_kv[length - REACH :], "ctx", upward(0, ctx - 1))
    below = lax.ppermute(own_kv[:REACH], "ctx", downward(1, ctx))
    padded_kv = jnp.concatenate([above, own_kv, below], axis=0)

    position = jnp.arange(length, dtype=jnp.int32)
    anchor = lax.axis_index("ctx") * length - REACH
    low = jnp.maximum(doc_span[0] - anchor, position[None])
    high = jnp.minimum(doc_span[1] - anchor, position[None] + 2 * REACH)
    attended = attend(low, high, queries, padded_kv, heads)

    head_slots = spread(attended, "tp")
    order = slot_order(tp)
    attended_slots, normed_slots, pre_slots, act_slots, sums = ([None] * tp for _ in range(5))
    for r in order:
        attended_slots[r] = jnp.concatenate([slice_of(slot, r) for slot in head_slots], axis=1)
        branch = dot_nt(attended_slots[r], full_out_t)
        unit, scale = normalize(slice_of(hidden, r).astype(F32) + branch)
        normed = unit * norm_gains[0] + norm_biases[0]
        normed_slots[r] = normed.astype(BF16)
        pre_slots[r] = dot(normed_slots[r], full_inner)
        act_slots[r] = gelu_tanh(pre_slots[r]).astype(BF16)
        sums[r] = dot_nt(act_slots[r], full_outer_t)
        if r:
            sums[r] = send_slot(sums[r].astype(BF16), "tp", r).astype(F32)
    unit_one, scale_one, own_normed = unit, scale, normed
    second = own_normed + sum(sums[1:], sums[0])

    unit_two, scale_two = normalize(second)
    own_out = (unit_two * norm_gains[1] + norm_biases[1]).astype(BF16)
    seed = slice_of(cotangent[0], 0).astype(F32)
    grad_two, gain_two, shift_two = norm_backward(seed, unit_two, scale_two, norm_gains[1])
    dffn_slots = spread(grad_two.astype(BF16), "tp")
    slopes = lax.optimization_barrier((*pre_slots, dffn_slots[0]))[:tp]
    slopes = [jax.vjp(gelu_tanh, pre)[1](jnp.ones_like(pre))[0] for pre in slopes]
    slopes = lax.optimization_barrier(slopes)
    dpre_slots, sums = [None] * tp, [None] * tp
    for r in order:
        dact = dot(dffn_slots[r], full_outer_t)
        dpre_slots[r] = (dact * slopes[r]).astype(BF16)
        sums[r] = dot_nt(dpre_slots[r], full_inner)
        if r:
            sums[r] = send_slot(sums[r].astype(BF16), "tp", r).astype(F32)
    act = jnp.concatenate(act_slots, axis=0)
    dffn = jnp.concatenate(dffn_slots, axis=0)
    act = after(act, *dpre_slots, sums[0])
    grad_outer_t = scatter_rows(dot_tn(dffn, act))
    normed_low = jnp.concatenate(normed_slots, axis=0)
    dpre = jnp.concatenate(dpre_slots, axis=0)
    grad_inner = scatter_rows(dot_tn(normed_low, dpre))
    dnormed = grad_two + sum(sums[1:], sums[0])

    grad_one, gain_one, shift_one = norm_backward(dnormed, unit_one, scale_one, norm_gains[0])
    dbranch_low = grad_one.astype(BF16)
    dattended_all = dot(dbranch_low, full_out_t).astype(BF16)
    dattended_slots = []
    for r in range(tp):
        sent = dattended_all[:, ((tp - r) % tp) * local : ((tp - r) % tp + 1) * local]
        if r:
            sent = lax.ppermute(sent, "tp", ring(tp, r))
        dattended_slots.append(sent)
    dattended = in_place(dattended_slots, BF16)

    part = width // tp
    dbranch_slots = []
    for r in range(tp):
        at = lax.rem(me + r, tp) * part
        sent = lax.dynamic_slice_in_dim(after(dbranch_low, dattended_all), at, part, 1)
        dbranch_slots.append(lax.ppermute(sent, "tp", ring(tp, r)) if r else sent)
    out_slots = spread(after(own_out, dattended), "tp")

    dq_low, key_grad, value_grad = attend_back(low, high, queries, padded_kv, dattended, heads)
    kv_grad = jnp.concatenate([key_grad, value_grad], axis=1)
    from_above = lax.ppermute(kv_grad[:REACH].astype(BF16), "ctx", downward(1, ctx))
    from_below = lax.ppermute(kv_grad[length + REACH :].astype(BF16), "ctx", upward(0, ctx - 1))
    centre = kv_grad[REACH : length + REACH]
    centre = centre.at[length - REACH :].add(from_above.astype(F32))
    centre = centre.at[:REACH].add(from_below.astype(F32))
    dqkv = jnp.concatenate([dq_low, centre.astype(BF16)], axis=1)
    grad_qkv = dot_tn(hidden, dqkv).astype(BF16)
    dqkv = after(dqkv, grad_qkv)
    grad_qkv = scatter_rows(grad_qkv)
    sums = [None] * tp
    for r in order:
        sums[r] = dot_nt(slice_of(dqkv, r), full_qkv)
        if r:
            sums[r] = send_slot(sums[r].astype(BF16), "tp", r).astype(F32)
    own_input_grad = grad_one + sum(sums[1:], sums[0])
    input_grad = in_place(spread(own_input_grad.astype(BF16), "tp"), F32)[None]
    layer_out = in_place(out_slots, BF16)[None]

    rows = w_query.shape[0]
    group = width // rows
    dbranch = jnp.concatenate(dbranch_slots, axis=0)
    attended_all = after(jnp.concatenate(attended_slots, axis=0), dqkv)
    pieces = dot_tn(dbranch, attended_all).astype(BF16).reshape(group // tp, rows, tp, local)
    pieces = jnp.transpose(pieces, (0, 2, 1, 3)).reshape(group * rows, local)
    piece = lax.psum_scatter(pieces, WEIGHT_AXES, scatter_dimension=0, tiled=True)
    homes = [
        (p * tp + t, (t * (group // tp) + p // tp) * tp + (t - p % tp) % tp)
        for p in range(group)
        for t in range(tp)
    ]
    grad_out_t = lax.ppermute(piece, (*WEIGHT_AXES, "tp"), homes).astype(F32)

    totals = total_over(
        jnp.stack([gain_one, gain_two, shift_one, shift_two]), ("ctx", "shard", "tp")
    )
    gain_grad, bias_grad = totals[:2], totals[2:]

    moment_inner = blend(mom_inner, grad_inner)
    moment_outer_t = blend(mom_outer.T, grad_outer_t)
    ortho = orthogonal_blocks(column_blocks(moment_inner) + column_blocks(moment_outer_t))
    half = len(ortho) // 2
    new_inner = w_inner - MATRIX_RATE * jnp.concatenate(ortho[:half], axis=1)
    new_outer = w_outer - MATRIX_RATE * jnp.concatenate(ortho[half:], axis=1).T

    grad_query, grad_key, grad_value = jnp.split(grad_qkv, 3, axis=1)
    moment_query = blend(mom_query, grad_query)
    moment_key = blend(mom_key, grad_key)
    moment_value = blend(mom_value, grad_value)
    moment_out_t = blend(mom_out.T, grad_out_t)
    ortho = orthogonal_blocks(
        sum(map(column_blocks, (moment_query, moment_key, moment_value, moment_out_t)), [])
    )
    per = len(ortho) // 4
    ortho = [jnp.concatenate(ortho[per * m : per * m + per], axis=1) for m in range(4)]
    new_query = w_query - MATRIX_RATE * ortho[0]
    new_key = w_key - MATRIX_RATE * ortho[1]
    new_value = w_value - MATRIX_RATE * ortho[2]
    new_out = w_out - MATRIX_RATE * ortho[3].T

    tokens_all = length * lax.axis_size("shard") * ctx
    gain_moment_new = blend(gain_moment, gain_grad)
    bias_moment_new = blend(bias_moment, bias_grad)
    new_gains = norm_gains - VECTOR_RATE * gain_moment_new / math.sqrt(tokens_all)
    new_biases = norm_biases - VECTOR_RATE * bias_moment_new / math.sqrt(tokens_all)
    return (
        layer_out,
        input_grad,
        grad_query,
        grad_key,
        grad_value,
        grad_out_t.T,
        grad_inner,
        grad_outer_t.T,
        gain_grad,
        bias_grad,
        moment_query,
        moment_key,
        moment_value,
        moment_out_t.T,
        moment_inner,
        moment_outer_t.T,
        gain_moment_new,
        bias_moment_new,
        new_query,
        new_key,
        new_value,
        new_out,
        new_inner,
        new_outer,
        new_gains,
        new_biases,
    )


def solution(mesh):
    tokens = P("shard", "ctx", None)
    by_rows = P(WEIGHT_AXES, "tp")
    by_columns = P("tp", WEIGHT_AXES)
    matrices = (by_rows, by_rows, by_rows, by_columns, by_rows, by_columns)
    return jax.shard_map(
        body,
        mesh=mesh,
        in_specs=(tokens, P(None, "shard", "ctx"), tokens, *matrices, P(), P(), *matrices, P(), P()),
        out_specs=(tokens, tokens, *matrices, P(), P(), *matrices, P(), P(), *matrices, P(), P()),
        check_vma=False,
    )
```

time: 2200 us -> 1410 us (0.64)
  waiting for transfers between devices: 1380 us -> 584 us
  matrix products: 477 us -> 165 us
  starting transfers between devices: 20.7 us -> 268 us
  Pallas kernels: 0 us -> 149 us
  blocking collectives: 57.6 us -> 0 us
  local copies, waits for them, and re-layouts: 120 us -> 94.5 us
    psum x4 -> x0, waiting for transfers between devices: 866 us -> none  [the longest x1 291 us: body(): lax.psum(jnp.dot(act_low, full_outer, preferred_element_type=jnp.float32)...]
    ppermute x4 -> x40, waiting for transfers between devices: 1.37 us -> 424 us  [the longest x9 201 us: send_slot(): return lax.ppermute(block, axis, ring(lax.axis_size(axis), -r))]
    reduce_scatter x6 -> x4, waiting for transfers between devices: 315 us -> 0.01 us  [the longest x3 0.01 us: scatter_rows(): lax.psum_scatter(low, WEIGHT_AXES, scatter_dimension=0, tiled=True)]
    dot_general x47 -> x30, matrix products: 477 us -> 165 us  [the longest x16 70 us: dot_nt(): lax.dot_general(left, right, (((1,), (1,)), ((), ())), preferred_element_...]
    ppermute x4 -> x40, starting transfers between devices: 9.16 us -> 227 us  [the longest x9 116 us: send_slot(): return lax.ppermute(block, axis, ring(lax.axis_size(axis), -r))]
    pallas_call x0 -> x4, Pallas kernels: none -> 149 us  [the longest x2 94.2 us: newton_schulz(): pl.pallas_call(newton_schulz_kernel, out_shape=jax.ShapeDtypeStruct((dept...]
    concatenate x2 -> x6, other arithmetic: 5.43 us -> 67.2 us  [the longest x1 57.9 us: body(): attended_all = after(jnp.concatenate(attended_slots, axis=0), dqkv)]
    psum x1 -> x0, blocking collectives: 57.6 us -> none  [body(): lax.psum((jnp.stack([gain_one, gain_two]), jnp.stack([shift_one, shift_tw...]
  transfers between devices with their start and end apart: 22 -> 52, of which waited for: 14 -> 27; matrix products, arithmetic and copies ran while one was open for 25% -> 22% of each run, Pallas kernels for 0% -> 8%
where the time goes in v1:
time: 1410 us; the launch traced here: 1400 us
  waiting for transfers between devices  584 us (41%)
  starting transfers between devices  268 us (19%)
  matrix products  165 us (12%)
  Pallas kernels  149 us (11%)
  other arithmetic  124 us (9%)
  local copies, waits for them, and re-layouts  94.5 us (7%)
  between operations  16.1 us (1%)
    ppermute x9, waiting for transfers between devices, send_slot(): return lax.ppermute(block, axis, ring(lax.axis_size(axis), -r))  201 us
    ppermute x15, waiting for transfers between devices, spread(): lax.ppermute(block, axis, ring(count, r))  197 us
    all_gather x4, waiting for transfers between devices, gather_rows(): return lax.all_gather(value, WEIGHT_AXES, axis=0, tiled=True)  136 us
    ppermute x9, starting transfers between devices, send_slot(): return lax.ppermute(block, axis, ring(lax.axis_size(axis), -r))  116 us
    pallas_call x2, Pallas kernels, newton_schulz(): pl.pallas_call(newton_schulz_kernel, out_shape=jax.ShapeDtypeStruct((dept...  94.2 us
    ppermute x15, starting transfers between devices, spread(): lax.ppermute(block, axis, ring(count, r))  78.7 us
    dot_general x16, matrix products, dot_nt(): lax.dot_general(left, right, (((1,), (1,)), ((), ())), preferred_element_...  70 us
    concatenate x1, other arithmetic, body(): attended_all = after(jnp.concatenate(attended_slots, axis=0), dqkv)  57.9 us
  transfers between devices with their start and end apart: 52, of which 27 were waited for; matrix products, arithmetic and copies ran while one was open for 22% of the time, Pallas kernels for 8%

profile of v1, /device:TPU:0, one launch (start us, length us, event | category | flops | bytes accessed | tf_op | source)
XLA Modules:
  0.0 1401.3 jit_solution(3916390861415029066)
XLA Ops:
  35.4 24.5 %all-gather.5.cloned.1.call-done = bf16[2048,1536]{1,0:T(8,128)(2,1)} async-done(((bf16[256,1536]{1,0:T(8,128)(2,1)}), bf16[2048,1536]{1,0:T(8,128)(2,1)}) %all-gather.5.cloned.1.call-update) | async-done | bytes 6291472 | tf_op jit(solution)/shard_map/all_gather | solution.py:271
  62.8 55.5 %all-gather.7.cloned.1.call-done = bf16[2048,2048]{0,1:T(8,128)(2,1)} async-done(((bf16[256,2048]{0,1:T(8,128)(2,1)}), bf16[2048,2048]{0,1:T(8,128)(2,1)}) %all-gather.7.cloned.1.call-update) | async-done | bytes 8388624 | tf_op jit(solution)/shard_map/all_gather | solution.py:271
  119.5 55.7 %all-gather.9.cloned.1.call-done = bf16[2048,2048]{1,0:T(8,128)(2,1)} async-done(((bf16[256,2048]{1,0:T(8,128)(2,1)}), bf16[2048,2048]{1,0:T(8,128)(2,1)}) %all-gather.9.cloned.1.call-update) | async-done | bytes 8388624 | tf_op jit(solution)/shard_map/all_gather | solution.py:271
  198.4 23.3 %attend.1 = bf16[1024,512]{1,0:T(8,128)(2,1)} custom-call(s32[1,1024]{1,0:T(1,128)} %get-tuple-element.195.low_ref, s32[1,1024]{1,0:T(1,128)} %get-tuple-element.194.high_ref, bf16[1024,512]{1,0:T(8,128)(2,1)} %slice.217.q_ref, bf16[2048,1024]{1,0:T(8,128)(2,1)} %pad_maximum_fusion.k_ref.v_ref, bf16[2048,1024]{1,0:T(8,128)(2,1)} %pad_maximum_fusion.k_ref.v_ref), custom_call_target="tpu_custom_call" | custom-call | flops 10737418240 | bytes 8388608 | tf_op jit(solution)/shard_map/attend/pallas_call | solution.py:147
  228.5 21.3 %collective-permute-done.2 = bf16[1024,512]{1,0:T(8,128)(2,1)} collective-permute-done((bf16[1024,512]{1,0:T(8,128)(2,1)}, bf16[1024,512]{1,0:T(8,128)(2,1)}, u32[]{:S(2)}, u32[]{:S(2)}) %collective-permute-start.2) | collective-permute-done | bytes 1048608 | tf_op jit(solution)/shard_map/ppermute | solution.py:42
  251.2 43.1 %collective-permute-done.3 = bf16[1024,512]{1,0:T(8,128)(2,1)S(1)} collective-permute-done((bf16[1024,512]{1,0:T(8,128)(2,1)}, bf16[1024,512]{1,0:T(8,128)(2,1)S(1)}, u32[]{:S(2)}, u32[]{:S(2)}) %collective-permute-start.3) | collective-permute-done | bytes 1048608 | tf_op jit(solution)/shard_map/ppermute | solution.py:42
  331.4 21.7 %collective-permute-start.9 = (bf16[256,2048]{1,0:T(8,128)(2,1)S(1)}, bf16[256,2048]{1,0:T(8,128)(2,1)S(1)}, u32[]{:S(2)}, u32[]{:S(2)}) collective-permute-start(bf16[256,2048]{1,0:T(8,128)(2,1)S(1)} %convolution_convert_fusion.12), channel_id=1, source_target_pairs={{0,2},{1,3},{2,0},{3,1},{4,6},{5,7},{6,4},{7,5},{8,10},{9,11},{10,... | collective-permute-start | bytes 3145736 | tf_op jit(solution)/shard_map/ppermute | solution.py:46
  365.1 56.9 %collective-permute-done.9 = bf16[256,2048]{1,0:T(8,128)(2,1)S(1)} collective-permute-done((bf16[256,2048]{1,0:T(8,128)(2,1)S(1)}, bf16[256,2048]{1,0:T(8,128)(2,1)S(1)}, u32[]{:S(2)}, u32[]{:S(2)}) %collective-permute-start.9) | collective-permute-done | bytes 1048608 | tf_op jit(solution)/shard_map/ppermute | solution.py:46
  433.1 39.7 %collective-permute-start.11 = (bf16[256,2048]{1,0:T(8,128)(2,1)S(1)}, bf16[256,2048]{1,0:T(8,128)(2,1)S(1)}, u32[]{:S(2)}, u32[]{:S(2)}) collective-permute-start(bf16[256,2048]{1,0:T(8,128)(2,1)S(1)} %fusion.172), channel_id=1, source_target_pairs={{0,1},{1,2},{2,3},{3,0},{4,5},{5,6},{6,7},{7,4},{8,9},{9,10},{10,1... | collective-permute-start | bytes 3145736 | tf_op jit(solution)/shard_map/ppermute | solution.py:42
  481.4 15.0 %collective-permute-done.11 = bf16[256,2048]{1,0:T(8,128)(2,1)S(1)} collective-permute-done((bf16[256,2048]{1,0:T(8,128)(2,1)S(1)}, bf16[256,2048]{1,0:T(8,128)(2,1)S(1)}, u32[]{:S(2)}, u32[]{:S(2)}) %collective-permute-start.11) | collective-permute-done | bytes 1048608 | tf_op jit(solution)/shard_map/ppermute | solution.py:42
  554.5 83.1 %collective-permute-start.16 = (bf16[256,2048]{1,0:T(8,128)(2,1)S(1)}, bf16[256,2048]{1,0:T(8,128)(2,1)S(1)}, u32[]{:S(2)}, u32[]{:S(2)}) collective-permute-start(bf16[256,2048]{1,0:T(8,128)(2,1)S(1)} %convolution_convert_fusion.8), channel_id=1, source_target_pairs={{0,1},{1,2},{2,3},{3,0},{4,5},{5,6},{6,7},{7,4},{8,9},{9,10},{10,1... | collective-permute-start | bytes 3145736 | tf_op jit(solution)/shard_map/ppermute | solution.py:46
  644.4 23.9 %collective-permute-done.16 = bf16[256,2048]{1,0:T(8,128)(2,1)S(1)} collective-permute-done((bf16[256,2048]{1,0:T(8,128)(2,1)S(1)}, bf16[256,2048]{1,0:T(8,128)(2,1)S(1)}, u32[]{:S(2)}, u32[]{:S(2)}) %collective-permute-start.16) | collective-permute-done | bytes 1048608 | tf_op jit(solution)/shard_map/ppermute | solution.py:46
  707.6 32.1 %attend_back.1 = (bf16[1024,512]{1,0:T(8,128)(2,1)}, f32[2048,512]{1,0:T(8,128)}, f32[2048,512]{1,0:T(8,128)}) custom-call(s32[1,1024]{1,0:T(1,128)} %get-tuple-element.195.low_ref, s32[1,1024]{1,0:T(1,128)} %get-tuple-element.194.high_ref, bf16[1024,512]{1,0:T(8,128)(2,1)} %slice.217.q_ref, bf16[2048,1024]{1,0:T(8,128)(2,1)} %pad_maximum_fusion.k_ref.v_ref, ...), custom_call_target="tpu_custom_call" | custom-call | flops 21474836480 | bytes 20971520 | tf_op jit(solution)/shard_map/attend_back/pallas_call | solution.py:166
  749.5 57.9 %maximum_maximum_fusion = bf16[1024,2048]{1,0:T(8,128)(2,1)} fusion(bf16[256,512]{1,0:T(8,128)(2,1)S(1)} %copy-done.56, bf16[256,512]{1,0:T(8,128)(2,1)S(1)} %copy-done.48, bf16[256,512]{1,0:T(8,128)(2,1)S(1)} %copy-done.40, bf16[256,512]{1,0:T(8,128)(2,1)S(1)} %copy-done.32, bf16[256,512]{1,0:T(8,128)(2,1)S(1)} %copy-done.58, ...), kind=kLoop, calls=%fused_computation.5 | loop fusion | flops 67108864 | bytes 8388608 | tf_op jit(solution)/shard_map/concatenate | solution.py:424
  851.4 13.1 convolution_convert_fusion.1
  868.6 11.4 convolution_convert_fusion
  949.7 108.0 %collective-permute-done.26 = bf16[256,2048]{1,0:T(8,128)(2,1)S(1)} collective-permute-done((bf16[256,2048]{1,0:T(8,128)(2,1)S(1)}, bf16[256,2048]{1,0:T(8,128)(2,1)S(1)}, u32[]{:S(2)}, u32[]{:S(2)}) %collective-permute-start.26) | collective-permute-done | bytes 1048608 | tf_op jit(solution)/shard_map/ppermute | solution.py:46
  1066.9 14.2 %collective-permute-start.29 = (bf16[256,2048]{1,0:T(8,128)(2,1)}, bf16[256,2048]{1,0:T(8,128)(2,1)S(1)}, u32[]{:S(2)}, u32[]{:S(2)}) collective-permute-start(bf16[256,2048]{1,0:T(8,128)(2,1)} %get-tuple-element.214), channel_id=1, source_target_pairs={{0,2},{1,3},{2,0},{3,1},{4,6},{5,7},{6,4},{7,5},{8,10},{9,11},{10,... | collective-permute-start | bytes 3145736 | tf_op jit(solution)/shard_map/ppermute | solution.py:42
  1081.1 43.9 %collective-permute-done.21 = bf16[256,2048]{1,0:T(8,128)(2,1)S(1)} collective-permute-done((bf16[256,2048]{1,0:T(8,128)(2,1)S(1)}, bf16[256,2048]{1,0:T(8,128)(2,1)S(1)}, u32[]{:S(2)}, u32[]{:S(2)}) %collective-permute-start.21) | collective-permute-done | bytes 1048608 | tf_op jit(solution)/shard_map/ppermute | solution.py:42
  1129.6 40.4 %collective-permute-done.29 = bf16[256,2048]{1,0:T(8,128)(2,1)S(1)} collective-permute-done((bf16[256,2048]{1,0:T(8,128)(2,1)}, bf16[256,2048]{1,0:T(8,128)(2,1)S(1)}, u32[]{:S(2)}, u32[]{:S(2)}) %collective-permute-start.29) | collective-permute-done | bytes 1048608 | tf_op jit(solution)/shard_map/ppermute | solution.py:42
  1182.3 27.6 %all-to-all-start = ((bf16[8,256,512]{1,2,0:T(8,128)(2,1)}), bf16[8,256,512]{1,2,0:T(8,128)(2,1)}, u32[]{:S(2)}, u32[]{:S(2)}) async-start(bf16[8,256,512]{1,2,0:T(8,128)(2,1)} %constant_dynamic-update-slice_fusion.2), calls=%async_computation.4 | async-start | bytes 4194304 | tf_op jit(solution)/shard_map/all_to_all | solution.py:260
  1220.2 16.5 %all-to-all-done = bf16[8,256,512]{1,2,0:T(8,128)(2,1)} async-done(((bf16[8,256,512]{1,2,0:T(8,128)(2,1)}), bf16[8,256,512]{1,2,0:T(8,128)(2,1)}, u32[]{:S(2)}, u32[]{:S(2)}) %all-to-all-start) | async-done | bytes 2097184 | tf_op jit(solution)/shard_map/all_to_all | solution.py:260
  1250.0 47.1 %newton_schulz.2 = bf16[2048,512]{1,0:T(8,128)(2,1)} custom-call(bf16[2048,512]{1,0:T(8,128)(2,1)} %bitcast.243), custom_call_target="tpu_custom_call" | custom-call | flops 29527900160 | bytes 4194304 | tf_op jit(solution)/shard_map/newton_schulz/pallas_call | solution.py:237
  1306.7 47.1 %newton_schulz.3 = bf16[2048,512]{1,0:T(8,128)(2,1)} custom-call(bf16[2048,512]{1,0:T(8,128)(2,1)} %bitcast.244), custom_call_target="tpu_custom_call" | custom-call | flops 29527900160 | bytes 4194304 | tf_op jit(solution)/shard_map/newton_schulz/pallas_call | solution.py:237
  (476 shorter events, 462.2 us)
Async XLA Ops:
  11.5 106.8 %all-gather.7.cloned.1.call-start = ((), (), s32[]{:S(2)}) async-start(), calls=%async_computation.9 | async-start | bytes 9437184 | tf_op jit(solution)/shard_map/all_gather | solution.py:271
  59.9 115.3 %all-gather.9.cloned.1.call-start = ((), (), s32[]{:S(2)}) async-start(), calls=%async_computation.10 | async-start | bytes 9437184 | tf_op jit(solution)/shard_map/all_gather | solution.py:271
  118.4 207.1 %all-gather.11.cloned.1.call-start = ((), (), s32[]{:S(2)}) async-start(), calls=%async_computation.11 | async-start | bytes 9437184 | tf_op jit(solution)/shard_map/all_gather | solution.py:271
  175.2 996.3 %reduce-scatter.7.cloned.1.call-start = ((), (), s32[]{:S(2)}) async-start(), calls=%async_computation.13 | async-start | bytes 2359296 | tf_op jit(solution)/shard_map/reduce_scatter | solution.py:427
  223.1 71.2 %collective-permute-start.3 = (bf16[1024,512]{1,0:T(8,128)(2,1)}, bf16[1024,512]{1,0:T(8,128)(2,1)S(1)}, u32[]{:S(2)}, u32[]{:S(2)}) collective-permute-start(bf16[1024,512]{1,0:T(8,128)(2,1)} %attend.1), channel_id=1, source_target_pairs={{0,2},{1,3},{2,0},{3,1},{4,6},{5,7},{6,4},{7,5},{8,10},{9,11},{10,... | collective-permute-start | bytes 3145736 | tf_op jit(solution)/shard_map/ppermute | solution.py:42
  225.6 68.9 %collective-permute-start.4 = (bf16[1024,512]{1,0:T(8,128)(2,1)}, bf16[1024,512]{1,0:T(8,128)(2,1)S(1)}, u32[]{:S(2)}, u32[]{:S(2)}) collective-permute-start(bf16[1024,512]{1,0:T(8,128)(2,1)} %attend.1), channel_id=1, source_target_pairs={{0,3},{1,0},{2,1},{3,2},{4,7},{5,4},{6,5},{7,6},{8,11},{9,8},{10,9... | collective-permute-start | bytes 3145736 | tf_op jit(solution)/shard_map/ppermute | solution.py:42
  331.4 90.7 %collective-permute-start.9 = (bf16[256,2048]{1,0:T(8,128)(2,1)S(1)}, bf16[256,2048]{1,0:T(8,128)(2,1)S(1)}, u32[]{:S(2)}, u32[]{:S(2)}) collective-permute-start(bf16[256,2048]{1,0:T(8,128)(2,1)S(1)} %convolution_convert_fusion.12), channel_id=1, source_target_pairs={{0,2},{1,3},{2,0},{3,1},{4,6},{5,7},{6,4},{7,5},{8,10},{9,11},{10,... | collective-permute-start | bytes 3145736 | tf_op jit(solution)/shard_map/ppermute | solution.py:46
  355.5 66.5 %collective-permute-start.10 = (bf16[256,2048]{1,0:T(8,128)(2,1)S(1)}, bf16[256,2048]{1,0:T(8,128)(2,1)S(1)}, u32[]{:S(2)}, u32[]{:S(2)}) collective-permute-start(bf16[256,2048]{1,0:T(8,128)(2,1)S(1)} %convolution_convert_fusion.11), channel_id=1, source_target_pairs={{0,1},{1,2},{2,3},{3,0},{4,5},{5,6},{6,7},{7,4},{8,9},{9,10},{10,1... | collective-permute-start | bytes 3145736 | tf_op jit(solution)/shard_map/ppermute | solution.py:46
  472.8 68.6 %collective-permute-start.15 = (bf16[256,2048]{1,0:T(8,128)(2,1)S(1)}, bf16[256,2048]{1,0:T(8,128)(2,1)S(1)}, u32[]{:S(2)}, u32[]{:S(2)}) collective-permute-start(bf16[256,2048]{1,0:T(8,128)(2,1)S(1)} %fusion.172), channel_id=1, source_target_pairs={{0,3},{1,0},{2,1},{3,2},{4,7},{5,4},{6,5},{7,6},{8,11},{9,8},{10,9... | collective-permute-start | bytes 3145736 | tf_op jit(solution)/shard_map/ppermute | solution.py:42
  508.9 135.5 %collective-permute-start.12 = (bf16[256,2048]{1,0:T(8,128)(2,1)S(1)}, bf16[256,2048]{1,0:T(8,128)(2,1)S(1)}, u32[]{:S(2)}, u32[]{:S(2)}) collective-permute-start(bf16[256,2048]{1,0:T(8,128)(2,1)S(1)} %convolution_convert_fusion.10), channel_id=1, source_target_pairs={{0,3},{1,0},{2,1},{3,2},{4,7},{5,4},{6,5},{7,6},{8,11},{9,8},{10,9... | collective-permute-start | bytes 3145736 | tf_op jit(solution)/shard_map/ppermute | solution.py:46
  533.5 110.9 %collective-permute-start.14 = (bf16[256,2048]{1,0:T(8,128)(2,1)S(1)}, bf16[256,2048]{1,0:T(8,128)(2,1)S(1)}, u32[]{:S(2)}, u32[]{:S(2)}) collective-permute-start(bf16[256,2048]{1,0:T(8,128)(2,1)S(1)} %convolution_convert_fusion.9), channel_id=1, source_target_pairs={{0,2},{1,3},{2,0},{3,1},{4,6},{5,7},{6,4},{7,5},{8,10},{9,11},{10,... | collective-permute-start | bytes 3145736 | tf_op jit(solution)/shard_map/ppermute | solution.py:46
  554.5 113.7 %collective-permute-start.16 = (bf16[256,2048]{1,0:T(8,128)(2,1)S(1)}, bf16[256,2048]{1,0:T(8,128)(2,1)S(1)}, u32[]{:S(2)}, u32[]{:S(2)}) collective-permute-start(bf16[256,2048]{1,0:T(8,128)(2,1)S(1)} %convolution_convert_fusion.8), channel_id=1, source_target_pairs={{0,1},{1,2},{2,3},{3,0},{4,5},{5,6},{6,7},{7,4},{8,9},{9,10},{10,1... | collective-permute-start | bytes 3145736 | tf_op jit(solution)/shard_map/ppermute | solution.py:46
  744.7 72.1 %collective-permute-start.23 = (bf16[512,1024]{1,0:T(8,128)(2,1)S(1)}, bf16[512,1024]{1,0:T(8,128)(2,1)S(1)}, u32[]{:S(2)}, u32[]{:S(2)}) collective-permute-start(bf16[512,1024]{1,0:T(8,128)(2,1)S(1)} %get-tuple-element.140), channel_id=1, source_target_pairs={{4,0},{5,1},{6,2},{7,3},{12,8},{13,9},{14,10},{15,11},{20,16},{21,... | collective-permute-start | bytes 3145736 | tf_op jit(solution)/shard_map/ppermute | solution.py:403
  746.2 70.9 %collective-permute-start.24 = (bf16[512,1024]{1,0:T(8,128)(2,1)S(1)}, bf16[512,1024]{1,0:T(8,128)(2,1)S(1)}, u32[]{:S(2)}, u32[]{:S(2)}) collective-permute-start(bf16[512,1024]{1,0:T(8,128)(2,1)S(1)} %get-tuple-element.139), channel_id=1, source_target_pairs={{0,4},{1,5},{2,6},{3,7},{8,12},{9,13},{10,14},{11,15},{16,20},{17,... | collective-permute-start | bytes 3145736 | tf_op jit(solution)/shard_map/ppermute | solution.py:404
  849.6 323.6 %reduce-scatter.5.cloned.1.call-start = ((), (), s32[]{:S(2)}) async-start(), calls=%async_computation.12 | async-start | bytes 7077888 | tf_op jit(solution)/shard_map/reduce_scatter | solution.py:276
  850.1 362.6 %reduce-scatter.9.cloned.1.call-start = ((), (), s32[]{:S(2)}) async-start(), calls=%async_computation.14 | async-start | bytes 9437184 | tf_op jit(solution)/shard_map/reduce_scatter | solution.py:276
  864.5 376.1 %reduce-scatter.11.cloned.1.call-start = ((), (), s32[]{:S(2)}) async-start(), calls=%async_computation.15 | async-start | bytes 9437184 | tf_op jit(solution)/shard_map/reduce_scatter | solution.py:276
  926.6 131.0 %collective-permute-start.26 = (bf16[256,2048]{1,0:T(8,128)(2,1)S(1)}, bf16[256,2048]{1,0:T(8,128)(2,1)S(1)}, u32[]{:S(2)}, u32[]{:S(2)}) collective-permute-start(bf16[256,2048]{1,0:T(8,128)(2,1)S(1)} %convolution_convert_fusion.5), channel_id=1, source_target_pairs={{0,2},{1,3},{2,0},{3,1},{4,6},{5,7},{6,4},{7,5},{8,10},{9,11},{10,... | collective-permute-start | bytes 3145736 | tf_op jit(solution)/shard_map/ppermute | solution.py:46
  928.6 129.1 %collective-permute-start.27 = (bf16[256,2048]{1,0:T(8,128)(2,1)S(1)}, bf16[256,2048]{1,0:T(8,128)(2,1)S(1)}, u32[]{:S(2)}, u32[]{:S(2)}) collective-permute-start(bf16[256,2048]{1,0:T(8,128)(2,1)S(1)} %convolution_convert_fusion.4), channel_id=1, source_target_pairs={{0,1},{1,2},{2,3},{3,0},{4,5},{5,6},{6,7},{7,4},{8,9},{9,10},{10,1... | collective-permute-start | bytes 3145736 | tf_op jit(solution)/shard_map/ppermute | solution.py:46
  930.0 135.8 %collective-permute-start.20 = (bf16[256,2048]{1,0:T(8,128)(2,1)S(1)}, bf16[256,2048]{1,0:T(8,128)(2,1)S(1)}, u32[]{:S(2)}, u32[]{:S(2)}) collective-permute-start(bf16[256,2048]{1,0:T(8,128)(2,1)S(1)} %copy-done.61), channel_id=1, source_target_pairs={{0,1},{1,2},{2,3},{3,0},{4,5},{5,6},{6,7},{7,4},{8,9},{9,10},{10,1... | collective-permute-start | bytes 3145736 | tf_op jit(solution)/shard_map/ppermute | solution.py:42
  933.3 191.7 %collective-permute-start.21 = (bf16[256,2048]{1,0:T(8,128)(2,1)S(1)}, bf16[256,2048]{1,0:T(8,128)(2,1)S(1)}, u32[]{:S(2)}, u32[]{:S(2)}) collective-permute-start(bf16[256,2048]{1,0:T(8,128)(2,1)S(1)} %copy-done.61), channel_id=1, source_target_pairs={{0,2},{1,3},{2,0},{3,1},{4,6},{5,7},{6,4},{7,5},{8,10},{9,11},{10,... | collective-permute-start | bytes 3145736 | tf_op jit(solution)/shard_map/ppermute | solution.py:42
  945.2 181.0 %collective-permute-start.22 = (bf16[256,2048]{1,0:T(8,128)(2,1)S(1)}, bf16[256,2048]{1,0:T(8,128)(2,1)S(1)}, u32[]{:S(2)}, u32[]{:S(2)}) collective-permute-start(bf16[256,2048]{1,0:T(8,128)(2,1)S(1)} %copy-done.61), channel_id=1, source_target_pairs={{0,3},{1,0},{2,1},{3,2},{4,7},{5,4},{6,5},{7,6},{8,11},{9,8},{10,9... | collective-permute-start | bytes 3145736 | tf_op jit(solution)/shard_map/ppermute | solution.py:42
  1066.9 103.1 %collective-permute-start.29 = (bf16[256,2048]{1,0:T(8,128)(2,1)}, bf16[256,2048]{1,0:T(8,128)(2,1)S(1)}, u32[]{:S(2)}, u32[]{:S(2)}) collective-permute-start(bf16[256,2048]{1,0:T(8,128)(2,1)} %get-tuple-element.214), channel_id=1, source_target_pairs={{0,2},{1,3},{2,0},{3,1},{4,6},{5,7},{6,4},{7,5},{8,10},{9,11},{10,... | collective-permute-start | bytes 3145736 | tf_op jit(solution)/shard_map/ppermute | solution.py:42
  1127.2 82.8 %collective-permute-start.30 = (bf16[256,2048]{1,0:T(8,128)(2,1)}, bf16[256,2048]{1,0:T(8,128)(2,1)}, u32[]{:S(2)}, u32[]{:S(2)}) collective-permute-start(bf16[256,2048]{1,0:T(8,128)(2,1)} %get-tuple-element.214), channel_id=1, source_target_pairs={{0,3},{1,0},{2,1},{3,2},{4,7},{5,4},{6,5},{7,6},{8,11},{9,8},{10,9... | collective-permute-start | bytes 3145736 | tf_op jit(solution)/shard_map/ppermute | solution.py:42
  (136 other events, 2117.6 us)
Sparse Core Ops, SparseCore 0:
  11.6 48.2 all-gather.4
  62.3 55.9 all-gather.6
  120.8 54.3 all-gather.8
  177.5 55.9 all-gather.10
  849.7 44.6 reduce-scatter.6
  897.9 61.7 reduce-scatter.4
  963.2 71.2 reduce-scatter.8
  1038.3 71.2 reduce-scatter.10

commit v2 on v1

v2 whole, which is shorter than its diff:
```python
import functools
import math

import jax
import jax.numpy as jnp
from jax import lax
from jax.experimental import pallas as pl
from jax.experimental.layout import Layout, with_layout_constraint
from jax.experimental.pallas import tpu as pltpu
from jax.sharding import PartitionSpec as P

HEAD_DIM = 128
REACH = 512
BW = 512
NS_STEPS = 5
QUERY_ROWS = 256

NS_COEFFS = (3.4445, -4.775, 2.0315)
LN_EPSILON = 1e-12
BETA = 0.5
MATRIX_RATE = 0.5
VECTOR_RATE = 0.3
MASKED = -1e30
WEIGHT_AXES = ("shard", "ctx")
BF16 = jnp.bfloat16
F32 = jnp.float32


def along(value, axis, pairs):
    return value, functools.partial(lax.ppermute, axis_name=axis, perm=pairs)


def upward(first, last):
    return [(i, i + 1) for i in range(first, last)]


def downward(first, last):
    return [(i, i - 1) for i in range(first, last)]


class Gather:
    def __init__(self, block, axis):
        self.count, self.axis = lax.axis_size(axis), axis
        self.block, self.ups, self.downs = block, [], []

    def sends(self):
        step = len(self.ups) + 1
        up, down = (self.ups[-1], self.downs[-1]) if self.ups else (self.block, self.block)
        return [
            along(up, self.axis, upward(step - 1, self.count - 1)),
            along(down, self.axis, downward(1, self.count - step + 1)),
        ]

    def take(self, got):
        self.ups.append(got[0])
        self.downs.append(got[1])

    def slot(self, r):
        return self.ups[r - 1] + self.downs[self.count - r - 1] if r else self.block

    def slots(self):
        return [self.slot(r) for r in range(self.count)]

    def terms(self):
        pairs = [[self.ups[r - 1], self.downs[self.count - r - 1]] for r in range(1, self.count)]
        return [[self.block], *pairs]


class Scatter:
    def __init__(self, parts, axis):
        self.count, self.axis = lax.axis_size(axis), axis
        self.parts, self.step, self.got = parts, 0, None

    def sends(self):
        self.step += 1
        step, count = self.step, self.count
        terms = [self.parts[step], self.parts[count - step]]
        if self.got:
            terms = [
                term.astype(F32) + got.astype(F32) for term, got in zip(terms, self.got)
            ]
        return [
            along(terms[0].astype(BF16), self.axis, upward(0, step)),
            along(terms[1].astype(BF16), self.axis, downward(count - step, count)),
        ]

    def take(self, got):
        self.got = got

    def total(self):
        return self.parts[0].astype(F32) + (self.got[0].astype(F32) + self.got[1].astype(F32))


class Exchange:
    def __init__(self, blocks, axis):
        self.blocks, self.axis = blocks, axis

    def sends(self):
        count = len(self.blocks)
        return [
            along(self.blocks[r], self.axis, [(i, (i + r) % count) for i in range(count)])
            for r in range(1, count)
        ]

    def take(self, got):
        self.slots = [self.blocks[0], *got]


class Once:
    def __init__(self, *sends):
        self.all = list(sends)

    def sends(self):
        return self.all

    def take(self, got):
        self.got = got


class Total:
    def __init__(self, value, axes):
        self.value = value
        self.rounds = [
            (axis, 1 << k) for axis in axes for k in range(lax.axis_size(axis).bit_length() - 1)
        ]

    def sends(self):
        if not self.rounds:
            return []
        axis, by = self.rounds.pop(0)
        return [along(self.value, axis, [(i, i ^ by) for i in range(lax.axis_size(axis))])]

    def take(self, got):
        for other in got:
            self.value = self.value + other


class Halving:
    def __init__(self, value, axes):
        bits = [
            (axis, k)
            for axis in axes
            for k in reversed(range(lax.axis_size(axis).bit_length() - 1))
        ]
        blocks = math.prod(lax.axis_size(axis) for axis in axes)
        rows, width = value.shape[0] // blocks, value.shape[1] // 2
        first = [bit for bit in bits if bit[0] != axes[0]]
        last = [bit for bit in bits if bit[0] == axes[0]]
        self.rounds = len(bits)
        self.groups = []
        for g, order in enumerate((first + last, first + last[::-1])):
            columns = value[:, g * width : (g + 1) * width]
            self.groups.append([columns.reshape((2,) * len(bits) + (rows, width)), list(bits), order])

    def sends(self):
        sent = []
        self.kept = []
        for value, left, order in self.groups:
            axis, k = bit = order.pop(0)
            dim = left.index(bit)
            left.pop(dim)
            mine = (lax.axis_index(axis) >> k) & 1
            pairs = [(i, i ^ (1 << k)) for i in range(lax.axis_size(axis))]
            self.kept.append(lax.dynamic_index_in_dim(value, mine, dim, keepdims=False))
            away = lax.dynamic_index_in_dim(value, 1 - mine, dim, keepdims=False)
            sent.append(along(away, axis, pairs))
        self.rounds -= 1
        return sent

    def take(self, got):
        for group, kept, other in zip(self.groups, self.kept, got):
            group[0] = (kept.astype(F32) + other.astype(F32)).astype(BF16)

    def total(self):
        return jnp.concatenate([group[0] for group in self.groups], axis=1)


def step(movers, work=None, *operands):
    sends = [mover.sends() for mover in movers]
    values = [[value for value, _ in group] for group in sends]
    values, operands = lax.optimization_barrier((values, operands))
    got = [
        [send(value) for value, (_, send) in zip(vals, group)] for vals, group in zip(values, sends)
    ]
    done = work(*operands) if work else ()
    got, done = lax.optimization_barrier((got, done))
    for mover, arrived in zip(movers, got):
        mover.take(arrived)
    return done


def slot_order(count):
    order = []
    for hop in range(1, count):
        order += [r for r in (hop, count - hop) if r not in order]
    return order + [0]


def after(value, *others):
    return lax.optimization_barrier((value, *others))[0]


def row_major(value):
    return with_layout_constraint(value, Layout(major_to_minor=tuple(range(value.ndim))))


def dot(left, right):
    return jnp.dot(left, right, preferred_element_type=F32)


def dot_nt(left, right):
    return lax.dot_general(left, right, (((1,), (1,)), ((), ())), preferred_element_type=F32)


def dot_tn(left, right):
    return lax.dot_general(left, right, (((0,), (0,)), ((), ())), preferred_element_type=F32)


def normalize(hidden):
    centred = hidden - jnp.mean(hidden, axis=-1, keepdims=True)
    variance = jnp.mean(centred * centred, axis=-1, keepdims=True)
    scale = lax.rsqrt(variance + LN_EPSILON)
    return centred * scale, scale


def norm_backward(grad, unit, scale, gain):
    scaled = grad * gain
    inner = jnp.mean(scaled * unit, axis=-1, keepdims=True)
    dhidden = scale * (scaled - jnp.mean(scaled, axis=-1, keepdims=True) - unit * inner)
    return dhidden, jnp.sum(grad * unit, axis=0), jnp.sum(grad, axis=0)


def gelu_tanh(values):
    return jax.nn.gelu(values, approximate=True)


def window_probs(q, keys, low_ref, high_ref, start):
    scores = dot_nt(keys, q) * (HEAD_DIM**-0.5)
    at = start + lax.broadcasted_iota(jnp.int32, scores.shape, 0)
    scores = jnp.where((at >= low_ref[...]) & (at <= high_ref[...]), scores, MASKED)
    expo = jnp.exp(scores - jnp.max(scores, axis=0, keepdims=True))
    return expo * (1.0 / jnp.sum(expo, axis=0, keepdims=True))


def attend_kernel(low_ref, high_ref, q_ref, k_ref, v_ref, o_ref):
    rows = q_ref.shape[0]
    span = rows + 2 * REACH
    start = pl.multiple_of(pl.program_id(1) * rows, rows)
    probs = window_probs(q_ref[...], k_ref[pl.ds(start, span), :], low_ref, high_ref, start)
    o_ref[...] = dot_tn(probs.astype(BF16), v_ref[pl.ds(start, span), :]).astype(BF16)


def attend_back_kernel(low_ref, high_ref, q_ref, k_ref, v_ref, g_ref, dq_ref, dk_ref, dv_ref):
    rows = q_ref.shape[0]
    span = rows + 2 * REACH
    start = pl.multiple_of(pl.program_id(1) * rows, rows)
    window = pl.ds(start, span)

    @pl.when(pl.program_id(1) == 0)
    def _():
        dk_ref[...] = jnp.zeros_like(dk_ref)
        dv_ref[...] = jnp.zeros_like(dv_ref)

    q, g, keys = q_ref[...], g_ref[...], k_ref[window, :]
    probs = window_probs(q, keys, low_ref, high_ref, start)
    dprobs = dot_nt(v_ref[window, :], g)
    offset = jnp.sum(dprobs * probs, axis=0, keepdims=True)
    dscores = (probs * (dprobs - offset) * (HEAD_DIM**-0.5)).astype(BF16)
    dv_ref[window, :] += dot(probs.astype(BF16), g)
    dk_ref[window, :] += dot(dscores, q)
    dq_ref[...] = dot_tn(dscores, keys).astype(BF16)


def attention_specs(rows, padded, heads):
    bounds = pl.BlockSpec((1, rows), lambda h, b: (0, b))
    queries = pl.BlockSpec((rows, HEAD_DIM), lambda h, b: (b, h))
    keys = pl.BlockSpec((padded, HEAD_DIM), lambda h, b: (0, h))
    values = pl.BlockSpec((padded, HEAD_DIM), lambda h, b: (0, h + heads))
    return bounds, queries, keys, values


def attend(low, high, qkv, padded_kv, heads):
    length, padded = qkv.shape[0], padded_kv.shape[0]
    rows = min(QUERY_ROWS, length)
    bounds, q_spec, k_spec, v_spec = attention_specs(rows, padded, heads)
    pairs = heads * length * (rows + 2 * REACH)
    return pl.pallas_call(
        attend_kernel,
        grid=(heads, length // rows),
        in_specs=[bounds, bounds, q_spec, k_spec, v_spec],
        out_specs=q_spec,
        out_shape=jax.ShapeDtypeStruct((length, heads * HEAD_DIM), BF16),
        cost_estimate=pl.CostEstimate(
            flops=16 * pairs * HEAD_DIM, transcendentals=pairs, bytes_accessed=8 << 20
        ),
        name="attend",
    )(low, high, qkv, padded_kv, padded_kv)


def attend_back(low, high, qkv, padded_kv, grads, heads):
    length, padded = qkv.shape[0], padded_kv.shape[0]
    rows = min(QUERY_ROWS, length)
    bounds, q_spec, k_spec, v_spec = attention_specs(rows, padded, heads)
    pairs = heads * length * (rows + 2 * REACH)
    total = jax.ShapeDtypeStruct((padded, heads * HEAD_DIM), F32)
    return pl.pallas_call(
        attend_back_kernel,
        grid=(heads, length // rows),
        in_specs=[bounds, bounds, q_spec, k_spec, v_spec, q_spec],
        out_specs=(q_spec, k_spec, k_spec),
        out_shape=(jax.ShapeDtypeStruct((length, heads * HEAD_DIM), BF16), total, total),
        cost_estimate=pl.CostEstimate(
            flops=32 * pairs * HEAD_DIM, transcendentals=pairs, bytes_accessed=20 << 20
        ),
        name="attend_back",
    )(low, high, qkv, padded_kv, padded_kv, grads)


def place_kernel(sizes, me_ref, *refs):
    at = 0
    for r, size in enumerate(sizes):
        terms = refs[at : at + size]
        at += size

        @pl.when(pl.program_id(0) == r)
        def _(terms=terms):
            value = terms[0][...]
            for term in terms[1:]:
                value = value + term[...]
            refs[-1][...] = value.astype(refs[-1].dtype)


def placed(slots, dtype, me):
    count = len(slots)
    share, width = slots[0][0].shape
    flat = [term for slot in slots for term in slot]
    whole = pl.BlockSpec((share, width), lambda r, me_ref: (0, 0))
    return pl.pallas_call(
        functools.partial(place_kernel, [len(slot) for slot in slots]),
        grid_spec=pltpu.PrefetchScalarGridSpec(
            num_scalar_prefetch=1,
            grid=(count,),
            in_specs=[whole] * len(flat),
            out_specs=pl.BlockSpec(
                (share, width), lambda r, me_ref: (lax.rem(me_ref[0] - r + count, count), 0)
            ),
        ),
        out_shape=jax.ShapeDtypeStruct((count * share, width), dtype),
        cost_estimate=pl.CostEstimate(
            flops=0, transcendentals=0, bytes_accessed=6 * count * share * width
        ),
        name="place",
    )(me.reshape(1), *flat)


def halves(value):
    top = value.astype(BF16)
    return top, (value - top.astype(F32)).astype(BF16)


def newton_schulz_kernel(steps, in_ref, out_ref, top, rest, iterate=None):
    opening = iterate is None
    iterate = out_ref if opening else iterate
    depth = top.shape[1]
    chunk = min(1024, depth)
    chunks = depth // chunk

    def columns(c):
        return pl.ds(pl.multiple_of(c * chunk, chunk), chunk)

    def load(c, total):
        part = in_ref[columns(c), :].astype(F32)
        iterate[:, columns(c)] = part.T
        return total + jnp.sum(part * part, axis=(0, 1), keepdims=True)

    if opening:
        norm = jnp.sqrt(lax.fori_loop(0, chunks, load, jnp.zeros((1, 1), F32)))
        inverse = 1.0 / (norm + 1e-07)

    def split(c, carry):
        value = iterate[:, columns(c)] * inverse if opening else in_ref[:, columns(c)]
        iterate[:, columns(c)] = value
        top[:, columns(c)], rest[:, columns(c)] = halves(value)
        return carry

    lax.fori_loop(0, chunks, split, 0)

    def step(index, carry):
        cross = dot_nt(rest[...], top[...])
        gram = dot_nt(top[...], top[...]) + (cross + cross.T)
        gram_top, gram_rest = halves(gram)
        cross = dot(gram_top, gram_rest)
        square = dot(gram_top, gram_top) + (cross + cross.T)
        poly_top, poly_rest = halves(NS_COEFFS[1] * gram + NS_COEFFS[2] * square)

        def update(c, carry):
            here = columns(c)
            change = dot(poly_top, top[:, here]) + dot(poly_rest, top[:, here])
            value = NS_COEFFS[0] * iterate[:, here] + (change + dot(poly_top, rest[:, here]))
            iterate[:, here] = value
            top[:, here], rest[:, here] = halves(value)
            return carry

        return lax.fori_loop(0, chunks, update, carry)

    lax.fori_loop(0, steps, step, 0)

    def store(c, carry):
        out_ref[columns(c), :] = iterate[:, columns(c)].T.astype(BF16)
        return carry

    if not opening:
        lax.fori_loop(0, chunks, store, 0)


def newton_schulz_part(steps, value, out, depth, width, scratch):
    return pl.pallas_call(
        functools.partial(newton_schulz_kernel, steps),
        out_shape=out,
        in_specs=[pl.BlockSpec(memory_space=pltpu.VMEM)],
        out_specs=pl.BlockSpec(memory_space=pltpu.VMEM),
        scratch_shapes=[pltpu.VMEM((width, depth), BF16), pltpu.VMEM((width, depth), BF16), *scratch],
        cost_estimate=pl.CostEstimate(
            flops=2 * steps * width * width * (5 * depth + 2 * width),
            transcendentals=0,
            bytes_accessed=6 * depth * width,
        ),
        name="newton_schulz",
    )(value)


def orthogonal_start(owned):
    depth, width = owned.shape[0] * owned.shape[1], owned.shape[2]
    out = jax.ShapeDtypeStruct((width, depth), F32)
    return newton_schulz_part(NS_STEPS // 2, owned.reshape(depth, width), out, depth, width, [])


def orthogonal_end(iterate, group):
    width, depth = iterate.shape
    out = jax.ShapeDtypeStruct((depth, width), BF16)
    scratch = [pltpu.VMEM((width, depth), F32)]
    done = newton_schulz_part(NS_STEPS - NS_STEPS // 2, iterate, out, depth, width, scratch)
    return done.reshape(group, depth // group, width)


def to_owners(blocks):
    copies = lax.axis_size("shard") * lax.axis_size("ctx") // len(blocks)
    return jnp.stack([block.astype(BF16) for block in blocks for _ in range(copies)])


def swapped(value):
    return value, functools.partial(
        lax.all_to_all, axis_name=WEIGHT_AXES, split_axis=0, concat_axis=0, tiled=True
    )


def from_owners(back, count):
    copies = back.shape[0] // count
    return [back[b * copies].astype(F32) for b in range(count)]


def column_blocks(value):
    return [value[:, at : at + BW] for at in range(0, value.shape[1], BW)]


def gather_rows(value):
    return lax.all_gather(value, WEIGHT_AXES, axis=0, tiled=True)


def scatter_rows(value):
    return lax.psum_scatter(value, WEIGHT_AXES, scatter_dimension=0, tiled=True)


def blend(old, grad):
    return BETA * old + (1.0 - BETA) * grad


def body(
    hidden_in,
    doc_span,
    cotangent,
    w_query,
    w_key,
    w_value,
    w_out,
    w_inner,
    w_outer,
    norm_gains,
    norm_biases,
    mom_query,
    mom_key,
    mom_value,
    mom_out,
    mom_inner,
    mom_outer,
    gain_moment,
    bias_moment,
):
    tp = lax.axis_size("tp")
    me = lax.axis_index("tp")
    hidden = hidden_in[0]
    length, width = hidden.shape
    share = length // tp
    local = w_query.shape[1]
    heads = local // HEAD_DIM

    def slice_of(value, r):
        return lax.dynamic_slice_in_dim(value, lax.rem(me - r + tp, tp) * share, share, 0)

    full_qkv = gather_rows(jnp.concatenate([w_query, w_key, w_value], axis=1).astype(BF16))
    w_out_t = Gather(w_out.T.astype(BF16), "tp")
    for _ in range(tp - 1):
        step([w_out_t])
    full_out_t = gather_rows(jnp.concatenate(w_out_t.slots(), axis=1))
    full_inner = gather_rows(w_inner.astype(BF16))
    full_outer_t = gather_rows(w_outer.T.astype(BF16))

    qkv = dot(hidden, full_qkv).astype(BF16)
    own_kv = qkv[:, local:]
    ctx = lax.axis_size("ctx")
    edges = Once(
        along(own_kv[length - REACH :], "ctx", upward(0, ctx - 1)),
        along(own_kv[:REACH], "ctx", downward(1, ctx)),
    )
    step([edges])
    padded_kv = jnp.concatenate([edges.got[0], own_kv, edges.got[1]], axis=0)

    position = jnp.arange(length, dtype=jnp.int32)
    anchor = lax.axis_index("ctx") * length - REACH
    low = jnp.maximum(doc_span[0] - anchor, position[None])
    high = jnp.minimum(doc_span[1] - anchor, position[None] + 2 * REACH)
    attended = attend(low, high, qkv, padded_kv, heads)

    all_heads = Gather(attended, "tp")
    mom_outer_t, mom_out_t = step([all_heads], lambda a, b: (a.T, b.T), mom_outer, mom_out)
    for _ in range(tp - 2):
        step([all_heads])
    head_slots = all_heads.slots()

    order = slot_order(tp)
    first, rest = order[:2], order[2:]
    normed_slots, pre_slots, act_slots, parts = ([None] * tp for _ in range(4))
    own = []

    def forward(slots, *head_slots):
        made = []
        for r in slots:
            attended_r = jnp.concatenate([slice_of(slot, r) for slot in head_slots], axis=1)
            branch = dot_nt(attended_r, full_out_t)
            unit, scale = normalize(slice_of(hidden, r).astype(F32) + branch)
            normed = unit * norm_gains[0] + norm_biases[0]
            normed_low = normed.astype(BF16)
            pre = dot(normed_low, full_inner)
            act = gelu_tanh(pre).astype(BF16)
            part = dot_nt(act, full_outer_t)
            made.append((normed_low, pre, act, part if r == 0 else part.astype(BF16)))
            if r == 0:
                made.append((unit, scale, normed))
        return made

    def keep(slots, made):
        for r, values in zip(slots, made):
            normed_slots[r], pre_slots[r], act_slots[r], parts[r] = values

    keep(first, forward(first, *head_slots))
    ffn_sum = Scatter(parts, "tp")
    made = step([ffn_sum], functools.partial(forward, rest), *head_slots)
    unit_one, scale_one, own_normed = made[-1]
    keep(rest, made)

    def slopes_of(*pres):
        return [jax.vjp(gelu_tanh, pre)[1](jnp.ones_like(pre))[0] for pre in pres]

    slopes = [None] * tp
    half = tp // 2
    slopes[:half] = step([ffn_sum], slopes_of, *pre_slots[:half])
    slopes[half:] = step([ffn_sum], slopes_of, *pre_slots[half:])
    for _ in range(tp - 4):
        step([ffn_sum])

    unit_two, scale_two = normalize(own_normed + ffn_sum.total())
    own_out = (unit_two * norm_gains[1] + norm_biases[1]).astype(BF16)
    seed = slice_of(cotangent[0], 0).astype(F32)
    grad_two, gain_two, shift_two = norm_backward(seed, unit_two, scale_two, norm_gains[1])
    dffn_all = Gather(grad_two.astype(BF16), "tp")
    dpre_slots, parts = [None] * tp, [None] * tp

    def backward(*pairs):
        made = []
        for dffn, slope in pairs:
            dpre = (dot(dffn, full_outer_t) * slope).astype(BF16)
            made.append((dpre, dot_nt(dpre, full_inner).astype(BF16)))
        return made

    def keep_back(slots, made):
        for r, values in zip(slots, made):
            dpre_slots[r], parts[r] = values

    step([dffn_all])
    keep_back([0], step([dffn_all], backward, (dffn_all.slot(0), slopes[0])))
    middle = [r for r in rest if r]
    ready = [(dffn_all.slot(r), slopes[r]) for r in middle] if tp == 4 else []
    made = step([dffn_all], backward, *ready)
    for _ in range(tp - 4):
        step([dffn_all])
    if not ready:
        made = backward(*[(dffn_all.slot(r), slopes[r]) for r in middle])
    keep_back(middle, made)
    dffn_slots = dffn_all.slots()
    out_all = Gather(own_out, "tp")
    keep_back(first, step([out_all], backward, *[(dffn_slots[r], slopes[r]) for r in first]))

    dnormed_sum = Scatter(parts, "tp")

    def weight_grad(lefts, rights):
        return dot_tn(jnp.concatenate(lefts, axis=0), jnp.concatenate(rights, axis=0)).astype(BF16)

    grad_outer_t = step([out_all, dnormed_sum], weight_grad, dffn_slots, act_slots)
    grad_outer_t = scatter_rows(grad_outer_t)
    grad_inner = step([out_all, dnormed_sum], weight_grad, normed_slots, dpre_slots)
    grad_inner = scatter_rows(grad_inner)
    layer_out = step([dnormed_sum], lambda *slots: placed(slots, BF16, me), *out_all.terms())[None]
    for _ in range(tp - 4):
        step([dnormed_sum])
    dnormed = grad_two + dnormed_sum.total()

    grad_one, gain_one, shift_one = norm_backward(dnormed, unit_one, scale_one, norm_gains[0])
    dbranch_low = grad_one.astype(BF16)
    dattended_all = dot(dbranch_low, full_out_t).astype(BF16)
    blocks = [dattended_all[:, (-r % tp) * local : (-r % tp + 1) * local] for r in range(tp)]
    dattended = Exchange(blocks, "tp")
    totals = Total(
        jnp.stack([gain_one, gain_two, shift_one, shift_two]), ("ctx", "shard", "tp")
    )
    step([dattended])
    part = width // tp
    dbranch = Exchange(
        [
            lax.dynamic_slice_in_dim(dbranch_low, lax.rem(me + r, tp) * part, part, 1)
            for r in range(tp)
        ],
        "tp",
    )

    def attention_back(*slots):
        return attend_back(low, high, qkv, padded_kv, placed([[slot] for slot in slots], BF16, me), heads)

    dq_low, key_grad, value_grad = step([dbranch, totals], attention_back, *dattended.slots)

    def kv_rows(start, count):
        rows = slice(start, start + count)
        return jnp.concatenate([key_grad[rows], value_grad[rows]], axis=1)

    edges = Once(
        along(kv_rows(0, REACH).astype(BF16), "ctx", downward(1, ctx)),
        along(kv_rows(length + REACH, REACH).astype(BF16), "ctx", upward(0, ctx - 1)),
    )
    rows = w_query.shape[0]
    group = width // rows

    def out_pieces(dbranch_slots, head_slots):
        columns = placed([[slot] for slot in dbranch_slots], BF16, me)
        sums = [dot_tn(columns, slot).astype(BF16).reshape(-1, rows, local) for slot in head_slots]
        return row_major(jnp.stack(sums, axis=1).reshape(group * rows, local))

    step([edges])
    from_above, from_below = (edge.astype(F32) for edge in edges.got)
    beyond = length - REACH
    added = jnp.pad(from_above, ((beyond, 0), (0, 0))) + jnp.pad(from_below, ((0, beyond), (0, 0)))
    dqkv = jnp.concatenate([dq_low, (kv_rows(REACH, length) + added).astype(BF16)], axis=1)
    grad_qkv = row_major(dot_tn(hidden, dqkv).astype(BF16))
    qkv_sum = Halving(grad_qkv, WEIGHT_AXES)

    parts = [None] * tp

    def input_terms(slots, dqkv):
        rows = jnp.concatenate([slice_of(dqkv, r) for r in slots], axis=0)
        sums = dot_nt(rows, full_qkv).astype(BF16)
        return [sums[n * share : (n + 1) * share] for n in range(len(slots))]

    for r, value in zip(first, step([qkv_sum], functools.partial(input_terms, first), dqkv)):
        parts[r] = value
    input_sum = Scatter(parts, "tp")

    def between(dqkv, dbranch_slots, head_slots, grad_inner, grad_outer_t):
        pieces = out_pieces(dbranch_slots, head_slots)
        moments = blend(mom_inner, grad_inner), blend(mom_outer_t, grad_outer_t)
        blocks = to_owners(sum(map(column_blocks, moments), []))
        return input_terms(rest, dqkv), moments, blocks, pieces

    terms, (moment_inner, moment_outer_t), blocks, pieces = step(
        [input_sum, qkv_sum, totals],
        between,
        dqkv,
        dbranch.slots,
        head_slots,
        grad_inner,
        grad_outer_t,
    )
    grad_inner, grad_outer_t = grad_inner.astype(F32), grad_outer_t.astype(F32)
    for r, value in zip(rest, terms):
        parts[r] = value
    grad_piece = scatter_rows(pieces)
    owners = Once(swapped(blocks))
    step([input_sum, qkv_sum, totals, owners])
    homes = [
        (p * tp + t, (t * (group // tp) + p // tp) * tp + (t - p % tp) % tp)
        for p in range(group)
        for t in range(tp)
    ]
    piece = Once(along(grad_piece, (*WEIGHT_AXES, "tp"), homes))
    iterate = step([input_sum, totals, piece], orthogonal_start, owners.got[0])
    for _ in range(tp - 4):
        step([input_sum])
    while qkv_sum.rounds:
        step([qkv_sum])
    own_input = Gather((grad_one + input_sum.total()).astype(BF16), "tp")

    grad_query, grad_key, grad_value = jnp.split(qkv_sum.total().astype(F32), 3, axis=1)
    grad_out_t = row_major(piece.got[0]).astype(F32)
    moment_query = blend(mom_query, grad_query)
    moment_key = blend(mom_key, grad_key)
    moment_value = blend(mom_value, grad_value)
    moment_out_t = blend(mom_out_t, grad_out_t)
    moments = moment_query, moment_key, moment_value, moment_out_t
    shard = lax.axis_size("shard")
    at_shard = lax.axis_index("shard")
    blocks = [row_major(m.astype(BF16)) for m in sum(map(column_blocks, moments), [])]
    blocks = row_major(jnp.stack(blocks))
    blocks = blocks.reshape(shard, -1, *blocks.shape[1:])

    def turned(value, r):
        return lax.dynamic_index_in_dim(value, lax.rem(at_shard + r, shard), 0, keepdims=False)

    owners = Exchange([turned(blocks, r) for r in range(shard)], "shard")
    finish = functools.partial(orthogonal_end, group=group)
    done = step([own_input, owners, totals], finish, iterate)
    spread = [owners.slots]
    for by in range(1, ctx):
        pairs = [(i, (i + by) % ctx) for i in range(ctx)]
        peers = Once(*[along(slot, "ctx", pairs) for slot in owners.slots])
        step([peers])
        spread.append(peers.got)
    at_ctx = lax.axis_index("ctx")
    owned = jnp.zeros((shard, ctx, *blocks.shape[2:]), BF16)
    for by, slots in enumerate(spread):
        for r, slot in enumerate(slots):
            where = lax.rem(at_shard - r + shard, shard), lax.rem(at_ctx - by + ctx, ctx)
            owned = lax.dynamic_update_slice(owned, slot[None], (*where, 0, 0))

    def update_ffn(back):
        ortho = from_owners(back, 2 * moment_inner.shape[1] // BW)
        half = len(ortho) // 2
        return (
            w_inner - MATRIX_RATE * jnp.concatenate(ortho[:half], axis=1),
            w_outer - MATRIX_RATE * jnp.concatenate(ortho[half:], axis=1).T,
        )

    ortho = Once(swapped(done))
    iterate = step([own_input, ortho], orthogonal_start, owned.reshape(group, rows, BW))
    done = step([own_input], finish, iterate).reshape(shard, ctx, rows, BW)
    for _ in range(tp - 4):
        step([own_input])
    done = lax.dynamic_index_in_dim(done, at_ctx, 1, keepdims=False)
    attn = Exchange([turned(done, r) for r in range(shard)], "shard")

    def closing(back, *slots):
        return update_ffn(back), placed(slots, F32, me)

    (new_inner, new_outer), input_grad = step([attn], closing, ortho.got[0], *own_input.terms())
    input_grad = input_grad[None]
    ortho = jnp.stack(attn.slots)
    ortho = [
        lax.dynamic_index_in_dim(ortho, lax.rem(at_shard - b + shard, shard), 0, keepdims=False)
        for b in range(shard)
    ]
    ortho = [block.astype(F32) for block in ortho]
    while totals.rounds:
        step([totals])
    gain_grad, bias_grad = totals.value[:2], totals.value[2:]
    new_query = w_query - MATRIX_RATE * ortho[0]
    new_key = w_key - MATRIX_RATE * ortho[1]
    new_value = w_value - MATRIX_RATE * ortho[2]
    new_out = w_out - MATRIX_RATE * ortho[3].T

    tokens_all = length * lax.axis_size("shard") * ctx
    gain_moment_new = blend(gain_moment, gain_grad)
    bias_moment_new = blend(bias_moment, bias_grad)
    new_gains = norm_gains - VECTOR_RATE * gain_moment_new / math.sqrt(tokens_all)
    new_biases = norm_biases - VECTOR_RATE * bias_moment_new / math.sqrt(tokens_all)
    return (
        layer_out,
        input_grad,
        grad_query,
        grad_key,
        grad_value,
        grad_out_t.T,
        grad_inner,
        grad_outer_t.T,
        gain_grad,
        bias_grad,
        moment_query,
        moment_key,
        moment_value,
        moment_out_t.T,
        moment_inner,
        moment_outer_t.T,
        gain_moment_new,
        bias_moment_new,
        new_query,
        new_key,
        new_value,
        new_out,
        new_inner,
        new_outer,
        new_gains,
        new_biases,
    )


def solution(mesh):
    tokens = P("shard", "ctx", None)
    by_rows = P(WEIGHT_AXES, "tp")
    by_columns = P("tp", WEIGHT_AXES)
    matrices = (by_rows, by_rows, by_rows, by_columns, by_rows, by_columns)
    return jax.shard_map(
        body,
        mesh=mesh,
        in_specs=(tokens, P(None, "shard", "ctx"), tokens, *matrices, P(), P(), *matrices, P(), P()),
        out_specs=(tokens, tokens, *matrices, P(), P(), *matrices, P(), P(), *matrices, P(), P()),
        check_vma=False,
    )
```

time: 1410 us -> 956 us (0.68)
  waiting for transfers between devices: 584 us -> 266 us
  starting transfers between devices: 268 us -> 178 us
  other arithmetic: 124 us -> 87 us
  local copies, waits for them, and re-layouts: 94.5 us -> 78.2 us
  Pallas kernels: 149 us -> 165 us
    ppermute x40 -> x80, waiting for transfers between devices: 424 us -> 247 us  [step(): send(value)]
    all_gather x4, waiting for transfers between devices: 136 us -> 15.1 us  [gather_rows(): return lax.all_gather(value, WEIGHT_AXES, axis=0, tiled=True)]
    concatenate x5, other arithmetic: 66.2 us -> 4.91 us  [the longest x1 3.39 us: body(): padded_kv = jnp.concatenate([edges.got[0], own_kv, edges.got[1]], axis=0)]
    ppermute x40 -> x80, starting transfers between devices: 227 us -> 170 us  [step(): send(value)]
    all_to_all x4 -> x2, starting transfers between devices: 40.1 us -> 7.95 us  [step(): send(value)]
    convert_element_type x7 -> x25, other arithmetic: 8.93 us -> 36.7 us  [the longest x6 10.6 us: sends(): terms[1].astype(BF16)]
    all_to_all x4 -> x2, waiting for transfers between devices: 23.2 us -> 0.01 us  [step(): send(value)]
    reshape x4 -> x0, local copies, waits for them, and re-layouts: 15.9 us -> none  [the longest x2 7.57 us: body(): dot_tn(dbranch, attended_all).astype(BF16)]
  transfers between devices with their start and end apart: 52 -> 89, of which waited for: 27 -> 37; matrix products, arithmetic and copies ran while one was open for 22% -> 25% of each run, Pallas kernels for 8% -> 17%
where the time goes in v2:
time: 956 us; the launch traced here: 947 us
  waiting for transfers between devices  266 us (28%)
  starting transfers between devices  178 us (19%)
  Pallas kernels  165 us (17%)
  matrix products  156 us (16%)
  other arithmetic  87 us (9%)
  local copies, waits for them, and re-layouts  78.2 us (8%)
  between operations  17.2 us (2%)
    ppermute x80, waiting for transfers between devices, step(): send(value)  247 us
    ppermute x80, starting transfers between devices, step(): send(value)  170 us
    pallas_call x4, Pallas kernels, newton_schulz_part(): pl.pallas_call(functools.partial(newton_schulz_kernel, steps), out_shape=...  91.1 us
    dot_general x14, matrix products, dot_nt(): lax.dot_general(left, right, (((1,), (1,)), ((), ())), preferred_element_...  62.8 us
    dot_general x10, matrix products, dot(): return jnp.dot(left, right, preferred_element_type=F32)  57.5 us
    unnamed x277, local copies, waits for them, and re-layouts  46.2 us
    dot_general x7, matrix products, dot_tn(): lax.dot_general(left, right, (((0,), (0,)), ((), ())), preferred_element_...  36.1 us
    pallas_call x1, Pallas kernels, attend_back(): pl.pallas_call(attend_back_kernel, grid=(heads, length // rows), in_specs...  32.1 us
  transfers between devices with their start and end apart: 89, of which 37 were waited for; matrix products, arithmetic and copies ran while one was open for 25% of the time, Pallas kernels for 17%

profile of v2, /device:TPU:0, one launch (start us, length us, event | category | flops | bytes accessed | tf_op | source)
XLA Modules:
  0.0 946.9 jit_solution(7479336541265245468)
XLA Ops:
  28.2 9.8 %collective-permute-done.11 = bf16[256,512]{0,1:T(8,128)(2,1)S(1)} collective-permute-done((bf16[256,512]{0,1:T(8,128)(2,1)S(1)}, bf16[256,512]{0,1:T(8,128)(2,1)S(1)}, u32[]{:S(2)}, u32[]{:S(2)}) %collective-permute-start.11) | collective-permute-done | bytes 262176 | tf_op jit(solution)/shard_map/ppermute | solution.py:183
  59.9 10.0 %fusion.36.q_ref = bf16[1024,1536]{1,0:T(8,128)(2,1)S(1)} fusion(bf16[2048,1536]{1,0:T(8,128)(2,1)} %all-gather.5.cloned.1.call-done, bf16[1,1024,2048]{2,1,0:T(8,128)(2,1)} %param.19), kind=kOutput, calls=%fused_computation.40 | convolution fusion | flops 6444023808 | bytes 13631488 | tf_op jit(solution)/shard_map/dot_general | solution.py:208
  83.3 23.4 %attend.1 = bf16[1024,512]{1,0:T(8,128)(2,1)} custom-call(s32[1,1024]{1,0:T(1,128)} %get-tuple-element.760.low_ref, s32[1,1024]{1,0:T(1,128)} %get-tuple-element.759.high_ref, bf16[1024,1536]{1,0:T(8,128)(2,1)} %copy-done.16, bf16[2048,1024]{1,0:T(8,128)(2,1)} %pad_maximum_fusion.k_ref.v_ref, bf16[2048,1024]{1,0:T(8,128)(2,1)} %pad_maximum_fusion.k_ref.v_ref), custom_call_target="tpu_custom_call" | custom-call | flops 10737418240 | bytes 8388608 | tf_op jit(solution)/shard_map/attend/pallas_call | solution.py:287
  115.4 17.8 %collective-permute-done.2 = bf16[1024,512]{1,0:T(8,128)(2,1)S(1)} collective-permute-done((bf16[1024,512]{1,0:T(8,128)(2,1)}, bf16[1024,512]{1,0:T(8,128)(2,1)S(1)}, u32[]{:S(2)}, u32[]{:S(2)}) %collective-permute-start.2) | collective-permute-done | bytes 1048608 | tf_op jit(solution)/shard_map/ppermute | solution.py:183
  139.4 27.1 %collective-permute-done.5 = bf16[1024,512]{1,0:T(8,128)(2,1)} collective-permute-done((bf16[1024,512]{1,0:T(8,128)(2,1)}, bf16[1024,512]{1,0:T(8,128)(2,1)}, u32[]{:S(2)}, u32[]{:S(2)}) %collective-permute-start.5) | collective-permute-done | bytes 1048608 | tf_op jit(solution)/shard_map/ppermute | solution.py:183
  171.2 22.2 %collective-permute-done.7 = bf16[1024,512]{1,0:T(8,128)(2,1)} collective-permute-done((bf16[1024,512]{1,0:T(8,128)(2,1)}, bf16[1024,512]{1,0:T(8,128)(2,1)}, u32[]{:S(2)}, u32[]{:S(2)}) %collective-permute-start.7) | collective-permute-done | bytes 1048608 | tf_op jit(solution)/shard_map/ppermute | solution.py:183
  268.3 9.0 collective-permute-done.14
  285.9 18.6 %collective-permute-done.16 = bf16[256,2048]{1,0:T(8,128)(2,1)S(1)} collective-permute-done((bf16[256,2048]{1,0:T(8,128)(2,1)S(1)}, bf16[256,2048]{1,0:T(8,128)(2,1)S(1)}, u32[]{:S(2)}, u32[]{:S(2)}) %collective-permute-start.16) | collective-permute-done | bytes 1048608 | tf_op jit(solution)/shard_map/ppermute | solution.py:183
  305.2 8.4 collective-permute-start.18
  317.4 17.0 %collective-permute-done.18 = bf16[256,2048]{1,0:T(8,128)(2,1)S(1)} collective-permute-done((bf16[256,2048]{1,0:T(8,128)(2,1)S(1)}, bf16[256,2048]{1,0:T(8,128)(2,1)S(1)}, u32[]{:S(2)}, u32[]{:S(2)}) %collective-permute-start.18) | collective-permute-done | bytes 1048608 | tf_op jit(solution)/shard_map/ppermute | solution.py:183
  346.1 18.5 %collective-permute-done.20 = bf16[256,2048]{1,0:T(8,128)(2,1)S(1)} collective-permute-done((bf16[256,2048]{1,0:T(8,128)(2,1)S(1)}, bf16[256,2048]{1,0:T(8,128)(2,1)S(1)}, u32[]{:S(2)}, u32[]{:S(2)}) %collective-permute-start.20) | collective-permute-done | bytes 1048608 | tf_op jit(solution)/shard_map/ppermute | solution.py:183
  383.9 8.9 collective-permute-done.23
  450.9 11.2 %convolution_convert_fusion.2 = bf16[2048,2048]{1,0:T(8,128)(2,1)} fusion(bf16[256,2048]{1,0:T(8,128)(2,1)S(1)} %add.645, bf16[256,2048]{1,0:T(8,128)(2,1)S(1)} %add.643, bf16[256,2048]{1,0:T(8,128)(2,1)S(1)} %add.644, bf16[256,2048]{1,0:T(8,128)(2,1)S(1)} %get-tuple-element.399, bf16[256,2048]{1,0:T(8,128)(2,1)S(1)} %copy-done.110, ...), kind=kOutput, calls=%fused_computation.2 | convolution fusion | flops 8627683328 | bytes 16777216 | tf_op jit(solution)/shard_map/dot_general | solution.py:216
  482.3 12.8 %convolution_convert_fusion.1 = bf16[2048,2048]{1,0:T(8,128)(2,1)} fusion(bf16[256,2048]{1,0:T(8,128)(2,1)S(1)} %copy-done.65, bf16[256,2048]{1,0:T(8,128)(2,1)S(1)} %copy-done.54, bf16[256,2048]{1,0:T(8,128)(2,1)S(1)} %copy-done.67, bf16[256,2048]{1,0:T(8,128)(2,1)S(1)} %copy-done.52, bf16[256,2048]{1,0:T(8,128)(2,1)} %copy-done.106, ...), kind=kOutput, calls=%fused_computation.1 | convolution fusion | flops 8627683328 | bytes 16777216 | tf_op jit(solution)/shard_map/dot_general | solution.py:216
  500.4 9.3 collective-permute-start.36
  554.4 13.6 %collective-permute-start.41 = (bf16[256,512]{1,0:T(8,128)(2,1)S(1)}, bf16[256,512]{1,0:T(8,128)(2,1)S(1)}, u32[]{:S(2)}, u32[]{:S(2)}) collective-permute-start(bf16[256,512]{1,0:T(8,128)(2,1)S(1)} %get-tuple-element.455), channel_id=1, source_target_pairs={{0,1},{1,2},{2,3},{3,0},{4,5},{5,6},{6,7},{7,4},{8,9},{9,10},{10,1... | collective-permute-start | bytes 786440 | tf_op jit(solution)/shard_map/ppermute | solution.py:183
  573.2 32.1 %attend_back.1 = (bf16[1024,512]{1,0:T(8,128)(2,1)}, f32[2048,512]{1,0:T(8,128)}, f32[2048,512]{1,0:T(8,128)}) custom-call(s32[1,1024]{1,0:T(1,128)} %get-tuple-element.760.low_ref, s32[1,1024]{1,0:T(1,128)} %get-tuple-element.759.high_ref, bf16[1024,1536]{1,0:T(8,128)(2,1)} %copy-done.16, bf16[2048,1024]{1,0:T(8,128)(2,1)} %pad_maximum_fusion.k_ref.v_ref, ...), custom_call_target="tpu_custom_call" | custom-call | flops 21474836480 | bytes 20971520 | tf_op jit(solution)/shard_map/attend_back/pallas_call | solution.py:306
  668.2 9.3 convolution_convert_fusion.3
  722.0 14.9 %collective-permute-done.58 = f32[4,2048]{1,0:T(4,128)} collective-permute-done((f32[4,2048]{1,0:T(4,128)}, f32[4,2048]{1,0:T(4,128)}, u32[]{:S(2)}, u32[]{:S(2)}) %collective-permute-start.58) | collective-permute-done | bytes 32800 | tf_op jit(solution)/shard_map/ppermute | solution.py:183
  762.0 19.9 %newton_schulz.4.in_ref = f32[512,2048]{1,0:T(8,128)} custom-call(bf16[2048,512]{1,0:T(8,128)(2,1)} %bitcast.55.in_ref), custom_call_target="tpu_custom_call" | custom-call | flops 11811160064 | bytes 6291456 | tf_op jit(solution)/shard_map/newton_schulz/pallas_call | solution.py:417
  798.1 25.7 %newton_schulz.5 = bf16[2048,512]{1,0:T(8,128)(2,1)} custom-call(f32[512,2048]{1,0:T(8,128)} %newton_schulz.4.in_ref), custom_call_target="tpu_custom_call" | custom-call | flops 17716740096 | bytes 6291456 | tf_op jit(solution)/shard_map/newton_schulz/pallas_call | solution.py:417
  856.3 19.8 %newton_schulz.6.in_ref = f32[512,2048]{1,0:T(8,128)} custom-call(bf16[2048,512]{1,0:T(8,128)(2,1)} %bitcast.72.in_ref), custom_call_target="tpu_custom_call" | custom-call | flops 11811160064 | bytes 6291456 | tf_op jit(solution)/shard_map/newton_schulz/pallas_call | solution.py:417
  876.1 9.0 collective-permute-done.74.refs_4_
  888.1 25.7 %newton_schulz.7 = bf16[2048,512]{1,0:T(8,128)(2,1)} custom-call(f32[512,2048]{1,0:T(8,128)} %newton_schulz.6.in_ref), custom_call_target="tpu_custom_call" | custom-call | flops 17716740096 | bytes 6291456 | tf_op jit(solution)/shard_map/newton_schulz/pallas_call | solution.py:417
  (624 shorter events, 535.7 us)
Async XLA Ops:
  7.2 52.7 %all-gather.5.cloned.1.call-start = ((), (), s32[]{:S(2)}) async-start(), calls=%async_computation.5 | async-start | bytes 7077888 | tf_op jit(solution)/shard_map/all_gather | solution.py:467
  11.5 188.0 %all-gather.7.cloned.1.call-start = ((), (), s32[]{:S(2)}) async-start(), calls=%async_computation.6 | async-start | bytes 9437184 | tf_op jit(solution)/shard_map/all_gather | solution.py:467
  48.2 165.3 %all-gather.9.cloned.1.call-start = ((), (), s32[]{:S(2)}) async-start(), calls=%async_computation.7 | async-start | bytes 9437184 | tf_op jit(solution)/shard_map/all_gather | solution.py:467
  51.1 182.4 %all-gather.11.cloned.1.call-start = ((), (), s32[]{:S(2)}) async-start(), calls=%async_computation.8 | async-start | bytes 9437184 | tf_op jit(solution)/shard_map/all_gather | solution.py:467
  52.3 590.4 %reduce-scatter.6.cloned.1.call-start = ((), (), s32[]{:S(2)}) async-start(), calls=%async_computation.10 | async-start | bytes 9437184 | tf_op jit(solution)/shard_map/reduce_scatter | solution.py:471
  138.1 28.4 %collective-permute-start.5 = (bf16[1024,512]{1,0:T(8,128)(2,1)}, bf16[1024,512]{1,0:T(8,128)(2,1)}, u32[]{:S(2)}, u32[]{:S(2)}) collective-permute-start(bf16[1024,512]{1,0:T(8,128)(2,1)} %collective-permute-done.3), channel_id=1, source_target_pairs={{1,0},{2,1},{5,4},{6,5},{9,8},{10,9},{13,12},{14,13},{17,16},{18,1... | collective-permute-start | bytes 3145736 | tf_op jit(solution)/shard_map/ppermute | solution.py:183
  305.2 29.2 %collective-permute-start.18 = (bf16[256,2048]{1,0:T(8,128)(2,1)S(1)}, bf16[256,2048]{1,0:T(8,128)(2,1)S(1)}, u32[]{:S(2)}, u32[]{:S(2)}) collective-permute-start(bf16[256,2048]{1,0:T(8,128)(2,1)S(1)} %add_convert_fusion.7), channel_id=1, source_target_pairs={{0,1},{1,2},{2,3},{4,5},{5,6},{6,7},{8,9},{9,10},{10,11},{12,13},{... | collective-permute-start | bytes 3145736 | tf_op jit(solution)/shard_map/ppermute | solution.py:183
  467.0 175.7 %reduce-scatter.4.cloned.1.call-start = ((), (), s32[]{:S(2)}) async-start(), calls=%async_computation.9 | async-start | bytes 9437184 | tf_op jit(solution)/shard_map/reduce_scatter | solution.py:471
  554.4 50.9 %collective-permute-start.41 = (bf16[256,512]{1,0:T(8,128)(2,1)S(1)}, bf16[256,512]{1,0:T(8,128)(2,1)S(1)}, u32[]{:S(2)}, u32[]{:S(2)}) collective-permute-start(bf16[256,512]{1,0:T(8,128)(2,1)S(1)} %get-tuple-element.455), channel_id=1, source_target_pairs={{0,1},{1,2},{2,3},{3,0},{4,5},{5,6},{6,7},{7,4},{8,9},{9,10},{10,1... | collective-permute-start | bytes 786440 | tf_op jit(solution)/shard_map/ppermute | solution.py:183
  568.0 37.3 %collective-permute-start.42 = (bf16[256,512]{1,0:T(8,128)(2,1)S(1)}, bf16[256,512]{1,0:T(8,128)(2,1)S(1)}, u32[]{:S(2)}, u32[]{:S(2)}) collective-permute-start(bf16[256,512]{1,0:T(8,128)(2,1)S(1)} %get-tuple-element.456), channel_id=1, source_target_pairs={{0,2},{1,3},{2,0},{3,1},{4,6},{5,7},{6,4},{7,5},{8,10},{9,11},{10,... | collective-permute-start | bytes 786440 | tf_op jit(solution)/shard_map/ppermute | solution.py:183
  568.0 37.3 %collective-permute-start.43 = (bf16[256,512]{1,0:T(8,128)(2,1)S(1)}, bf16[256,512]{1,0:T(8,128)(2,1)S(1)}, u32[]{:S(2)}, u32[]{:S(2)}) collective-permute-start(bf16[256,512]{1,0:T(8,128)(2,1)S(1)} %get-tuple-element.457), channel_id=1, source_target_pairs={{0,3},{1,0},{2,1},{3,2},{4,7},{5,4},{6,5},{7,6},{8,11},{9,8},{10,9... | collective-permute-start | bytes 786440 | tf_op jit(solution)/shard_map/ppermute | solution.py:183
  570.3 34.9 %collective-permute-start.44 = (f32[4,2048]{1,0:T(4,128)S(1)}, f32[4,2048]{1,0:T(4,128)S(1)}, u32[]{:S(2)}, u32[]{:S(2)}) collective-permute-start(f32[4,2048]{1,0:T(4,128)S(1)} %pad_maximum_fusion.9), channel_id=1, source_target_pairs={{0,4},{4,0},{1,5},{5,1},{2,6},{6,2},{3,7},{7,3},{8,12},{12,8},{9,1... | collective-permute-start | bytes 98312 | tf_op jit(solution)/shard_map/ppermute | solution.py:183
  693.2 43.8 %all-to-all-start = ((bf16[8,256,512]{2,1,0:T(8,128)(2,1)}), bf16[8,256,512]{2,1,0:T(8,128)(2,1)}, u32[]{:S(2)}, u32[]{:S(2)}) async-start(bf16[8,256,512]{2,1,0:T(8,128)(2,1)} %fusion.160), calls=%async_computation.2 | async-start | bytes 4194304 | tf_op jit(solution)/shard_map/all_to_all | solution.py:183
  697.5 52.5 %reduce-scatter.8.cloned.1.call-start = ((), (), s32[]{:S(2)}) async-start(), calls=%async_computation.11 | async-start | bytes 2359296 | tf_op jit(solution)/shard_map/reduce_scatter | solution.py:471
  697.6 39.3 %collective-permute-start.54 = (bf16[256,2048]{1,0:T(8,128)(2,1)}, bf16[256,2048]{1,0:T(8,128)(2,1)}, u32[]{:S(2)}, u32[]{:S(2)}) collective-permute-start(bf16[256,2048]{1,0:T(8,128)(2,1)} %get-tuple-element.511), channel_id=1, source_target_pairs={{0,1},{1,2},{4,5},{5,6},{8,9},{9,10},{12,13},{13,14},{16,17},{17,1... | collective-permute-start | bytes 3145736 | tf_op jit(solution)/shard_map/ppermute | solution.py:183
  703.1 33.8 %collective-permute-start.55 = (bf16[256,2048]{1,0:T(8,128)(2,1)}, bf16[256,2048]{1,0:T(8,128)(2,1)}, u32[]{:S(2)}, u32[]{:S(2)}) collective-permute-start(bf16[256,2048]{1,0:T(8,128)(2,1)} %get-tuple-element.512), channel_id=1, source_target_pairs={{2,1},{3,2},{6,5},{7,6},{10,9},{11,10},{14,13},{15,14},{18,17},{19... | collective-permute-start | bytes 3145736 | tf_op jit(solution)/shard_map/ppermute | solution.py:183
  750.1 33.1 %collective-permute-start.59 = (bf16[256,2048]{1,0:T(8,128)(2,1)}, bf16[256,2048]{1,0:T(8,128)(2,1)}, u32[]{:S(2)}, u32[]{:S(2)}) collective-permute-start(bf16[256,2048]{1,0:T(8,128)(2,1)} %add_convert_fusion.2), channel_id=1, source_target_pairs={{0,1},{1,2},{2,3},{4,5},{5,6},{6,7},{8,9},{9,10},{10,11},{12,13},{... | collective-permute-start | bytes 3145736 | tf_op jit(solution)/shard_map/ppermute | solution.py:183
  754.5 28.7 %collective-permute-start.60 = (bf16[256,2048]{1,0:T(8,128)(2,1)S(1)}, bf16[256,2048]{1,0:T(8,128)(2,1)}, u32[]{:S(2)}, u32[]{:S(2)}) collective-permute-start(bf16[256,2048]{1,0:T(8,128)(2,1)S(1)} %add_convert_fusion.1), channel_id=1, source_target_pairs={{1,0},{2,1},{3,2},{5,4},{6,5},{7,6},{9,8},{10,9},{11,10},{13,12},{... | collective-permute-start | bytes 3145736 | tf_op jit(solution)/shard_map/ppermute | solution.py:183
  788.9 50.9 %collective-permute-start.63 = (bf16[256,2048]{1,0:T(8,128)(2,1)S(1)}, bf16[256,2048]{1,0:T(8,128)(2,1)}, u32[]{:S(2)}, u32[]{:S(2)}) collective-permute-start(bf16[256,2048]{1,0:T(8,128)(2,1)S(1)} %add_convert_fusion.refs_0_), channel_id=1, source_target_pairs={{0,1},{1,2},{2,3},{4,5},{5,6},{6,7},{8,9},{9,10},{10,11},{12,13},{... | collective-permute-start | bytes 3145736 | tf_op jit(solution)/shard_map/ppermute | solution.py:183
  792.6 47.2 %collective-permute-start.64 = (bf16[256,2048]{1,0:T(8,128)(2,1)S(1)}, bf16[256,2048]{1,0:T(8,128)(2,1)}, u32[]{:S(2)}, u32[]{:S(2)}) collective-permute-start(bf16[256,2048]{1,0:T(8,128)(2,1)S(1)} %add_convert_fusion.refs_0_), channel_id=1, source_target_pairs={{1,0},{2,1},{3,2},{5,4},{6,5},{7,6},{9,8},{10,9},{11,10},{13,12},{... | collective-permute-start | bytes 3145736 | tf_op jit(solution)/shard_map/ppermute | solution.py:183
  793.9 35.6 %collective-permute-start.68 = (f32[4,2048]{1,0:T(4,128)S(1)}, f32[4,2048]{1,0:T(4,128)S(1)}, u32[]{:S(2)}, u32[]{:S(2)}) collective-permute-start(f32[4,2048]{1,0:T(4,128)S(1)} %add.693), channel_id=1, source_target_pairs={{0,2},{1,3},{2,0},{3,1},{4,6},{5,7},{6,4},{7,5},{8,10},{9,11},{10,... | collective-permute-start | bytes 98312 | tf_op jit(solution)/shard_map/ppermute | solution.py:183
  849.4 35.7 %all-to-all-start.1 = ((bf16[8,256,512]{2,1,0:T(8,128)(2,1)}), bf16[8,256,512]{2,1,0:T(8,128)(2,1)S(1)}, u32[]{:S(2)}, u32[]{:S(2)}) async-start(bf16[8,256,512]{2,1,0:T(8,128)(2,1)} %bitcast.285), calls=%async_computation.4 | async-start | bytes 4194304 | tf_op jit(solution)/shard_map/all_to_all | solution.py:183
  855.0 30.1 %collective-permute-start.74 = (bf16[256,2048]{1,0:T(8,128)(2,1)}, bf16[256,2048]{1,0:T(8,128)(2,1)}, u32[]{:S(2)}, u32[]{:S(2)}) collective-permute-start(bf16[256,2048]{1,0:T(8,128)(2,1)} %collective-permute-done.64.refs_6_), channel_id=1, source_target_pairs={{1,0},{2,1},{5,4},{6,5},{9,8},{10,9},{13,12},{14,13},{17,16},{18,1... | collective-permute-start | bytes 3145736 | tf_op jit(solution)/shard_map/ppermute | solution.py:183
  885.1 28.7 %collective-permute-start.75 = (bf16[256,2048]{1,0:T(8,128)(2,1)S(1)}, bf16[256,2048]{1,0:T(8,128)(2,1)}, u32[]{:S(2)}, u32[]{:S(2)}) collective-permute-start(bf16[256,2048]{1,0:T(8,128)(2,1)S(1)} %collective-permute-done.73.refs_3_), channel_id=1, source_target_pairs={{2,3},{6,7},{10,11},{14,15},{18,19},{22,23},{26,27},{30,31}} | collective-permute-start | bytes 3145736 | tf_op jit(solution)/shard_map/ppermute | solution.py:183
  (192 other events, 2341.7 us)
Sparse Core Ops, SparseCore 0:
  11.6 48.2 all-gather.4
  62.3 56.1 all-gather.6
  121.0 54.2 all-gather.8
  177.5 55.9 all-gather.10
  467.1 72.3 reduce-scatter.5
  543.7 71.2 reduce-scatter.3
  704.9 45.0 reduce-scatter.7

commit v3 on v2

--- a/solution.py
+++ b/solution.py
@@ -117,64 +117,6 @@
         self.got = got
 
 
-class Total:
-    def __init__(self, value, axes):
-        self.value = value
-        self.rounds = [
-            (axis, 1 << k) for axis in axes for k in range(lax.axis_size(axis).bit_length() - 1)
-        ]
-
-    def sends(self):
-        if not self.rounds:
-            return []
-        axis, by = self.rounds.pop(0)
-        return [along(self.value, axis, [(i, i ^ by) for i in range(lax.axis_size(axis))])]
-
-    def take(self, got):
-        for other in got:
-            self.value = self.value + other
-
-
-class Halving:
-    def __init__(self, value, axes):
-        bits = [
-            (axis, k)
-            for axis in axes
-            for k in reversed(range(lax.axis_size(axis).bit_length() - 1))
-        ]
-        blocks = math.prod(lax.axis_size(axis) for axis in axes)
-        rows, width = value.shape[0] // blocks, value.shape[1] // 2
-        first = [bit for bit in bits if bit[0] != axes[0]]
-        last = [bit for bit in bits if bit[0] == axes[0]]
-        self.rounds = len(bits)
-        self.groups = []
-        for g, order in enumerate((first + last, first + last[::-1])):
-            columns = value[:, g * width : (g + 1) * width]
-            self.groups.append([columns.reshape((2,) * len(bits) + (rows, width)), list(bits), order])
-
-    def sends(self):
-        sent = []
-        self.kept = []
-        for value, left, order in self.groups:
-            axis, k = bit = order.pop(0)
-            dim = left.index(bit)
-            left.pop(dim)
-            mine = (lax.axis_index(axis) >> k) & 1
-            pairs = [(i, i ^ (1 << k)) for i in range(lax.axis_size(axis))]
-            self.kept.append(lax.dynamic_index_in_dim(value, mine, dim, keepdims=False))
-            away = lax.dynamic_index_in_dim(value, 1 - mine, dim, keepdims=False)
-            sent.append(along(away, axis, pairs))
-        self.rounds -= 1
-        return sent
-
-    def take(self, got):
-        for group, kept, other in zip(self.groups, self.kept, got):
-            group[0] = (kept.astype(F32) + other.astype(F32)).astype(BF16)
-
-    def total(self):
-        return jnp.concatenate([group[0] for group in self.groups], axis=1)
-
-
 def step(movers, work=None, *operands):
     sends = [mover.sends() for mover in movers]
     values = [[value for value, _ in group] for group in sends]
@@ -192,7 +134,7 @@
 def slot_order(count):
     order = []
     for hop in range(1, count):
-        order += [r for r in (hop, count - hop) if r not in order]
+        order += [r for r in dict.fromkeys((hop, count - hop)) if r not in order]
     return order + [0]
 
 
@@ -386,8 +328,7 @@
     lax.fori_loop(0, chunks, split, 0)
 
     def step(index, carry):
-        cross = dot_nt(rest[...], top[...])
-        gram = dot_nt(top[...], top[...]) + (cross + cross.T)
+        gram = dot_nt(top[...], top[...])
         gram_top, gram_rest = halves(gram)
         cross = dot(gram_top, gram_rest)
         square = dot(gram_top, gram_top) + (cross + cross.T)
@@ -421,7 +362,7 @@
         out_specs=pl.BlockSpec(memory_space=pltpu.VMEM),
         scratch_shapes=[pltpu.VMEM((width, depth), BF16), pltpu.VMEM((width, depth), BF16), *scratch],
         cost_estimate=pl.CostEstimate(
-            flops=2 * steps * width * width * (5 * depth + 2 * width),
+            flops=2 * steps * width * width * (4 * depth + 2 * width),
             transcendentals=0,
             bytes_accessed=6 * depth * width,
         ),
@@ -540,33 +481,29 @@
     order = slot_order(tp)
     first, rest = order[:2], order[2:]
     normed_slots, pre_slots, act_slots, parts = ([None] * tp for _ in range(4))
-    own = []
-
-    def forward(slots, *head_slots):
-        made = []
-        for r in slots:
-            attended_r = jnp.concatenate([slice_of(slot, r) for slot in head_slots], axis=1)
-            branch = dot_nt(attended_r, full_out_t)
-            unit, scale = normalize(slice_of(hidden, r).astype(F32) + branch)
-            normed = unit * norm_gains[0] + norm_biases[0]
-            normed_low = normed.astype(BF16)
-            pre = dot(normed_low, full_inner)
-            act = gelu_tanh(pre).astype(BF16)
-            part = dot_nt(act, full_outer_t)
-            made.append((normed_low, pre, act, part if r == 0 else part.astype(BF16)))
-            if r == 0:
-                made.append((unit, scale, normed))
-        return made
-
-    def keep(slots, made):
-        for r, values in zip(slots, made):
-            normed_slots[r], pre_slots[r], act_slots[r], parts[r] = values
-
-    keep(first, forward(first, *head_slots))
+    def forward(r):
+        attended_r = jnp.concatenate([slice_of(slot, r) for slot in head_slots], axis=1)
+        branch = dot_nt(attended_r, full_out_t)
+        unit, scale = normalize(slice_of(hidden, r).astype(F32) + branch)
+        normed = unit * norm_gains[0] + norm_biases[0]
+        normed_slots[r] = normed.astype(BF16)
+        pre_slots[r] = dot(normed_slots[r], full_inner)
+        act_slots[r] = gelu_tanh(pre_slots[r]).astype(BF16)
+        return unit, scale, normed
+
+    def terms_of(slots, *acts):
+        return [
+            dot_nt(act, full_outer_t).astype(F32 if r == 0 else BF16) for r, act in zip(slots, acts)
+        ]
+
+    for r in order:
+        unit_one, scale_one, own_normed = forward(r)
+    for r, value in zip(first, terms_of(first, *[act_slots[r] for r in first])):
+        parts[r] = value
     ffn_sum = Scatter(parts, "tp")
-    made = step([ffn_sum], functools.partial(forward, rest), *head_slots)
-    unit_one, scale_one, own_normed = made[-1]
-    keep(rest, made)
+    acts = [act_slots[r] for r in rest]
+    for r, value in zip(rest, step([ffn_sum], functools.partial(terms_of, rest), *acts)):
+        parts[r] = value
 
     def slopes_of(*pres):
         return [jax.vjp(gelu_tanh, pre)[1](jnp.ones_like(pre))[0] for pre in pres]
@@ -629,9 +566,7 @@
     dattended_all = dot(dbranch_low, full_out_t).astype(BF16)
     blocks = [dattended_all[:, (-r % tp) * local : (-r % tp + 1) * local] for r in range(tp)]
     dattended = Exchange(blocks, "tp")
-    totals = Total(
-        jnp.stack([gain_one, gain_two, shift_one, shift_two]), ("ctx", "shard", "tp")
-    )
+    sums = jnp.stack([gain_one, gain_two, shift_one, shift_two])
     step([dattended])
     part = width // tp
     dbranch = Exchange(
@@ -645,7 +580,7 @@
     def attention_back(*slots):
         return attend_back(low, high, qkv, padded_kv, placed([[slot] for slot in slots], BF16, me), heads)
 
-    dq_low, key_grad, value_grad = step([dbranch, totals], attention_back, *dattended.slots)
+    dq_low, key_grad, value_grad = step([dbranch], attention_back, *dattended.slots)
 
     def kv_rows(start, count):
         rows = slice(start, start + count)
@@ -663,13 +598,14 @@
         sums = [dot_tn(columns, slot).astype(BF16).reshape(-1, rows, local) for slot in head_slots]
         return row_major(jnp.stack(sums, axis=1).reshape(group * rows, local))
 
-    step([edges])
+    pieces = step([edges], out_pieces, dbranch.slots, head_slots)
     from_above, from_below = (edge.astype(F32) for edge in edges.got)
     beyond = length - REACH
     added = jnp.pad(from_above, ((beyond, 0), (0, 0))) + jnp.pad(from_below, ((0, beyond), (0, 0)))
     dqkv = jnp.concatenate([dq_low, (kv_rows(REACH, length) + added).astype(BF16)], axis=1)
-    grad_qkv = row_major(dot_tn(hidden, dqkv).astype(BF16))
-    qkv_sum = Halving(grad_qkv, WEIGHT_AXES)
+    grad_attn = row_major(jnp.concatenate([dot_tn(hidden, dqkv).astype(BF16), pieces], axis=1))
+    dqkv = after(dqkv, grad_attn)
+    grad_attn = scatter_rows(grad_attn)
 
     parts = [None] * tp
 
@@ -678,45 +614,44 @@
         sums = dot_nt(rows, full_qkv).astype(BF16)
         return [sums[n * share : (n + 1) * share] for n in range(len(slots))]
 
-    for r, value in zip(first, step([qkv_sum], functools.partial(input_terms, first), dqkv)):
+    for r, value in zip(first, input_terms(first, dqkv)):
         parts[r] = value
     input_sum = Scatter(parts, "tp")
 
-    def between(dqkv, dbranch_slots, head_slots, grad_inner, grad_outer_t):
-        pieces = out_pieces(dbranch_slots, head_slots)
+    def between(dqkv, grad_inner, grad_outer_t):
         moments = blend(mom_inner, grad_inner), blend(mom_outer_t, grad_outer_t)
         blocks = to_owners(sum(map(column_blocks, moments), []))
-        return input_terms(rest, dqkv), moments, blocks, pieces
-
-    terms, (moment_inner, moment_outer_t), blocks, pieces = step(
-        [input_sum, qkv_sum, totals],
-        between,
-        dqkv,
-        dbranch.slots,
-        head_slots,
-        grad_inner,
-        grad_outer_t,
+        return input_terms(rest, dqkv), moments, blocks
+
+    terms, (moment_inner, moment_outer_t), blocks = step(
+        [input_sum], between, dqkv, grad_inner, grad_outer_t
     )
     grad_inner, grad_outer_t = grad_inner.astype(F32), grad_outer_t.astype(F32)
     for r, value in zip(rest, terms):
         parts[r] = value
-    grad_piece = scatter_rows(pieces)
     owners = Once(swapped(blocks))
-    step([input_sum, qkv_sum, totals, owners])
+    grad_outer, moment_outer = step(
+        [input_sum, owners], lambda a, b: (a.T, b.T), grad_outer_t, moment_outer_t
+    )
     homes = [
         (p * tp + t, (t * (group // tp) + p // tp) * tp + (t - p % tp) % tp)
         for p in range(group)
         for t in range(tp)
     ]
-    piece = Once(along(grad_piece, (*WEIGHT_AXES, "tp"), homes))
-    iterate = step([input_sum, totals, piece], orthogonal_start, owners.got[0])
+    piece = Once(along(grad_attn[:, 3 * local :], (*WEIGHT_AXES, "tp"), homes))
+    iterate, grad_qkv, sums = step(
+        [input_sum, piece],
+        lambda owned, *values: (orthogonal_start(owned), *values),
+        owners.got[0],
+        grad_attn[:, : 3 * local],
+        sums,
+    )
+    totals = jnp.sum(lax.all_gather(sums, (*WEIGHT_AXES, "tp"), axis=0), axis=0)
     for _ in range(tp - 4):
         step([input_sum])
-    while qkv_sum.rounds:
-        step([qkv_sum])
     own_input = Gather((grad_one + input_sum.total()).astype(BF16), "tp")
 
-    grad_query, grad_key, grad_value = jnp.split(qkv_sum.total().astype(F32), 3, axis=1)
+    grad_query, grad_key, grad_value = jnp.split(grad_qkv.astype(F32), 3, axis=1)
     grad_out_t = row_major(piece.got[0]).astype(F32)
     moment_query = blend(mom_query, grad_query)
     moment_key = blend(mom_key, grad_key)
@@ -732,21 +667,15 @@
     def turned(value, r):
         return lax.dynamic_index_in_dim(value, lax.rem(at_shard + r, shard), 0, keepdims=False)
 
-    owners = Exchange([turned(blocks, r) for r in range(shard)], "shard")
+    owners = Exchange([turned(blocks, r)[0] for r in range(shard)], "shard")
     finish = functools.partial(orthogonal_end, group=group)
-    done = step([own_input, owners, totals], finish, iterate)
-    spread = [owners.slots]
-    for by in range(1, ctx):
-        pairs = [(i, (i + by) % ctx) for i in range(ctx)]
-        peers = Once(*[along(slot, "ctx", pairs) for slot in owners.slots])
-        step([peers])
-        spread.append(peers.got)
-    at_ctx = lax.axis_index("ctx")
-    owned = jnp.zeros((shard, ctx, *blocks.shape[2:]), BF16)
-    for by, slots in enumerate(spread):
-        for r, slot in enumerate(slots):
-            where = lax.rem(at_shard - r + shard, shard), lax.rem(at_ctx - by + ctx, ctx)
-            owned = lax.dynamic_update_slice(owned, slot[None], (*where, 0, 0))
+    step([owners])
+    mine = row_major(jnp.stack(owners.slots))
+    peers = Once(
+        *[along(mine, "ctx", [(i, (i + by) % ctx) for i in range(ctx)]) for by in range(1, ctx)]
+    )
+    done = step([own_input, peers], finish, iterate)
+    owned = jnp.concatenate([mine, *peers.got], axis=0)
 
     def update_ffn(back):
         ortho = from_owners(back, 2 * moment_inner.shape[1] // BW)
@@ -757,27 +686,29 @@
         )
 
     ortho = Once(swapped(done))
-    iterate = step([own_input, ortho], orthogonal_start, owned.reshape(group, rows, BW))
-    done = step([own_input], finish, iterate).reshape(shard, ctx, rows, BW)
+    iterate = step([own_input, ortho], orthogonal_start, owned)
+    done = row_major(step([own_input], finish, iterate))
     for _ in range(tp - 4):
         step([own_input])
-    done = lax.dynamic_index_in_dim(done, at_ctx, 1, keepdims=False)
-    attn = Exchange([turned(done, r) for r in range(shard)], "shard")
+    attn = Once(
+        *[
+            along(done[r], "shard", [(i, (i - r) % shard) for i in range(shard)])
+            for r in range(1, shard)
+        ]
+    )
 
     def closing(back, *slots):
         return update_ffn(back), placed(slots, F32, me)
 
     (new_inner, new_outer), input_grad = step([attn], closing, ortho.got[0], *own_input.terms())
     input_grad = input_grad[None]
-    ortho = jnp.stack(attn.slots)
+    ortho = row_major(jnp.stack([done[0], *map(row_major, attn.got)]))
     ortho = [
-        lax.dynamic_index_in_dim(ortho, lax.rem(at_shard - b + shard, shard), 0, keepdims=False)
+        lax.dynamic_index_in_dim(ortho, lax.rem(b - at_shard + shard, shard), 0, keepdims=False)
         for b in range(shard)
     ]
-    ortho = [block.astype(F32) for block in ortho]
-    while totals.rounds:
-        step([totals])
-    gain_grad, bias_grad = totals.value[:2], totals.value[2:]
+    ortho = [row_major(block).astype(F32) for block in ortho]
+    gain_grad, bias_grad = totals[:2], totals[2:]
     new_query = w_query - MATRIX_RATE * ortho[0]
     new_key = w_key - MATRIX_RATE * ortho[1]
     new_value = w_value - MATRIX_RATE * ortho[2]
@@ -796,7 +727,7 @@
         grad_value,
         grad_out_t.T,
         grad_inner,
-        grad_outer_t.T,
+        grad_outer,
         gain_grad,
         bias_grad,
         moment_query,
@@ -804,7 +735,7 @@
         moment_value,
         moment_out_t.T,
         moment_inner,
-        moment_outer_t.T,
+        moment_outer,
         gain_moment_new,
         bias_moment_new,
         new_query,

time: 956 us -> 938 us (0.981)
  local copies, waits for them, and re-layouts: 78.2 us -> 53.6 us
  waiting for transfers between devices: 266 us -> 287 us
  starting transfers between devices: 178 us -> 160 us
  other arithmetic: 87 us -> 101 us
  Pallas kernels: 165 us -> 154 us
    reduce_scatter x3, waiting for transfers between devices: 3.46 us -> 32.7 us  [scatter_rows(): return lax.psum_scatter(value, WEIGHT_AXES, scatter_dimension=0, tiled=True)]
    ppermute x80 -> x66, starting transfers between devices: 170 us -> 149 us  [step(): send(value)]
    unnamed x277 -> x193, local copies, waits for them, and re-layouts: 46.2 us -> 32.3 us
    pallas_call x4, Pallas kernels: 91.1 us -> 80.2 us  [newton_schulz_part(): pl.pallas_call(functools.partial(newton_schulz_kernel, steps), out_shape=...]
    concatenate x0 -> x2, other arithmetic: none -> 10.2 us  [the longest x1 7.5 us: body(): jnp.concatenate([dot_tn(hidden, dqkv).astype(BF16), pieces], axis=1)]
    ppermute x80 -> x66, waiting for transfers between devices: 247 us -> 240 us  [step(): send(value)]
  transfers between devices with their start and end apart: 89 -> 76, of which waited for: 37 -> 36; matrix products, arithmetic and copies ran while one was open for 25% -> 27% of each run, Pallas kernels for 17% -> 17%
where the time goes in v3:
time: 938 us; the launch traced here: 929 us
  waiting for transfers between devices  287 us (31%)
  starting transfers between devices  160 us (17%)
  matrix products  157 us (17%)
  Pallas kernels  154 us (16%)
  other arithmetic  101 us (11%)
  local copies, waits for them, and re-layouts  53.6 us (6%)
  between operations  16.4 us (2%)
    ppermute x66, waiting for transfers between devices, step(): send(value)  240 us
    ppermute x66, starting transfers between devices, step(): send(value)  149 us
    pallas_call x4, Pallas kernels, newton_schulz_part(): pl.pallas_call(functools.partial(newton_schulz_kernel, steps), out_shape=...  80.2 us
    dot_general x14, matrix products, dot_nt(): lax.dot_general(left, right, (((1,), (1,)), ((), ())), preferred_element_...  62.1 us
    dot_general x10, matrix products, dot(): return jnp.dot(left, right, preferred_element_type=F32)  57.6 us
    dot_general x7, matrix products, dot_tn(): lax.dot_general(left, right, (((0,), (0,)), ((), ())), preferred_element_...  37.2 us
    reduce_scatter x3, waiting for transfers between devices, scatter_rows(): return lax.psum_scatter(value, WEIGHT_AXES, scatter_dimension=0, tiled=True)  32.7 us
    unnamed x193, local copies, waits for them, and re-layouts  32.3 us
  transfers between devices with their start and end apart: 76, of which 36 were waited for; matrix products, arithmetic and copies ran while one was open for 27% of the time, Pallas kernels for 17%

profile of v3, /device:TPU:0, one launch (start us, length us, event | category | flops | bytes accessed | tf_op | source)
XLA Modules:
  0.0 928.9 jit_solution(2103990994792857343)
XLA Ops:
  28.2 9.8 %collective-permute-done.11 = bf16[256,512]{0,1:T(8,128)(2,1)S(1)} collective-permute-done((bf16[256,512]{0,1:T(8,128)(2,1)S(1)}, bf16[256,512]{0,1:T(8,128)(2,1)S(1)}, u32[]{:S(2)}, u32[]{:S(2)}) %collective-permute-start.11) | collective-permute-done | bytes 262176 | tf_op jit(solution)/shard_map/ppermute | solution.py:125
  59.9 10.0 %fusion.36.q_ref = bf16[1024,1536]{1,0:T(8,128)(2,1)S(1)} fusion(bf16[2048,1536]{1,0:T(8,128)(2,1)} %all-gather.8.cloned.1.call-done, bf16[1,1024,2048]{2,1,0:T(8,128)(2,1)} %param.19), kind=kOutput, calls=%fused_computation.40 | convolution fusion | flops 6444023808 | bytes 13631488 | tf_op jit(solution)/shard_map/dot_general | solution.py:150
  83.2 23.4 %attend.1 = bf16[1024,512]{1,0:T(8,128)(2,1)} custom-call(s32[1,1024]{1,0:T(1,128)} %get-tuple-element.691.low_ref, s32[1,1024]{1,0:T(1,128)} %get-tuple-element.690.high_ref, bf16[1024,1536]{1,0:T(8,128)(2,1)} %copy-done.16, bf16[2048,1024]{1,0:T(8,128)(2,1)} %pad_maximum_fusion.1.k_ref.v_ref, bf16[2048,1024]{1,0:T(8,128)(2,1)} %pad_maximum_fusion.1.k_ref.v_ref), custom_call_target="tpu_custom_call" | custom-call | flops 10737418240 | bytes 8388608 | tf_op jit(solution)/shard_map/attend/pallas_call | solution.py:229
  115.4 17.8 %collective-permute-done.2 = bf16[1024,512]{1,0:T(8,128)(2,1)S(1)} collective-permute-done((bf16[1024,512]{1,0:T(8,128)(2,1)}, bf16[1024,512]{1,0:T(8,128)(2,1)S(1)}, u32[]{:S(2)}, u32[]{:S(2)}) %collective-permute-start.2) | collective-permute-done | bytes 1048608 | tf_op jit(solution)/shard_map/ppermute | solution.py:125
  139.4 27.0 %collective-permute-done.5 = bf16[1024,512]{1,0:T(8,128)(2,1)S(1)} collective-permute-done((bf16[1024,512]{1,0:T(8,128)(2,1)}, bf16[1024,512]{1,0:T(8,128)(2,1)S(1)}, u32[]{:S(2)}, u32[]{:S(2)}) %collective-permute-start.5) | collective-permute-done | bytes 1048608 | tf_op jit(solution)/shard_map/ppermute | solution.py:125
  169.9 23.3 %collective-permute-done.7 = bf16[1024,512]{1,0:T(8,128)(2,1)} collective-permute-done((bf16[1024,512]{1,0:T(8,128)(2,1)S(1)}, bf16[1024,512]{1,0:T(8,128)(2,1)}, u32[]{:S(2)}, u32[]{:S(2)}) %collective-permute-start.7) | collective-permute-done | bytes 1048608 | tf_op jit(solution)/shard_map/ppermute | solution.py:125
  219.7 8.5 fusion.89
  257.1 17.4 %collective-permute-done.14 = bf16[256,2048]{1,0:T(8,128)(2,1)S(1)} collective-permute-done((bf16[256,2048]{1,0:T(8,128)(2,1)S(1)}, bf16[256,2048]{1,0:T(8,128)(2,1)S(1)}, u32[]{:S(2)}, u32[]{:S(2)}) %collective-permute-start.14) | collective-permute-done | bytes 1048608 | tf_op jit(solution)/shard_map/ppermute | solution.py:125
  282.9 18.7 %collective-permute-done.16 = bf16[256,2048]{1,0:T(8,128)(2,1)S(1)} collective-permute-done((bf16[256,2048]{1,0:T(8,128)(2,1)S(1)}, bf16[256,2048]{1,0:T(8,128)(2,1)S(1)}, u32[]{:S(2)}, u32[]{:S(2)}) %collective-permute-start.16) | collective-permute-done | bytes 1048608 | tf_op jit(solution)/shard_map/ppermute | solution.py:125
  302.4 8.3 collective-permute-start.18
  314.7 16.7 %collective-permute-done.18 = bf16[256,2048]{1,0:T(8,128)(2,1)S(1)} collective-permute-done((bf16[256,2048]{1,0:T(8,128)(2,1)S(1)}, bf16[256,2048]{1,0:T(8,128)(2,1)S(1)}, u32[]{:S(2)}, u32[]{:S(2)}) %collective-permute-start.18) | collective-permute-done | bytes 1048608 | tf_op jit(solution)/shard_map/ppermute | solution.py:125
  343.7 18.5 %collective-permute-done.20 = bf16[256,2048]{1,0:T(8,128)(2,1)S(1)} collective-permute-done((bf16[256,2048]{1,0:T(8,128)(2,1)S(1)}, bf16[256,2048]{1,0:T(8,128)(2,1)S(1)}, u32[]{:S(2)}, u32[]{:S(2)}) %collective-permute-start.20) | collective-permute-done | bytes 1048608 | tf_op jit(solution)/shard_map/ppermute | solution.py:125
  381.3 9.1 collective-permute-done.23
  448.1 11.2 %convolution_convert_fusion.2 = bf16[2048,2048]{1,0:T(8,128)(2,1)} fusion(bf16[256,2048]{1,0:T(8,128)(2,1)S(1)} %add.494, bf16[256,2048]{1,0:T(8,128)(2,1)S(1)} %add.492, bf16[256,2048]{1,0:T(8,128)(2,1)S(1)} %add.493, bf16[256,2048]{1,0:T(8,128)(2,1)S(1)} %get-tuple-element.359, bf16[256,2048]{1,0:T(8,128)(2,1)S(1)} %copy-done.82, ...), kind=kOutput, calls=%fused_computation.3 | convolution fusion | flops 8627683328 | bytes 16777216 | tf_op jit(solution)/shard_map/dot_general | solution.py:158
  477.5 12.9 %convolution_convert_fusion.1 = bf16[2048,2048]{1,0:T(8,128)(2,1)} fusion(bf16[256,2048]{1,0:T(8,128)(2,1)S(1)} %copy-done.47, bf16[256,2048]{1,0:T(8,128)(2,1)S(1)} %copy-done.49, bf16[256,2048]{1,0:T(8,128)(2,1)S(1)} %copy-done.45, bf16[256,2048]{1,0:T(8,128)(2,1)S(1)} %copy-done.43, bf16[256,2048]{1,0:T(8,128)(2,1)} %copy-done.80, ...), kind=kOutput, calls=%fused_computation.2 | convolution fusion | flops 8627683328 | bytes 16777216 | tf_op jit(solution)/shard_map/dot_general | solution.py:158
  496.4 11.1 %collective-permute-start.36 = (bf16[256,2048]{1,0:T(8,128)(2,1)}, bf16[256,2048]{1,0:T(8,128)(2,1)}, u32[]{:S(2)}, u32[]{:S(2)}) collective-permute-start(bf16[256,2048]{1,0:T(8,128)(2,1)} %add_convert_fusion.4), channel_id=1, source_target_pairs={{0,1},{1,2},{2,3},{4,5},{5,6},{6,7},{8,9},{9,10},{10,11},{12,13},{... | collective-permute-start | bytes 3145736 | tf_op jit(solution)/shard_map/ppermute | solution.py:125
  555.3 8.9 collective-permute-start.41
  569.4 32.2 %attend_back.1 = (bf16[1024,512]{1,0:T(8,128)(2,1)}, f32[2048,512]{1,0:T(8,128)}, f32[2048,512]{1,0:T(8,128)}) custom-call(s32[1,1024]{1,0:T(1,128)} %get-tuple-element.691.low_ref, s32[1,1024]{1,0:T(1,128)} %get-tuple-element.690.high_ref, bf16[1024,1536]{1,0:T(8,128)(2,1)} %copy-done.16, bf16[2048,1024]{1,0:T(8,128)(2,1)} %pad_maximum_fusion.1.k_ref.v_ref, ...), custom_call_target="tpu_custom_call" | custom-call | flops 21474836480 | bytes 20971520 | tf_op jit(solution)/shard_map/attend_back/pallas_call | solution.py:248
  632.6 8.9 fusion
  702.8 32.7 %reduce-scatter.8.cloned.1.call-done = bf16[256,2048]{1,0:T(8,128)(2,1)} async-done(((bf16[2048,2048]{1,0:T(8,128)(2,1)}), bf16[256,2048]{1,0:T(8,128)(2,1)}) %reduce-scatter.8.cloned.1.call-update) | async-done | bytes 1048592 | tf_op jit(solution)/shard_map/reduce_scatter | solution.py:412
  752.8 17.6 %newton_schulz.4.in_ref = f32[512,2048]{1,0:T(8,128)} custom-call(bf16[2048,512]{1,0:T(8,128)(2,1)} %bitcast.43.in_ref), custom_call_target="tpu_custom_call" | custom-call | flops 9663676416 | bytes 6291456 | tf_op jit(solution)/shard_map/newton_schulz/pallas_call | solution.py:358
  804.9 22.5 %newton_schulz.5 = bf16[2048,512]{1,0:T(8,128)(2,1)} custom-call(f32[512,2048]{1,0:T(8,128)} %newton_schulz.4.in_ref), custom_call_target="tpu_custom_call" | custom-call | flops 14495514624 | bytes 6291456 | tf_op jit(solution)/shard_map/newton_schulz/pallas_call | solution.py:358
  841.3 17.6 %newton_schulz.6.in_ref = f32[512,2048]{1,0:T(8,128)} custom-call(bf16[2048,512]{1,0:T(8,128)(2,1)} %bitcast.238), custom_call_target="tpu_custom_call" | custom-call | flops 9663676416 | bytes 6291456 | tf_op jit(solution)/shard_map/newton_schulz/pallas_call | solution.py:358
  871.0 22.5 %newton_schulz.7 = bf16[2048,512]{1,0:T(8,128)(2,1)} custom-call(f32[512,2048]{1,0:T(8,128)} %newton_schulz.6.in_ref), custom_call_target="tpu_custom_call" | custom-call | flops 14495514624 | bytes 6291456 | tf_op jit(solution)/shard_map/newton_schulz/pallas_call | solution.py:358
  (484 shorter events, 505.9 us)
Async XLA Ops:
  7.2 52.7 %all-gather.8.cloned.1.call-start = ((), (), s32[]{:S(2)}) async-start(), calls=%async_computation.5 | async-start | bytes 7077888 | tf_op jit(solution)/shard_map/all_gather | solution.py:408
  11.5 187.5 %all-gather.10.cloned.1.call-start = ((), (), s32[]{:S(2)}) async-start(), calls=%async_computation.6 | async-start | bytes 9437184 | tf_op jit(solution)/shard_map/all_gather | solution.py:408
  48.2 171.5 %all-gather.12.cloned.1.call-start = ((), (), s32[]{:S(2)}) async-start(), calls=%async_computation.7 | async-start | bytes 9437184 | tf_op jit(solution)/shard_map/all_gather | solution.py:408
  51.1 181.8 %all-gather.14.cloned.1.call-start = ((), (), s32[]{:S(2)}) async-start(), calls=%async_computation.8 | async-start | bytes 9437184 | tf_op jit(solution)/shard_map/all_gather | solution.py:408
  52.3 608.7 %reduce-scatter.6.cloned.1.call-start = ((), (), s32[]{:S(2)}) async-start(), calls=%async_computation.10 | async-start | bytes 9437184 | tf_op jit(solution)/shard_map/reduce_scatter | solution.py:412
  110.2 27.1 %collective-permute-start.3 = (bf16[1024,512]{1,0:T(8,128)(2,1)}, bf16[1024,512]{1,0:T(8,128)(2,1)}, u32[]{:S(2)}, u32[]{:S(2)}) collective-permute-start(bf16[1024,512]{1,0:T(8,128)(2,1)} %attend.1), channel_id=1, source_target_pairs={{1,0},{2,1},{3,2},{5,4},{6,5},{7,6},{9,8},{10,9},{11,10},{13,12},{... | collective-permute-start | bytes 3145736 | tf_op jit(solution)/shard_map/ppermute | solution.py:125
  138.1 28.3 %collective-permute-start.5 = (bf16[1024,512]{1,0:T(8,128)(2,1)}, bf16[1024,512]{1,0:T(8,128)(2,1)S(1)}, u32[]{:S(2)}, u32[]{:S(2)}) collective-permute-start(bf16[1024,512]{1,0:T(8,128)(2,1)} %collective-permute-done.3), channel_id=1, source_target_pairs={{1,0},{2,1},{5,4},{6,5},{9,8},{10,9},{13,12},{14,13},{17,16},{18,1... | collective-permute-start | bytes 3145736 | tf_op jit(solution)/shard_map/ppermute | solution.py:125
  302.4 29.0 %collective-permute-start.18 = (bf16[256,2048]{1,0:T(8,128)(2,1)S(1)}, bf16[256,2048]{1,0:T(8,128)(2,1)S(1)}, u32[]{:S(2)}, u32[]{:S(2)}) collective-permute-start(bf16[256,2048]{1,0:T(8,128)(2,1)S(1)} %add_convert_fusion.7), channel_id=1, source_target_pairs={{0,1},{1,2},{2,3},{4,5},{5,6},{6,7},{8,9},{9,10},{10,11},{12,13},{... | collective-permute-start | bytes 3145736 | tf_op jit(solution)/shard_map/ppermute | solution.py:125
  462.1 201.8 %reduce-scatter.4.cloned.1.call-start = ((), (), s32[]{:S(2)}) async-start(), calls=%async_computation.9 | async-start | bytes 9437184 | tf_op jit(solution)/shard_map/reduce_scatter | solution.py:412
  490.5 245.0 %reduce-scatter.8.cloned.1.call-start = ((), (), s32[]{:S(2)}) async-start(), calls=%async_computation.11 | async-start | bytes 9437184 | tf_op jit(solution)/shard_map/reduce_scatter | solution.py:412
  555.3 46.2 %collective-permute-start.41 = (bf16[256,512]{1,0:T(8,128)(2,1)S(1)}, bf16[256,512]{1,0:T(8,128)(2,1)S(1)}, u32[]{:S(2)}, u32[]{:S(2)}) collective-permute-start(bf16[256,512]{1,0:T(8,128)(2,1)S(1)} %get-tuple-element.411), channel_id=1, source_target_pairs={{0,1},{1,2},{2,3},{3,0},{4,5},{5,6},{6,7},{7,4},{8,9},{9,10},{10,1... | collective-permute-start | bytes 786440 | tf_op jit(solution)/shard_map/ppermute | solution.py:125
  564.2 37.3 %collective-permute-start.42 = (bf16[256,512]{1,0:T(8,128)(2,1)S(1)}, bf16[256,512]{1,0:T(8,128)(2,1)S(1)}, u32[]{:S(2)}, u32[]{:S(2)}) collective-permute-start(bf16[256,512]{1,0:T(8,128)(2,1)S(1)} %get-tuple-element.412), channel_id=1, source_target_pairs={{0,2},{1,3},{2,0},{3,1},{4,6},{5,7},{6,4},{7,5},{8,10},{9,11},{10,... | collective-permute-start | bytes 786440 | tf_op jit(solution)/shard_map/ppermute | solution.py:125
  564.2 37.3 %collective-permute-start.43 = (bf16[256,512]{1,0:T(8,128)(2,1)S(1)}, bf16[256,512]{1,0:T(8,128)(2,1)S(1)}, u32[]{:S(2)}, u32[]{:S(2)}) collective-permute-start(bf16[256,512]{1,0:T(8,128)(2,1)S(1)} %get-tuple-element.413), channel_id=1, source_target_pairs={{0,3},{1,0},{2,1},{3,2},{4,7},{5,4},{6,5},{7,6},{8,11},{9,8},{10,9... | collective-permute-start | bytes 786440 | tf_op jit(solution)/shard_map/ppermute | solution.py:125
  688.6 48.6 %all-to-all-start = ((bf16[8,256,512]{2,1,0:T(8,128)(2,1)}), bf16[8,256,512]{2,1,0:T(8,128)(2,1)}, u32[]{:S(2)}, u32[]{:S(2)}) async-start(bf16[8,256,512]{2,1,0:T(8,128)(2,1)} %copy-done.28), calls=%async_computation.2 | async-start | bytes 4194304 | tf_op jit(solution)/shard_map/all_to_all | solution.py:125
  693.7 165.3 %all-gather.16.cloned.1.call-start = ((), (), s32[]{:S(2)}) async-start(), calls=%async_computation.12 | async-start | bytes 1081344 | tf_op jit(solution)/shard_map/all_gather | solution.py:649
  693.7 43.5 %collective-permute-start.48 = (bf16[256,2048]{1,0:T(8,128)(2,1)}, bf16[256,2048]{1,0:T(8,128)(2,1)}, u32[]{:S(2)}, u32[]{:S(2)}) collective-permute-start(bf16[256,2048]{1,0:T(8,128)(2,1)} %get-tuple-element.455), channel_id=1, source_target_pairs={{0,1},{1,2},{4,5},{5,6},{8,9},{9,10},{12,13},{13,14},{16,17},{17,1... | collective-permute-start | bytes 3145736 | tf_op jit(solution)/shard_map/ppermute | solution.py:125
  699.1 38.1 %collective-permute-start.49 = (bf16[256,2048]{1,0:T(8,128)(2,1)S(1)}, bf16[256,2048]{1,0:T(8,128)(2,1)}, u32[]{:S(2)}, u32[]{:S(2)}) collective-permute-start(bf16[256,2048]{1,0:T(8,128)(2,1)S(1)} %get-tuple-element.456), channel_id=1, source_target_pairs={{2,1},{3,2},{6,5},{7,6},{10,9},{11,10},{14,13},{15,14},{18,17},{19... | collective-permute-start | bytes 3145736 | tf_op jit(solution)/shard_map/ppermute | solution.py:125
  740.8 34.5 %collective-permute-start.50 = (bf16[256,2048]{1,0:T(8,128)(2,1)}, bf16[256,2048]{1,0:T(8,128)(2,1)}, u32[]{:S(2)}, u32[]{:S(2)}) collective-permute-start(bf16[256,2048]{1,0:T(8,128)(2,1)} %get-tuple-element.463), channel_id=1, source_target_pairs={{0,1},{1,2},{2,3},{4,5},{5,6},{6,7},{8,9},{9,10},{10,11},{12,13},{... | collective-permute-start | bytes 3145736 | tf_op jit(solution)/shard_map/ppermute | solution.py:125
  745.2 30.1 %collective-permute-start.51 = (bf16[256,2048]{1,0:T(8,128)(2,1)}, bf16[256,2048]{1,0:T(8,128)(2,1)}, u32[]{:S(2)}, u32[]{:S(2)}) collective-permute-start(bf16[256,2048]{1,0:T(8,128)(2,1)} %get-tuple-element.464), channel_id=1, source_target_pairs={{1,0},{2,1},{3,2},{5,4},{6,5},{7,6},{9,8},{10,9},{11,10},{13,12},{... | collective-permute-start | bytes 3145736 | tf_op jit(solution)/shard_map/ppermute | solution.py:125
  803.5 28.3 %collective-permute-start.57 = (bf16[256,2048]{1,0:T(8,128)(2,1)S(1)}, bf16[256,2048]{1,0:T(8,128)(2,1)}, u32[]{:S(2)}, u32[]{:S(2)}) collective-permute-start(bf16[256,2048]{1,0:T(8,128)(2,1)S(1)} %add_convert_fusion.refs_0_), channel_id=1, source_target_pairs={{1,0},{2,1},{3,2},{5,4},{6,5},{7,6},{9,8},{10,9},{11,10},{13,12},{... | collective-permute-start | bytes 3145736 | tf_op jit(solution)/shard_map/ppermute | solution.py:125
  804.8 27.0 %collective-permute-start.58 = (bf16[4,256,512]{2,1,0:T(8,128)(2,1)S(1)}, bf16[4,256,512]{2,1,0:T(8,128)(2,1)S(1)}, u32[]{:S(2)}, u32[]{:S(2)}) collective-permute-start(bf16[4,256,512]{2,1,0:T(8,128)(2,1)S(1)} %pad_maximum_fusion.9), channel_id=1, source_target_pairs={{0,4},{4,0},{1,5},{5,1},{2,6},{6,2},{3,7},{7,3},{8,12},{12,8},{9,1... | collective-permute-start | bytes 3145736 | tf_op jit(solution)/shard_map/ppermute | solution.py:125
  834.5 27.8 %collective-permute-start.59 = (bf16[256,2048]{1,0:T(8,128)(2,1)}, bf16[256,2048]{1,0:T(8,128)(2,1)S(1)}, u32[]{:S(2)}, u32[]{:S(2)}) collective-permute-start(bf16[256,2048]{1,0:T(8,128)(2,1)} %collective-permute-done.56.refs_1_), channel_id=1, source_target_pairs={{1,2},{2,3},{5,6},{6,7},{9,10},{10,11},{13,14},{14,15},{17,18},{18... | collective-permute-start | bytes 3145736 | tf_op jit(solution)/shard_map/ppermute | solution.py:125
  835.2 27.3 %collective-permute-start.60 = (bf16[256,2048]{1,0:T(8,128)(2,1)}, bf16[256,2048]{1,0:T(8,128)(2,1)}, u32[]{:S(2)}, u32[]{:S(2)}) collective-permute-start(bf16[256,2048]{1,0:T(8,128)(2,1)} %collective-permute-done.57.refs_6_), channel_id=1, source_target_pairs={{1,0},{2,1},{5,4},{6,5},{9,8},{10,9},{13,12},{14,13},{17,16},{18,1... | collective-permute-start | bytes 3145736 | tf_op jit(solution)/shard_map/ppermute | solution.py:125
  836.5 31.4 %all-to-all-start.1 = ((bf16[8,256,512]{2,1,0:T(8,128)(2,1)}), bf16[8,256,512]{2,1,0:T(8,128)(2,1)S(1)}, u32[]{:S(2)}, u32[]{:S(2)}) async-start(bf16[8,256,512]{2,1,0:T(8,128)(2,1)} %bitcast.237), calls=%async_computation.4 | async-start | bytes 4194304 | tf_op jit(solution)/shard_map/all_to_all | solution.py:125
  (142 other events, 1914.5 us)
Sparse Core Ops, SparseCore 0:
  11.6 48.2 all-gather.7
  62.3 56.0 all-gather.9
  120.9 54.2 all-gather.11
  177.0 55.9 all-gather.13
  462.3 74.2 reduce-scatter.5
  540.2 71.2 reduce-scatter.3
  649.1 86.3 reduce-scatter.7
  790.2 52.1 all-gather.15

commit v4 on v3

--- a/solution.py
+++ b/solution.py
@@ -192,7 +192,9 @@
     o_ref[...] = dot_tn(probs.astype(BF16), v_ref[pl.ds(start, span), :]).astype(BF16)
 
 
-def attend_back_kernel(low_ref, high_ref, q_ref, k_ref, v_ref, g_ref, dq_ref, dk_ref, dv_ref):
+def attend_back_kernel(
+    low_ref, high_ref, q_ref, k_ref, v_ref, g_ref, dq_ref, above_ref, centre_ref, below_ref, total
+):
     rows = q_ref.shape[0]
     span = rows + 2 * REACH
     start = pl.multiple_of(pl.program_id(1) * rows, rows)
@@ -200,17 +202,23 @@
 
     @pl.when(pl.program_id(1) == 0)
     def _():
-        dk_ref[...] = jnp.zeros_like(dk_ref)
-        dv_ref[...] = jnp.zeros_like(dv_ref)
+        total[...] = jnp.zeros_like(total)
 
     q, g, keys = q_ref[...], g_ref[...], k_ref[window, :]
     probs = window_probs(q, keys, low_ref, high_ref, start)
     dprobs = dot_nt(v_ref[window, :], g)
     offset = jnp.sum(dprobs * probs, axis=0, keepdims=True)
     dscores = (probs * (dprobs - offset) * (HEAD_DIM**-0.5)).astype(BF16)
-    dv_ref[window, :] += dot(probs.astype(BF16), g)
-    dk_ref[window, :] += dot(dscores, q)
+    total[1, window, :] += dot(probs.astype(BF16), g)
+    total[0, window, :] += dot(dscores, q)
     dq_ref[...] = dot_tn(dscores, keys).astype(BF16)
+
+    @pl.when(pl.program_id(1) == pl.num_programs(1) - 1)
+    def _():
+        length = centre_ref.shape[1]
+        above_ref[...] = total[:, :REACH, :].astype(BF16)
+        centre_ref[...] = total[:, REACH : REACH + length, :]
+        below_ref[...] = total[:, REACH + length :, :].astype(BF16)
 
 
 def attention_specs(rows, padded, heads):
@@ -244,13 +252,23 @@
     rows = min(QUERY_ROWS, length)
     bounds, q_spec, k_spec, v_spec = attention_specs(rows, padded, heads)
     pairs = heads * length * (rows + 2 * REACH)
-    total = jax.ShapeDtypeStruct((padded, heads * HEAD_DIM), F32)
+    width = heads * HEAD_DIM
+
+    def stacked(count):
+        return pl.BlockSpec((2, count, HEAD_DIM), lambda h, b: (0, 0, h))
+
     return pl.pallas_call(
         attend_back_kernel,
         grid=(heads, length // rows),
         in_specs=[bounds, bounds, q_spec, k_spec, v_spec, q_spec],
-        out_specs=(q_spec, k_spec, k_spec),
-        out_shape=(jax.ShapeDtypeStruct((length, heads * HEAD_DIM), BF16), total, total),
+        out_specs=(q_spec, stacked(REACH), stacked(length), stacked(REACH)),
+        out_shape=(
+            jax.ShapeDtypeStruct((length, width), BF16),
+            jax.ShapeDtypeStruct((2, REACH, width), BF16),
+            jax.ShapeDtypeStruct((2, length, width), F32),
+            jax.ShapeDtypeStruct((2, REACH, width), BF16),
+        ),
+        scratch_shapes=[pltpu.VMEM((2, padded, HEAD_DIM), F32)],
         cost_estimate=pl.CostEstimate(
             flops=32 * pairs * HEAD_DIM, transcendentals=pairs, bytes_accessed=20 << 20
         ),
@@ -402,6 +420,49 @@
 
 def column_blocks(value):
     return [value[:, at : at + BW] for at in range(0, value.shape[1], BW)]
+
+
+def turn_kernel(grad_ref, old_ref, out_ref, moment_ref):
+    turned = grad_ref[...].astype(F32).T
+    out_ref[...] = turned
+    moment_ref[...] = BETA * old_ref[...] + (1.0 - BETA) * turned
+
+
+def turned_moment(grad_t, old):
+    rows, width = grad_t.shape
+    here = pl.BlockSpec((BW, rows), lambda j: (j, 0))
+    out = jax.ShapeDtypeStruct((width, rows), F32)
+    return pl.pallas_call(
+        turn_kernel,
+        grid=(width // BW,),
+        in_specs=[pl.BlockSpec((rows, BW), lambda j: (0, j)), here],
+        out_specs=(here, here),
+        out_shape=(out, out),
+        cost_estimate=pl.CostEstimate(
+            flops=3 * rows * width, transcendentals=0, bytes_accessed=14 * rows * width
+        ),
+        name="turn",
+    )(grad_t, old)
+
+
+def update_kernel(ortho_ref, old_ref, out_ref):
+    out_ref[...] = old_ref[...] - MATRIX_RATE * ortho_ref[...].astype(F32).T
+
+
+def turned_update(back, first, copies, old):
+    width, rows = old.shape
+    here = pl.BlockSpec((BW, rows), lambda j: (j, 0))
+    return pl.pallas_call(
+        update_kernel,
+        grid=(width // BW,),
+        in_specs=[pl.BlockSpec((None, rows, BW), lambda j: ((first + j) * copies, 0, 0)), here],
+        out_specs=here,
+        out_shape=jax.ShapeDtypeStruct((width, rows), F32),
+        cost_estimate=pl.CostEstimate(
+            flops=2 * rows * width, transcendentals=0, bytes_accessed=10 * rows * width
+        ),
+        name="update",
+    )(back, old)
 
 
 def gather_rows(value):
@@ -580,15 +641,9 @@
     def attention_back(*slots):
         return attend_back(low, high, qkv, padded_kv, placed([[slot] for slot in slots], BF16, me), heads)
 
-    dq_low, key_grad, value_grad = step([dbranch], attention_back, *dattended.slots)
-
-    def kv_rows(start, count):
-        rows = slice(start, start + count)
-        return jnp.concatenate([key_grad[rows], value_grad[rows]], axis=1)
-
+    dq_low, kv_above, kv_centre, kv_below = step([dbranch], attention_back, *dattended.slots)
     edges = Once(
-        along(kv_rows(0, REACH).astype(BF16), "ctx", downward(1, ctx)),
-        along(kv_rows(length + REACH, REACH).astype(BF16), "ctx", upward(0, ctx - 1)),
+        along(kv_above, "ctx", downward(1, ctx)), along(kv_below, "ctx", upward(0, ctx - 1))
     )
     rows = w_query.shape[0]
     group = width // rows
@@ -601,8 +656,11 @@
     pieces = step([edges], out_pieces, dbranch.slots, head_slots)
     from_above, from_below = (edge.astype(F32) for edge in edges.got)
     beyond = length - REACH
-    added = jnp.pad(from_above, ((beyond, 0), (0, 0))) + jnp.pad(from_below, ((0, beyond), (0, 0)))
-    dqkv = jnp.concatenate([dq_low, (kv_rows(REACH, length) + added).astype(BF16)], axis=1)
+    added = jnp.pad(from_above, ((0, 0), (beyond, 0), (0, 0))) + jnp.pad(
+        from_below, ((0, 0), (0, beyond), (0, 0))
+    )
+    kv_low = (kv_centre + added).astype(BF16)
+    dqkv = jnp.concatenate([dq_low, kv_low[0], kv_low[1]], axis=1)
     grad_attn = row_major(jnp.concatenate([dot_tn(hidden, dqkv).astype(BF16), pieces], axis=1))
     dqkv = after(dqkv, grad_attn)
     grad_attn = scatter_rows(grad_attn)
@@ -626,26 +684,22 @@
     terms, (moment_inner, moment_outer_t), blocks = step(
         [input_sum], between, dqkv, grad_inner, grad_outer_t
     )
-    grad_inner, grad_outer_t = grad_inner.astype(F32), grad_outer_t.astype(F32)
+    grad_inner = grad_inner.astype(F32)
     for r, value in zip(rest, terms):
         parts[r] = value
     owners = Once(swapped(blocks))
-    grad_outer, moment_outer = step(
-        [input_sum, owners], lambda a, b: (a.T, b.T), grad_outer_t, moment_outer_t
-    )
+    grad_outer, moment_outer = step([input_sum, owners], turned_moment, grad_outer_t, mom_outer)
     homes = [
         (p * tp + t, (t * (group // tp) + p // tp) * tp + (t - p % tp) % tp)
         for p in range(group)
         for t in range(tp)
     ]
+    iterate = step([input_sum], orthogonal_start, owners.got[0])
+    for _ in range(tp - 4):
+        step([input_sum])
+    iterate, grad_attn = lax.optimization_barrier((iterate, grad_attn))
     piece = Once(along(grad_attn[:, 3 * local :], (*WEIGHT_AXES, "tp"), homes))
-    iterate, grad_qkv, sums = step(
-        [input_sum, piece],
-        lambda owned, *values: (orthogonal_start(owned), *values),
-        owners.got[0],
-        grad_attn[:, : 3 * local],
-        sums,
-    )
+    grad_qkv, sums = step([piece], lambda *values: values, grad_attn[:, : 3 * local], sums)
     totals = jnp.sum(lax.all_gather(sums, (*WEIGHT_AXES, "tp"), axis=0), axis=0)
     for _ in range(tp - 4):
         step([input_sum])
@@ -678,11 +732,11 @@
     owned = jnp.concatenate([mine, *peers.got], axis=0)
 
     def update_ffn(back):
-        ortho = from_owners(back, 2 * moment_inner.shape[1] // BW)
-        half = len(ortho) // 2
+        half = moment_inner.shape[1] // BW
+        ortho = from_owners(back, 2 * half)
         return (
             w_inner - MATRIX_RATE * jnp.concatenate(ortho[:half], axis=1),
-            w_outer - MATRIX_RATE * jnp.concatenate(ortho[half:], axis=1).T,
+            turned_update(back, half, group // (2 * half), w_outer),
         )
 
     ortho = Once(swapped(done))

time: 938 us -> 912 us (0.972)
  local copies, waits for them, and re-layouts: 53.6 us -> 34.9 us
  other arithmetic: 101 us -> 89.3 us
    reduce_scatter x3, waiting for transfers between devices: 32.7 us -> 0.01 us  [scatter_rows(): return lax.psum_scatter(value, WEIGHT_AXES, scatter_dimension=0, tiled=True)]
    ppermute x66, waiting for transfers between devices: 240 us -> 261 us  [step(): send(value)]
    unnamed x193 -> x189, local copies, waits for them, and re-layouts: 32.3 us -> 17.3 us
  transfers between devices with their start and end apart: 76 -> 76, of which waited for: 36 -> 38; matrix products, arithmetic and copies ran while one was open for 27% -> 26% of each run, Pallas kernels for 17% -> 18%
where the time goes in v4:
time: 912 us; the launch traced here: 904 us
  waiting for transfers between devices  278 us (30%)
  starting transfers between devices  166 us (18%)
  Pallas kernels  163 us (18%)
  matrix products  156 us (17%)
  other arithmetic  89.3 us (10%)
  local copies, waits for them, and re-layouts  34.9 us (4%)
  between operations  16.3 us (2%)
    ppermute x66, waiting for transfers between devices, step(): send(value)  261 us
    ppermute x66, starting transfers between devices, step(): send(value)  158 us
    pallas_call x4, Pallas kernels, newton_schulz_part(): pl.pallas_call(functools.partial(newton_schulz_kernel, steps), out_shape=...  80.2 us
    dot_general x14, matrix products, dot_nt(): lax.dot_general(left, right, (((1,), (1,)), ((), ())), preferred_element_...  61.4 us
    dot_general x10, matrix products, dot(): return jnp.dot(left, right, preferred_element_type=F32)  57.9 us
    dot_general x7, matrix products, dot_tn(): lax.dot_general(left, right, (((0,), (0,)), ((), ())), preferred_element_...  37 us
    pallas_call x1, Pallas kernels, attend_back(): pl.pallas_call(attend_back_kernel, grid=(heads, length // rows), in_specs...  32.5 us
    pallas_call x1, Pallas kernels, attend(): pl.pallas_call(attend_kernel, grid=(heads, length // rows), in_specs=[bou...  23.4 us
  transfers between devices with their start and end apart: 76, of which 38 were waited for; matrix products, arithmetic and copies ran while one was open for 26% of the time, Pallas kernels for 18%

profile of v4, /device:TPU:0, one launch (start us, length us, event | category | flops | bytes accessed | tf_op | source)
XLA Modules:
  0.0 903.6 jit_solution(1771856280379179296)
XLA Ops:
  28.2 9.8 %collective-permute-done.11 = bf16[256,512]{0,1:T(8,128)(2,1)S(1)} collective-permute-done((bf16[256,512]{0,1:T(8,128)(2,1)S(1)}, bf16[256,512]{0,1:T(8,128)(2,1)S(1)}, u32[]{:S(2)}, u32[]{:S(2)}) %collective-permute-start.11) | collective-permute-done | bytes 262176 | tf_op jit(solution)/shard_map/ppermute | solution.py:125
  59.9 10.0 %fusion.35.q_ref = bf16[1024,1536]{1,0:T(8,128)(2,1)S(1)} fusion(bf16[2048,1536]{1,0:T(8,128)(2,1)} %all-gather.8.cloned.1.call-done, bf16[1,1024,2048]{2,1,0:T(8,128)(2,1)} %param.19), kind=kOutput, calls=%fused_computation.39 | convolution fusion | flops 6444023808 | bytes 13631488 | tf_op jit(solution)/shard_map/dot_general | solution.py:150
  83.2 23.4 %attend.1 = bf16[1024,512]{1,0:T(8,128)(2,1)} custom-call(s32[1,1024]{1,0:T(1,128)} %get-tuple-element.693.low_ref, s32[1,1024]{1,0:T(1,128)} %get-tuple-element.692.high_ref, bf16[1024,1536]{1,0:T(8,128)(2,1)} %copy-done.11, bf16[2048,1024]{1,0:T(8,128)(2,1)} %pad_maximum_fusion.1.k_ref.v_ref, bf16[2048,1024]{1,0:T(8,128)(2,1)} %pad_maximum_fusion.1.k_ref.v_ref), custom_call_target="tpu_custom_call" | custom-call | flops 10737418240 | bytes 8388608 | tf_op jit(solution)/shard_map/attend/pallas_call | solution.py:237
  115.3 17.8 %collective-permute-done.2 = bf16[1024,512]{1,0:T(8,128)(2,1)S(1)} collective-permute-done((bf16[1024,512]{1,0:T(8,128)(2,1)}, bf16[1024,512]{1,0:T(8,128)(2,1)S(1)}, u32[]{:S(2)}, u32[]{:S(2)}) %collective-permute-start.2) | collective-permute-done | bytes 1048608 | tf_op jit(solution)/shard_map/ppermute | solution.py:125
  139.3 27.0 %collective-permute-done.5 = bf16[1024,512]{1,0:T(8,128)(2,1)S(1)} collective-permute-done((bf16[1024,512]{1,0:T(8,128)(2,1)}, bf16[1024,512]{1,0:T(8,128)(2,1)S(1)}, u32[]{:S(2)}, u32[]{:S(2)}) %collective-permute-start.5) | collective-permute-done | bytes 1048608 | tf_op jit(solution)/shard_map/ppermute | solution.py:125
  169.8 23.3 %collective-permute-done.7 = bf16[1024,512]{1,0:T(8,128)(2,1)} collective-permute-done((bf16[1024,512]{1,0:T(8,128)(2,1)S(1)}, bf16[1024,512]{1,0:T(8,128)(2,1)}, u32[]{:S(2)}, u32[]{:S(2)}) %collective-permute-start.7) | collective-permute-done | bytes 1048608 | tf_op jit(solution)/shard_map/ppermute | solution.py:125
  219.4 8.5 fusion.88
  257.3 17.4 %collective-permute-done.14 = bf16[256,2048]{1,0:T(8,128)(2,1)S(1)} collective-permute-done((bf16[256,2048]{1,0:T(8,128)(2,1)S(1)}, bf16[256,2048]{1,0:T(8,128)(2,1)S(1)}, u32[]{:S(2)}, u32[]{:S(2)}) %collective-permute-start.14) | collective-permute-done | bytes 1048608 | tf_op jit(solution)/shard_map/ppermute | solution.py:125
  283.1 18.7 %collective-permute-done.16 = bf16[256,2048]{1,0:T(8,128)(2,1)S(1)} collective-permute-done((bf16[256,2048]{1,0:T(8,128)(2,1)S(1)}, bf16[256,2048]{1,0:T(8,128)(2,1)S(1)}, u32[]{:S(2)}, u32[]{:S(2)}) %collective-permute-start.16) | collective-permute-done | bytes 1048608 | tf_op jit(solution)/shard_map/ppermute | solution.py:125
  302.7 8.3 collective-permute-start.18
  314.9 16.8 %collective-permute-done.18 = bf16[256,2048]{1,0:T(8,128)(2,1)S(1)} collective-permute-done((bf16[256,2048]{1,0:T(8,128)(2,1)S(1)}, bf16[256,2048]{1,0:T(8,128)(2,1)S(1)}, u32[]{:S(2)}, u32[]{:S(2)}) %collective-permute-start.18) | collective-permute-done | bytes 1048608 | tf_op jit(solution)/shard_map/ppermute | solution.py:125
  343.9 18.5 %collective-permute-done.20 = bf16[256,2048]{1,0:T(8,128)(2,1)S(1)} collective-permute-done((bf16[256,2048]{1,0:T(8,128)(2,1)S(1)}, bf16[256,2048]{1,0:T(8,128)(2,1)S(1)}, u32[]{:S(2)}, u32[]{:S(2)}) %collective-permute-start.20) | collective-permute-done | bytes 1048608 | tf_op jit(solution)/shard_map/ppermute | solution.py:125
  381.6 9.1 %collective-permute-done.23 = bf16[256,2048]{1,0:T(8,128)(2,1)S(1)} collective-permute-done((bf16[256,2048]{1,0:T(8,128)(2,1)S(1)}, bf16[256,2048]{1,0:T(8,128)(2,1)S(1)}, u32[]{:S(2)}, u32[]{:S(2)}) %collective-permute-start.23) | collective-permute-done | bytes 1048608 | tf_op jit(solution)/shard_map/ppermute | solution.py:125
  448.4 11.2 %convolution_convert_fusion.2 = bf16[2048,2048]{1,0:T(8,128)(2,1)} fusion(bf16[256,2048]{1,0:T(8,128)(2,1)S(1)} %add.494, bf16[256,2048]{1,0:T(8,128)(2,1)S(1)} %add.492, bf16[256,2048]{1,0:T(8,128)(2,1)S(1)} %add.493, bf16[256,2048]{1,0:T(8,128)(2,1)S(1)} %get-tuple-element.364, bf16[256,2048]{1,0:T(8,128)(2,1)S(1)} %copy-done.82, ...), kind=kOutput, calls=%fused_computation.3 | convolution fusion | flops 8627683328 | bytes 16777216 | tf_op jit(solution)/shard_map/dot_general | solution.py:158
  477.7 12.9 %convolution_convert_fusion.1 = bf16[2048,2048]{1,0:T(8,128)(2,1)} fusion(bf16[256,2048]{1,0:T(8,128)(2,1)S(1)} %copy-done.50, bf16[256,2048]{1,0:T(8,128)(2,1)S(1)} %copy-done.52, bf16[256,2048]{1,0:T(8,128)(2,1)S(1)} %copy-done.48, bf16[256,2048]{1,0:T(8,128)(2,1)S(1)} %copy-done.46, bf16[256,2048]{1,0:T(8,128)(2,1)} %copy-done.80, ...), kind=kOutput, calls=%fused_computation.2 | convolution fusion | flops 8627683328 | bytes 16777216 | tf_op jit(solution)/shard_map/dot_general | solution.py:158
  496.7 11.2 %collective-permute-start.36 = (bf16[256,2048]{1,0:T(8,128)(2,1)}, bf16[256,2048]{1,0:T(8,128)(2,1)}, u32[]{:S(2)}, u32[]{:S(2)}) collective-permute-start(bf16[256,2048]{1,0:T(8,128)(2,1)} %add_convert_fusion.5), channel_id=1, source_target_pairs={{0,1},{1,2},{2,3},{4,5},{5,6},{6,7},{8,9},{9,10},{10,11},{12,13},{... | collective-permute-start | bytes 3145736 | tf_op jit(solution)/shard_map/ppermute | solution.py:125
  555.5 10.4 %collective-permute-start.41 = (bf16[256,512]{1,0:T(8,128)(2,1)S(1)}, bf16[256,512]{1,0:T(8,128)(2,1)S(1)}, u32[]{:S(2)}, u32[]{:S(2)}) collective-permute-start(bf16[256,512]{1,0:T(8,128)(2,1)S(1)} %get-tuple-element.416), channel_id=1, source_target_pairs={{0,1},{1,2},{2,3},{3,0},{4,5},{5,6},{6,7},{7,4},{8,9},{9,10},{10,1... | collective-permute-start | bytes 786440 | tf_op jit(solution)/shard_map/ppermute | solution.py:125
  571.1 32.5 %attend_back.1 = (bf16[1024,512]{1,0:T(8,128)(2,1)}, bf16[2,512,512]{2,1,0:T(8,128)(2,1)}, f32[2,1024,512]{2,1,0:T(8,128)}, bf16[2,512,512]{2,1,0:T(8,128)(2,1)}) custom-call(s32[1,1024]{1,0:T(1,128)} %get-tuple-element.693.low_ref, s32[1,1024]{1,0:T(1,128)} %get-tuple-element.692.high_ref, bf16[1024,1536]{1,0:T(8,128)(2,1)} %copy-done.11, ...), custom_call_target="tpu_custom_call" | custom-call | flops 21474836480 | bytes 20971520 | tf_op jit(solution)/shard_map/attend_back/pallas_call | solution.py:260
  624.3 8.6 fusion
  694.2 14.6 %collective-permute-done.48 = bf16[256,2048]{1,0:T(8,128)(2,1)} collective-permute-done((bf16[256,2048]{1,0:T(8,128)(2,1)}, bf16[256,2048]{1,0:T(8,128)(2,1)}, u32[]{:S(2)}, u32[]{:S(2)}) %collective-permute-start.48) | collective-permute-done | bytes 1048608 | tf_op jit(solution)/shard_map/ppermute | solution.py:125
  722.9 17.6 %newton_schulz.4.in_ref = f32[512,2048]{1,0:T(8,128)} custom-call(bf16[2048,512]{1,0:T(8,128)(2,1)} %bitcast.39.in_ref), custom_call_target="tpu_custom_call" | custom-call | flops 9663676416 | bytes 6291456 | tf_op jit(solution)/shard_map/newton_schulz/pallas_call | solution.py:376
  784.7 22.5 %newton_schulz.5 = bf16[2048,512]{1,0:T(8,128)(2,1)} custom-call(f32[512,2048]{1,0:T(8,128)} %newton_schulz.4.in_ref), custom_call_target="tpu_custom_call" | custom-call | flops 14495514624 | bytes 6291456 | tf_op jit(solution)/shard_map/newton_schulz/pallas_call | solution.py:376
  820.1 17.6 %newton_schulz.6.in_ref = f32[512,2048]{1,0:T(8,128)} custom-call(bf16[2048,512]{1,0:T(8,128)(2,1)} %bitcast.228), custom_call_target="tpu_custom_call" | custom-call | flops 9663676416 | bytes 6291456 | tf_op jit(solution)/shard_map/newton_schulz/pallas_call | solution.py:376
  849.8 22.5 %newton_schulz.7 = bf16[2048,512]{1,0:T(8,128)(2,1)} custom-call(f32[512,2048]{1,0:T(8,128)} %newton_schulz.6.in_ref), custom_call_target="tpu_custom_call" | custom-call | flops 14495514624 | bytes 6291456 | tf_op jit(solution)/shard_map/newton_schulz/pallas_call | solution.py:376
  (473 shorter events, 497.3 us)
Async XLA Ops:
  7.2 52.7 %all-gather.8.cloned.1.call-start = ((), (), s32[]{:S(2)}) async-start(), calls=%async_computation.5 | async-start | bytes 7077888 | tf_op jit(solution)/shard_map/all_gather | solution.py:469
  11.5 187.5 %all-gather.10.cloned.1.call-start = ((), (), s32[]{:S(2)}) async-start(), calls=%async_computation.6 | async-start | bytes 9437184 | tf_op jit(solution)/shard_map/all_gather | solution.py:469
  48.2 171.3 %all-gather.12.cloned.1.call-start = ((), (), s32[]{:S(2)}) async-start(), calls=%async_computation.7 | async-start | bytes 9437184 | tf_op jit(solution)/shard_map/all_gather | solution.py:469
  51.1 181.8 %all-gather.14.cloned.1.call-start = ((), (), s32[]{:S(2)}) async-start(), calls=%async_computation.8 | async-start | bytes 9437184 | tf_op jit(solution)/shard_map/all_gather | solution.py:469
  52.3 600.1 %reduce-scatter.6.cloned.1.call-start = ((), (), s32[]{:S(2)}) async-start(), calls=%async_computation.10 | async-start | bytes 9437184 | tf_op jit(solution)/shard_map/reduce_scatter | solution.py:473
  106.6 26.6 %collective-permute-start.2 = (bf16[1024,512]{1,0:T(8,128)(2,1)}, bf16[1024,512]{1,0:T(8,128)(2,1)S(1)}, u32[]{:S(2)}, u32[]{:S(2)}) collective-permute-start(bf16[1024,512]{1,0:T(8,128)(2,1)} %attend.1), channel_id=1, source_target_pairs={{0,1},{1,2},{2,3},{4,5},{5,6},{6,7},{8,9},{9,10},{10,11},{12,13},{... | collective-permute-start | bytes 3145736 | tf_op jit(solution)/shard_map/ppermute | solution.py:125
  110.2 27.1 %collective-permute-start.3 = (bf16[1024,512]{1,0:T(8,128)(2,1)}, bf16[1024,512]{1,0:T(8,128)(2,1)}, u32[]{:S(2)}, u32[]{:S(2)}) collective-permute-start(bf16[1024,512]{1,0:T(8,128)(2,1)} %attend.1), channel_id=1, source_target_pairs={{1,0},{2,1},{3,2},{5,4},{6,5},{7,6},{9,8},{10,9},{11,10},{13,12},{... | collective-permute-start | bytes 3145736 | tf_op jit(solution)/shard_map/ppermute | solution.py:125
  138.0 28.3 %collective-permute-start.5 = (bf16[1024,512]{1,0:T(8,128)(2,1)}, bf16[1024,512]{1,0:T(8,128)(2,1)S(1)}, u32[]{:S(2)}, u32[]{:S(2)}) collective-permute-start(bf16[1024,512]{1,0:T(8,128)(2,1)} %collective-permute-done.3), channel_id=1, source_target_pairs={{1,0},{2,1},{5,4},{6,5},{9,8},{10,9},{13,12},{14,13},{17,16},{18,1... | collective-permute-start | bytes 3145736 | tf_op jit(solution)/shard_map/ppermute | solution.py:125
  275.3 26.5 %collective-permute-start.16 = (bf16[256,2048]{1,0:T(8,128)(2,1)S(1)}, bf16[256,2048]{1,0:T(8,128)(2,1)S(1)}, u32[]{:S(2)}, u32[]{:S(2)}) collective-permute-start(bf16[256,2048]{1,0:T(8,128)(2,1)S(1)} %get-tuple-element.318), channel_id=1, source_target_pairs={{0,1},{1,2},{4,5},{5,6},{8,9},{9,10},{12,13},{13,14},{16,17},{17,1... | collective-permute-start | bytes 3145736 | tf_op jit(solution)/shard_map/ppermute | solution.py:125
  302.7 29.0 %collective-permute-start.18 = (bf16[256,2048]{1,0:T(8,128)(2,1)S(1)}, bf16[256,2048]{1,0:T(8,128)(2,1)S(1)}, u32[]{:S(2)}, u32[]{:S(2)}) collective-permute-start(bf16[256,2048]{1,0:T(8,128)(2,1)S(1)} %add_convert_fusion.8), channel_id=1, source_target_pairs={{0,1},{1,2},{2,3},{4,5},{5,6},{6,7},{8,9},{9,10},{10,11},{12,13},{... | collective-permute-start | bytes 3145736 | tf_op jit(solution)/shard_map/ppermute | solution.py:125
  462.4 189.9 %reduce-scatter.4.cloned.1.call-start = ((), (), s32[]{:S(2)}) async-start(), calls=%async_computation.9 | async-start | bytes 9437184 | tf_op jit(solution)/shard_map/reduce_scatter | solution.py:473
  490.8 255.8 %reduce-scatter.8.cloned.1.call-start = ((), (), s32[]{:S(2)}) async-start(), calls=%async_computation.11 | async-start | bytes 9437184 | tf_op jit(solution)/shard_map/reduce_scatter | solution.py:473
  555.5 48.0 %collective-permute-start.41 = (bf16[256,512]{1,0:T(8,128)(2,1)S(1)}, bf16[256,512]{1,0:T(8,128)(2,1)S(1)}, u32[]{:S(2)}, u32[]{:S(2)}) collective-permute-start(bf16[256,512]{1,0:T(8,128)(2,1)S(1)} %get-tuple-element.416), channel_id=1, source_target_pairs={{0,1},{1,2},{2,3},{3,0},{4,5},{5,6},{6,7},{7,4},{8,9},{9,10},{10,1... | collective-permute-start | bytes 786440 | tf_op jit(solution)/shard_map/ppermute | solution.py:125
  565.9 37.6 %collective-permute-start.42 = (bf16[256,512]{1,0:T(8,128)(2,1)S(1)}, bf16[256,512]{1,0:T(8,128)(2,1)S(1)}, u32[]{:S(2)}, u32[]{:S(2)}) collective-permute-start(bf16[256,512]{1,0:T(8,128)(2,1)S(1)} %get-tuple-element.417), channel_id=1, source_target_pairs={{0,2},{1,3},{2,0},{3,1},{4,6},{5,7},{6,4},{7,5},{8,10},{9,11},{10,... | collective-permute-start | bytes 786440 | tf_op jit(solution)/shard_map/ppermute | solution.py:125
  565.9 37.7 %collective-permute-start.43 = (bf16[256,512]{1,0:T(8,128)(2,1)S(1)}, bf16[256,512]{1,0:T(8,128)(2,1)S(1)}, u32[]{:S(2)}, u32[]{:S(2)}) collective-permute-start(bf16[256,512]{1,0:T(8,128)(2,1)S(1)} %get-tuple-element.418), channel_id=1, source_target_pairs={{0,3},{1,0},{2,1},{3,2},{4,7},{5,4},{6,5},{7,6},{8,11},{9,8},{10,9... | collective-permute-start | bytes 786440 | tf_op jit(solution)/shard_map/ppermute | solution.py:125
  676.7 36.4 %all-to-all-start = ((bf16[8,256,512]{2,1,0:T(8,128)(2,1)}), bf16[8,256,512]{2,1,0:T(8,128)(2,1)}, u32[]{:S(2)}, u32[]{:S(2)}) async-start(bf16[8,256,512]{2,1,0:T(8,128)(2,1)} %copy-done.27), calls=%async_computation.2 | async-start | bytes 4194304 | tf_op jit(solution)/shard_map/all_to_all | solution.py:125
  681.1 156.6 %all-gather.16.cloned.1.call-start = ((), (), s32[]{:S(2)}) async-start(), calls=%async_computation.12 | async-start | bytes 1081344 | tf_op jit(solution)/shard_map/all_gather | solution.py:703
  681.2 27.7 %collective-permute-start.48 = (bf16[256,2048]{1,0:T(8,128)(2,1)}, bf16[256,2048]{1,0:T(8,128)(2,1)}, u32[]{:S(2)}, u32[]{:S(2)}) collective-permute-start(bf16[256,2048]{1,0:T(8,128)(2,1)} %get-tuple-element.461), channel_id=1, source_target_pairs={{0,1},{1,2},{4,5},{5,6},{8,9},{9,10},{12,13},{13,14},{16,17},{17,1... | collective-permute-start | bytes 3145736 | tf_op jit(solution)/shard_map/ppermute | solution.py:125
  780.8 26.4 %collective-permute-start.56 = (bf16[256,2048]{1,0:T(8,128)(2,1)S(1)}, bf16[256,2048]{1,0:T(8,128)(2,1)}, u32[]{:S(2)}, u32[]{:S(2)}) collective-permute-start(bf16[256,2048]{1,0:T(8,128)(2,1)S(1)} %add_convert_fusion.1.refs_0_), channel_id=1, source_target_pairs={{0,1},{1,2},{2,3},{4,5},{5,6},{6,7},{8,9},{9,10},{10,11},{12,13},{... | collective-permute-start | bytes 3145736 | tf_op jit(solution)/shard_map/ppermute | solution.py:125
  783.4 28.0 %collective-permute-start.57 = (bf16[256,2048]{1,0:T(8,128)(2,1)S(1)}, bf16[256,2048]{1,0:T(8,128)(2,1)}, u32[]{:S(2)}, u32[]{:S(2)}) collective-permute-start(bf16[256,2048]{1,0:T(8,128)(2,1)S(1)} %add_convert_fusion.1.refs_0_), channel_id=1, source_target_pairs={{1,0},{2,1},{3,2},{5,4},{6,5},{7,6},{9,8},{10,9},{11,10},{13,12},{... | collective-permute-start | bytes 3145736 | tf_op jit(solution)/shard_map/ppermute | solution.py:125
  784.7 26.7 %collective-permute-start.58 = (bf16[4,256,512]{2,1,0:T(8,128)(2,1)S(1)}, bf16[4,256,512]{2,1,0:T(8,128)(2,1)}, u32[]{:S(2)}, u32[]{:S(2)}) collective-permute-start(bf16[4,256,512]{2,1,0:T(8,128)(2,1)S(1)} %pad_maximum_fusion.7), channel_id=1, source_target_pairs={{0,4},{4,0},{1,5},{5,1},{2,6},{6,2},{3,7},{7,3},{8,12},{12,8},{9,1... | collective-permute-start | bytes 3145736 | tf_op jit(solution)/shard_map/ppermute | solution.py:125
  814.4 26.7 %collective-permute-start.59 = (bf16[256,2048]{1,0:T(8,128)(2,1)}, bf16[256,2048]{1,0:T(8,128)(2,1)S(1)}, u32[]{:S(2)}, u32[]{:S(2)}) collective-permute-start(bf16[256,2048]{1,0:T(8,128)(2,1)} %collective-permute-done.56.refs_1_), channel_id=1, source_target_pairs={{1,2},{2,3},{5,6},{6,7},{9,10},{10,11},{13,14},{14,15},{17,18},{18... | collective-permute-start | bytes 3145736 | tf_op jit(solution)/shard_map/ppermute | solution.py:125
  815.1 27.4 %collective-permute-start.60 = (bf16[256,2048]{1,0:T(8,128)(2,1)}, bf16[256,2048]{1,0:T(8,128)(2,1)}, u32[]{:S(2)}, u32[]{:S(2)}) collective-permute-start(bf16[256,2048]{1,0:T(8,128)(2,1)} %collective-permute-done.57.refs_6_), channel_id=1, source_target_pairs={{1,0},{2,1},{5,4},{6,5},{9,8},{10,9},{13,12},{14,13},{17,16},{18,1... | collective-permute-start | bytes 3145736 | tf_op jit(solution)/shard_map/ppermute | solution.py:125
  816.4 30.2 %all-to-all-start.1 = ((bf16[8,256,512]{2,1,0:T(8,128)(2,1)}), bf16[8,256,512]{2,1,0:T(8,128)(2,1)S(1)}, u32[]{:S(2)}, u32[]{:S(2)}) async-start(bf16[8,256,512]{2,1,0:T(8,128)(2,1)} %bitcast.227), calls=%async_computation.4 | async-start | bytes 4194304 | tf_op jit(solution)/shard_map/all_to_all | solution.py:125
  (142 other events, 1942.3 us)
Sparse Core Ops, SparseCore 0:
  11.6 48.2 all-gather.7
  62.3 56.0 all-gather.9
  120.9 54.2 all-gather.11
  176.9 55.9 all-gather.13
  462.5 74.1 reduce-scatter.5
  540.5 71.2 reduce-scatter.3
  640.6 87.7 reduce-scatter.7
  775.4 50.5 all-gather.15

commit v5 on v4

--- a/solution.py
+++ b/solution.py
@@ -651,7 +651,8 @@
     def out_pieces(dbranch_slots, head_slots):
         columns = placed([[slot] for slot in dbranch_slots], BF16, me)
         sums = [dot_tn(columns, slot).astype(BF16).reshape(-1, rows, local) for slot in head_slots]
-        return row_major(jnp.stack(sums, axis=1).reshape(group * rows, local))
+        sums = jnp.stack(sums, axis=1).reshape(group * rows, local)
+        return row_major(jnp.pad(sums, ((0, 0), (3 * local, 0))))
 
     pieces = step([edges], out_pieces, dbranch.slots, head_slots)
     from_above, from_below = (edge.astype(F32) for edge in edges.got)
@@ -661,7 +662,8 @@
     )
     kv_low = (kv_centre + added).astype(BF16)
     dqkv = jnp.concatenate([dq_low, kv_low[0], kv_low[1]], axis=1)
-    grad_attn = row_major(jnp.concatenate([dot_tn(hidden, dqkv).astype(BF16), pieces], axis=1))
+    grad_qkv = dot_tn(hidden, dqkv).astype(BF16)
+    grad_attn = row_major(lax.dynamic_update_slice(pieces, grad_qkv, (0, 0)))
     dqkv = after(dqkv, grad_attn)
     grad_attn = scatter_rows(grad_attn)
 

time: 912 us -> 908 us (level)
  no operation moved by 1% of the time
where the time goes in v5:
time: 908 us; the launch traced here: 899 us
  waiting for transfers between devices  278 us (31%)
  starting transfers between devices  167 us (18%)
  Pallas kernels  163 us (18%)
  matrix products  156 us (17%)
  other arithmetic  82.1 us (9%)
  local copies, waits for them, and re-layouts  36.7 us (4%)
  between operations  16.3 us (2%)
    ppermute x66, waiting for transfers between devices, step(): send(value)  261 us
    ppermute x66, starting transfers between devices, step(): send(value)  159 us
    pallas_call x4, Pallas kernels, newton_schulz_part(): pl.pallas_call(functools.partial(newton_schulz_kernel, steps), out_shape=...  80.2 us
    dot_general x14, matrix products, dot_nt(): lax.dot_general(left, right, (((1,), (1,)), ((), ())), preferred_element_...  61.4 us
    dot_general x10, matrix products, dot(): return jnp.dot(left, right, preferred_element_type=F32)  57.9 us
    dot_general x7, matrix products, dot_tn(): lax.dot_general(left, right, (((0,), (0,)), ((), ())), preferred_element_...  36.9 us
    pallas_call x1, Pallas kernels, attend_back(): pl.pallas_call(attend_back_kernel, grid=(heads, length // rows), in_specs...  32.5 us
    pallas_call x1, Pallas kernels, attend(): pl.pallas_call(attend_kernel, grid=(heads, length // rows), in_specs=[bou...  23.4 us
  transfers between devices with their start and end apart: 76, of which 38 were waited for; matrix products, arithmetic and copies ran while one was open for 26% of the time, Pallas kernels for 18%

profile of v5, /device:TPU:0, one launch (start us, length us, event | category | flops | bytes accessed | tf_op | source)
XLA Modules:
  0.0 899.4 jit_solution(15836541110458604972)
XLA Ops:
  28.2 9.8 %collective-permute-done.11 = bf16[256,512]{0,1:T(8,128)(2,1)S(1)} collective-permute-done((bf16[256,512]{0,1:T(8,128)(2,1)S(1)}, bf16[256,512]{0,1:T(8,128)(2,1)S(1)}, u32[]{:S(2)}, u32[]{:S(2)}) %collective-permute-start.11) | collective-permute-done | bytes 262176 | tf_op jit(solution)/shard_map/ppermute | solution.py:125
  59.9 10.0 %fusion.36.q_ref = bf16[1024,1536]{1,0:T(8,128)(2,1)S(1)} fusion(bf16[2048,1536]{1,0:T(8,128)(2,1)} %all-gather.8.cloned.1.call-done, bf16[1,1024,2048]{2,1,0:T(8,128)(2,1)} %param.19), kind=kOutput, calls=%fused_computation.39 | convolution fusion | flops 6444023808 | bytes 13631488 | tf_op jit(solution)/shard_map/dot_general | solution.py:150
  83.2 23.4 %attend.1 = bf16[1024,512]{1,0:T(8,128)(2,1)} custom-call(s32[1,1024]{1,0:T(1,128)} %get-tuple-element.693.low_ref, s32[1,1024]{1,0:T(1,128)} %get-tuple-element.692.high_ref, bf16[1024,1536]{1,0:T(8,128)(2,1)} %copy-done.11, bf16[2048,1024]{1,0:T(8,128)(2,1)} %pad_maximum_fusion.k_ref.v_ref, bf16[2048,1024]{1,0:T(8,128)(2,1)} %pad_maximum_fusion.k_ref.v_ref), custom_call_target="tpu_custom_call" | custom-call | flops 10737418240 | bytes 8388608 | tf_op jit(solution)/shard_map/attend/pallas_call | solution.py:237
  115.3 17.8 %collective-permute-done.2 = bf16[1024,512]{1,0:T(8,128)(2,1)S(1)} collective-permute-done((bf16[1024,512]{1,0:T(8,128)(2,1)}, bf16[1024,512]{1,0:T(8,128)(2,1)S(1)}, u32[]{:S(2)}, u32[]{:S(2)}) %collective-permute-start.2) | collective-permute-done | bytes 1048608 | tf_op jit(solution)/shard_map/ppermute | solution.py:125
  139.3 27.0 %collective-permute-done.5 = bf16[1024,512]{1,0:T(8,128)(2,1)S(1)} collective-permute-done((bf16[1024,512]{1,0:T(8,128)(2,1)}, bf16[1024,512]{1,0:T(8,128)(2,1)S(1)}, u32[]{:S(2)}, u32[]{:S(2)}) %collective-permute-start.5) | collective-permute-done | bytes 1048608 | tf_op jit(solution)/shard_map/ppermute | solution.py:125
  169.8 23.3 %collective-permute-done.7 = bf16[1024,512]{1,0:T(8,128)(2,1)} collective-permute-done((bf16[1024,512]{1,0:T(8,128)(2,1)S(1)}, bf16[1024,512]{1,0:T(8,128)(2,1)}, u32[]{:S(2)}, u32[]{:S(2)}) %collective-permute-start.7) | collective-permute-done | bytes 1048608 | tf_op jit(solution)/shard_map/ppermute | solution.py:125
  219.4 8.5 fusion.89
  257.3 17.4 %collective-permute-done.14 = bf16[256,2048]{1,0:T(8,128)(2,1)S(1)} collective-permute-done((bf16[256,2048]{1,0:T(8,128)(2,1)S(1)}, bf16[256,2048]{1,0:T(8,128)(2,1)S(1)}, u32[]{:S(2)}, u32[]{:S(2)}) %collective-permute-start.14) | collective-permute-done | bytes 1048608 | tf_op jit(solution)/shard_map/ppermute | solution.py:125
  283.1 18.7 %collective-permute-done.16 = bf16[256,2048]{1,0:T(8,128)(2,1)S(1)} collective-permute-done((bf16[256,2048]{1,0:T(8,128)(2,1)S(1)}, bf16[256,2048]{1,0:T(8,128)(2,1)S(1)}, u32[]{:S(2)}, u32[]{:S(2)}) %collective-permute-start.16) | collective-permute-done | bytes 1048608 | tf_op jit(solution)/shard_map/ppermute | solution.py:125
  302.7 8.3 collective-permute-start.18
  314.9 16.8 %collective-permute-done.18 = bf16[256,2048]{1,0:T(8,128)(2,1)S(1)} collective-permute-done((bf16[256,2048]{1,0:T(8,128)(2,1)S(1)}, bf16[256,2048]{1,0:T(8,128)(2,1)S(1)}, u32[]{:S(2)}, u32[]{:S(2)}) %collective-permute-start.18) | collective-permute-done | bytes 1048608 | tf_op jit(solution)/shard_map/ppermute | solution.py:125
  343.9 18.5 %collective-permute-done.20 = bf16[256,2048]{1,0:T(8,128)(2,1)S(1)} collective-permute-done((bf16[256,2048]{1,0:T(8,128)(2,1)S(1)}, bf16[256,2048]{1,0:T(8,128)(2,1)S(1)}, u32[]{:S(2)}, u32[]{:S(2)}) %collective-permute-start.20) | collective-permute-done | bytes 1048608 | tf_op jit(solution)/shard_map/ppermute | solution.py:125
  381.6 9.1 %collective-permute-done.23 = bf16[256,2048]{1,0:T(8,128)(2,1)S(1)} collective-permute-done((bf16[256,2048]{1,0:T(8,128)(2,1)S(1)}, bf16[256,2048]{1,0:T(8,128)(2,1)S(1)}, u32[]{:S(2)}, u32[]{:S(2)}) %collective-permute-start.23) | collective-permute-done | bytes 1048608 | tf_op jit(solution)/shard_map/ppermute | solution.py:125
  448.4 11.2 %convolution_convert_fusion.2 = bf16[2048,2048]{1,0:T(8,128)(2,1)} fusion(bf16[256,2048]{1,0:T(8,128)(2,1)S(1)} %add.496, bf16[256,2048]{1,0:T(8,128)(2,1)S(1)} %add.494, bf16[256,2048]{1,0:T(8,128)(2,1)S(1)} %add.495, bf16[256,2048]{1,0:T(8,128)(2,1)S(1)} %get-tuple-element.364, bf16[256,2048]{1,0:T(8,128)(2,1)S(1)} %copy-done.82, ...), kind=kOutput, calls=%fused_computation.2 | convolution fusion | flops 8627683328 | bytes 16777216 | tf_op jit(solution)/shard_map/dot_general | solution.py:158
  477.7 12.9 %convolution_convert_fusion.1 = bf16[2048,2048]{1,0:T(8,128)(2,1)} fusion(bf16[256,2048]{1,0:T(8,128)(2,1)S(1)} %copy-done.50, bf16[256,2048]{1,0:T(8,128)(2,1)S(1)} %copy-done.52, bf16[256,2048]{1,0:T(8,128)(2,1)S(1)} %copy-done.48, bf16[256,2048]{1,0:T(8,128)(2,1)S(1)} %copy-done.46, bf16[256,2048]{1,0:T(8,128)(2,1)} %copy-done.80, ...), kind=kOutput, calls=%fused_computation.1 | convolution fusion | flops 8627683328 | bytes 16777216 | tf_op jit(solution)/shard_map/dot_general | solution.py:158
  496.7 11.2 %collective-permute-start.36 = (bf16[256,2048]{1,0:T(8,128)(2,1)}, bf16[256,2048]{1,0:T(8,128)(2,1)}, u32[]{:S(2)}, u32[]{:S(2)}) collective-permute-start(bf16[256,2048]{1,0:T(8,128)(2,1)} %add_convert_fusion.5), channel_id=1, source_target_pairs={{0,1},{1,2},{2,3},{4,5},{5,6},{6,7},{8,9},{9,10},{10,11},{12,13},{... | collective-permute-start | bytes 3145736 | tf_op jit(solution)/shard_map/ppermute | solution.py:125
  555.5 10.4 %collective-permute-start.41 = (bf16[256,512]{1,0:T(8,128)(2,1)S(1)}, bf16[256,512]{1,0:T(8,128)(2,1)S(1)}, u32[]{:S(2)}, u32[]{:S(2)}) collective-permute-start(bf16[256,512]{1,0:T(8,128)(2,1)S(1)} %get-tuple-element.416), channel_id=1, source_target_pairs={{0,1},{1,2},{2,3},{3,0},{4,5},{5,6},{6,7},{7,4},{8,9},{9,10},{10,1... | collective-permute-start | bytes 786440 | tf_op jit(solution)/shard_map/ppermute | solution.py:125
  571.1 32.5 %attend_back.1 = (bf16[1024,512]{1,0:T(8,128)(2,1)}, bf16[2,512,512]{2,1,0:T(8,128)(2,1)}, f32[2,1024,512]{2,1,0:T(8,128)}, bf16[2,512,512]{2,1,0:T(8,128)(2,1)}) custom-call(s32[1,1024]{1,0:T(1,128)} %get-tuple-element.693.low_ref, s32[1,1024]{1,0:T(1,128)} %get-tuple-element.692.high_ref, bf16[1024,1536]{1,0:T(8,128)(2,1)} %copy-done.11, ...), custom_call_target="tpu_custom_call" | custom-call | flops 21474836480 | bytes 20971520 | tf_op jit(solution)/shard_map/attend_back/pallas_call | solution.py:260
  627.6 8.6 fusion.1
  690.0 14.6 %collective-permute-done.48 = bf16[256,2048]{1,0:T(8,128)(2,1)} collective-permute-done((bf16[256,2048]{1,0:T(8,128)(2,1)}, bf16[256,2048]{1,0:T(8,128)(2,1)}, u32[]{:S(2)}, u32[]{:S(2)}) %collective-permute-start.48) | collective-permute-done | bytes 1048608 | tf_op jit(solution)/shard_map/ppermute | solution.py:125
  718.6 17.6 %newton_schulz.4.in_ref = f32[512,2048]{1,0:T(8,128)} custom-call(bf16[2048,512]{1,0:T(8,128)(2,1)} %bitcast.39.in_ref), custom_call_target="tpu_custom_call" | custom-call | flops 9663676416 | bytes 6291456 | tf_op jit(solution)/shard_map/newton_schulz/pallas_call | solution.py:376
  780.5 22.5 %newton_schulz.5 = bf16[2048,512]{1,0:T(8,128)(2,1)} custom-call(f32[512,2048]{1,0:T(8,128)} %newton_schulz.4.in_ref), custom_call_target="tpu_custom_call" | custom-call | flops 14495514624 | bytes 6291456 | tf_op jit(solution)/shard_map/newton_schulz/pallas_call | solution.py:376
  815.8 17.6 %newton_schulz.6.in_ref = f32[512,2048]{1,0:T(8,128)} custom-call(bf16[2048,512]{1,0:T(8,128)(2,1)} %bitcast.230), custom_call_target="tpu_custom_call" | custom-call | flops 9663676416 | bytes 6291456 | tf_op jit(solution)/shard_map/newton_schulz/pallas_call | solution.py:376
  845.6 22.5 %newton_schulz.7 = bf16[2048,512]{1,0:T(8,128)(2,1)} custom-call(f32[512,2048]{1,0:T(8,128)} %newton_schulz.6.in_ref), custom_call_target="tpu_custom_call" | custom-call | flops 14495514624 | bytes 6291456 | tf_op jit(solution)/shard_map/newton_schulz/pallas_call | solution.py:376
  (473 shorter events, 493.1 us)
Async XLA Ops:
  7.2 52.7 %all-gather.8.cloned.1.call-start = ((), (), s32[]{:S(2)}) async-start(), calls=%async_computation.5 | async-start | bytes 7077888 | tf_op jit(solution)/shard_map/all_gather | solution.py:469
  11.5 187.5 %all-gather.10.cloned.1.call-start = ((), (), s32[]{:S(2)}) async-start(), calls=%async_computation.6 | async-start | bytes 9437184 | tf_op jit(solution)/shard_map/all_gather | solution.py:469
  48.2 171.3 %all-gather.12.cloned.1.call-start = ((), (), s32[]{:S(2)}) async-start(), calls=%async_computation.7 | async-start | bytes 9437184 | tf_op jit(solution)/shard_map/all_gather | solution.py:469
  51.1 181.8 %all-gather.14.cloned.1.call-start = ((), (), s32[]{:S(2)}) async-start(), calls=%async_computation.8 | async-start | bytes 9437184 | tf_op jit(solution)/shard_map/all_gather | solution.py:469
  52.3 595.8 %reduce-scatter.6.cloned.1.call-start = ((), (), s32[]{:S(2)}) async-start(), calls=%async_computation.10 | async-start | bytes 9437184 | tf_op jit(solution)/shard_map/reduce_scatter | solution.py:473
  106.6 26.6 %collective-permute-start.2 = (bf16[1024,512]{1,0:T(8,128)(2,1)}, bf16[1024,512]{1,0:T(8,128)(2,1)S(1)}, u32[]{:S(2)}, u32[]{:S(2)}) collective-permute-start(bf16[1024,512]{1,0:T(8,128)(2,1)} %attend.1), channel_id=1, source_target_pairs={{0,1},{1,2},{2,3},{4,5},{5,6},{6,7},{8,9},{9,10},{10,11},{12,13},{... | collective-permute-start | bytes 3145736 | tf_op jit(solution)/shard_map/ppermute | solution.py:125
  110.2 27.1 %collective-permute-start.3 = (bf16[1024,512]{1,0:T(8,128)(2,1)}, bf16[1024,512]{1,0:T(8,128)(2,1)}, u32[]{:S(2)}, u32[]{:S(2)}) collective-permute-start(bf16[1024,512]{1,0:T(8,128)(2,1)} %attend.1), channel_id=1, source_target_pairs={{1,0},{2,1},{3,2},{5,4},{6,5},{7,6},{9,8},{10,9},{11,10},{13,12},{... | collective-permute-start | bytes 3145736 | tf_op jit(solution)/shard_map/ppermute | solution.py:125
  138.0 28.3 %collective-permute-start.5 = (bf16[1024,512]{1,0:T(8,128)(2,1)}, bf16[1024,512]{1,0:T(8,128)(2,1)S(1)}, u32[]{:S(2)}, u32[]{:S(2)}) collective-permute-start(bf16[1024,512]{1,0:T(8,128)(2,1)} %collective-permute-done.3), channel_id=1, source_target_pairs={{1,0},{2,1},{5,4},{6,5},{9,8},{10,9},{13,12},{14,13},{17,16},{18,1... | collective-permute-start | bytes 3145736 | tf_op jit(solution)/shard_map/ppermute | solution.py:125
  275.3 26.5 %collective-permute-start.16 = (bf16[256,2048]{1,0:T(8,128)(2,1)S(1)}, bf16[256,2048]{1,0:T(8,128)(2,1)S(1)}, u32[]{:S(2)}, u32[]{:S(2)}) collective-permute-start(bf16[256,2048]{1,0:T(8,128)(2,1)S(1)} %get-tuple-element.318), channel_id=1, source_target_pairs={{0,1},{1,2},{4,5},{5,6},{8,9},{9,10},{12,13},{13,14},{16,17},{17,1... | collective-permute-start | bytes 3145736 | tf_op jit(solution)/shard_map/ppermute | solution.py:125
  302.7 29.0 %collective-permute-start.18 = (bf16[256,2048]{1,0:T(8,128)(2,1)S(1)}, bf16[256,2048]{1,0:T(8,128)(2,1)S(1)}, u32[]{:S(2)}, u32[]{:S(2)}) collective-permute-start(bf16[256,2048]{1,0:T(8,128)(2,1)S(1)} %add_convert_fusion.8), channel_id=1, source_target_pairs={{0,1},{1,2},{2,3},{4,5},{5,6},{6,7},{8,9},{9,10},{10,11},{12,13},{... | collective-permute-start | bytes 3145736 | tf_op jit(solution)/shard_map/ppermute | solution.py:125
  462.4 185.7 %reduce-scatter.4.cloned.1.call-start = ((), (), s32[]{:S(2)}) async-start(), calls=%async_computation.9 | async-start | bytes 9437184 | tf_op jit(solution)/shard_map/reduce_scatter | solution.py:473
  490.8 251.6 %reduce-scatter.8.cloned.1.call-start = ((), (), s32[]{:S(2)}) async-start(), calls=%async_computation.11 | async-start | bytes 9437184 | tf_op jit(solution)/shard_map/reduce_scatter | solution.py:473
  555.5 48.0 %collective-permute-start.41 = (bf16[256,512]{1,0:T(8,128)(2,1)S(1)}, bf16[256,512]{1,0:T(8,128)(2,1)S(1)}, u32[]{:S(2)}, u32[]{:S(2)}) collective-permute-start(bf16[256,512]{1,0:T(8,128)(2,1)S(1)} %get-tuple-element.416), channel_id=1, source_target_pairs={{0,1},{1,2},{2,3},{3,0},{4,5},{5,6},{6,7},{7,4},{8,9},{9,10},{10,1... | collective-permute-start | bytes 786440 | tf_op jit(solution)/shard_map/ppermute | solution.py:125
  565.9 37.6 %collective-permute-start.42 = (bf16[256,512]{1,0:T(8,128)(2,1)S(1)}, bf16[256,512]{1,0:T(8,128)(2,1)S(1)}, u32[]{:S(2)}, u32[]{:S(2)}) collective-permute-start(bf16[256,512]{1,0:T(8,128)(2,1)S(1)} %get-tuple-element.417), channel_id=1, source_target_pairs={{0,2},{1,3},{2,0},{3,1},{4,6},{5,7},{6,4},{7,5},{8,10},{9,11},{10,... | collective-permute-start | bytes 786440 | tf_op jit(solution)/shard_map/ppermute | solution.py:125
  565.9 37.7 %collective-permute-start.43 = (bf16[256,512]{1,0:T(8,128)(2,1)S(1)}, bf16[256,512]{1,0:T(8,128)(2,1)S(1)}, u32[]{:S(2)}, u32[]{:S(2)}) collective-permute-start(bf16[256,512]{1,0:T(8,128)(2,1)S(1)} %get-tuple-element.418), channel_id=1, source_target_pairs={{0,3},{1,0},{2,1},{3,2},{4,7},{5,4},{6,5},{7,6},{8,11},{9,8},{10,9... | collective-permute-start | bytes 786440 | tf_op jit(solution)/shard_map/ppermute | solution.py:125
  672.5 36.4 %all-to-all-start = ((bf16[8,256,512]{2,1,0:T(8,128)(2,1)}), bf16[8,256,512]{2,1,0:T(8,128)(2,1)}, u32[]{:S(2)}, u32[]{:S(2)}) async-start(bf16[8,256,512]{2,1,0:T(8,128)(2,1)} %copy-done.27), calls=%async_computation.2 | async-start | bytes 4194304 | tf_op jit(solution)/shard_map/all_to_all | solution.py:125
  676.8 156.7 %all-gather.16.cloned.1.call-start = ((), (), s32[]{:S(2)}) async-start(), calls=%async_computation.12 | async-start | bytes 1081344 | tf_op jit(solution)/shard_map/all_gather | solution.py:705
  676.9 27.7 %collective-permute-start.48 = (bf16[256,2048]{1,0:T(8,128)(2,1)}, bf16[256,2048]{1,0:T(8,128)(2,1)}, u32[]{:S(2)}, u32[]{:S(2)}) collective-permute-start(bf16[256,2048]{1,0:T(8,128)(2,1)} %get-tuple-element.461), channel_id=1, source_target_pairs={{0,1},{1,2},{4,5},{5,6},{8,9},{9,10},{12,13},{13,14},{16,17},{17,1... | collective-permute-start | bytes 3145736 | tf_op jit(solution)/shard_map/ppermute | solution.py:125
  776.5 26.4 %collective-permute-start.56 = (bf16[256,2048]{1,0:T(8,128)(2,1)S(1)}, bf16[256,2048]{1,0:T(8,128)(2,1)}, u32[]{:S(2)}, u32[]{:S(2)}) collective-permute-start(bf16[256,2048]{1,0:T(8,128)(2,1)S(1)} %add_convert_fusion.1.refs_0_), channel_id=1, source_target_pairs={{0,1},{1,2},{2,3},{4,5},{5,6},{6,7},{8,9},{9,10},{10,11},{12,13},{... | collective-permute-start | bytes 3145736 | tf_op jit(solution)/shard_map/ppermute | solution.py:125
  779.1 28.0 %collective-permute-start.57 = (bf16[256,2048]{1,0:T(8,128)(2,1)S(1)}, bf16[256,2048]{1,0:T(8,128)(2,1)}, u32[]{:S(2)}, u32[]{:S(2)}) collective-permute-start(bf16[256,2048]{1,0:T(8,128)(2,1)S(1)} %add_convert_fusion.1.refs_0_), channel_id=1, source_target_pairs={{1,0},{2,1},{3,2},{5,4},{6,5},{7,6},{9,8},{10,9},{11,10},{13,12},{... | collective-permute-start | bytes 3145736 | tf_op jit(solution)/shard_map/ppermute | solution.py:125
  780.4 26.7 %collective-permute-start.58 = (bf16[4,256,512]{2,1,0:T(8,128)(2,1)S(1)}, bf16[4,256,512]{2,1,0:T(8,128)(2,1)}, u32[]{:S(2)}, u32[]{:S(2)}) collective-permute-start(bf16[4,256,512]{2,1,0:T(8,128)(2,1)S(1)} %pad_maximum_fusion.6), channel_id=1, source_target_pairs={{0,4},{4,0},{1,5},{5,1},{2,6},{6,2},{3,7},{7,3},{8,12},{12,8},{9,1... | collective-permute-start | bytes 3145736 | tf_op jit(solution)/shard_map/ppermute | solution.py:125
  810.2 26.7 %collective-permute-start.59 = (bf16[256,2048]{1,0:T(8,128)(2,1)}, bf16[256,2048]{1,0:T(8,128)(2,1)S(1)}, u32[]{:S(2)}, u32[]{:S(2)}) collective-permute-start(bf16[256,2048]{1,0:T(8,128)(2,1)} %collective-permute-done.56.refs_1_), channel_id=1, source_target_pairs={{1,2},{2,3},{5,6},{6,7},{9,10},{10,11},{13,14},{14,15},{17,18},{18... | collective-permute-start | bytes 3145736 | tf_op jit(solution)/shard_map/ppermute | solution.py:125
  810.9 27.4 %collective-permute-start.60 = (bf16[256,2048]{1,0:T(8,128)(2,1)}, bf16[256,2048]{1,0:T(8,128)(2,1)}, u32[]{:S(2)}, u32[]{:S(2)}) collective-permute-start(bf16[256,2048]{1,0:T(8,128)(2,1)} %collective-permute-done.57.refs_6_), channel_id=1, source_target_pairs={{1,0},{2,1},{5,4},{6,5},{9,8},{10,9},{13,12},{14,13},{17,16},{18,1... | collective-permute-start | bytes 3145736 | tf_op jit(solution)/shard_map/ppermute | solution.py:125
  812.2 30.2 %all-to-all-start.1 = ((bf16[8,256,512]{2,1,0:T(8,128)(2,1)}), bf16[8,256,512]{2,1,0:T(8,128)(2,1)S(1)}, u32[]{:S(2)}, u32[]{:S(2)}) async-start(bf16[8,256,512]{2,1,0:T(8,128)(2,1)} %bitcast.229), calls=%async_computation.4 | async-start | bytes 4194304 | tf_op jit(solution)/shard_map/all_to_all | solution.py:125
  (142 other events, 1969.4 us)
Sparse Core Ops, SparseCore 0:
  11.6 48.2 all-gather.7
  62.3 56.0 all-gather.9
  120.9 54.2 all-gather.11
  176.9 55.9 all-gather.13
  462.5 74.1 reduce-scatter.5
  540.5 71.2 reduce-scatter.3
  636.4 87.7 reduce-scatter.7
  771.1 50.5 all-gather.15
